TPU v7x, 32 devices: a whole 2x2x4 slice. The times are simulated.
32 devices in a mesh: worker: 8 (over z, y), mp: 4 (over x, core).
Axes of the slice: x: 2, y: 2, z: 4, core: 2. Of those that a mesh axis runs over, the one named last changes fastest.
Arguments:
- gradients: bfloat16 [128, 1048576], P('worker', 'mp'), may hold values from -30 to 30
- center: float32 [1048576], P('mp'), may hold values from -6 to 6
- outside_sq: float32 [3, 128], P(None, 'worker'), may hold values from 209715.2 to 2097152
- radius: float32 [3], replicated, may hold values from 1.5 to 3
Outputs:
- new_center: float32 [1048576], P('mp')
- norms: float32 [128], P('worker')
All inputs are finite; a program needn't handle non-finite values.
Results may differ from a plain program's by a relative error of at most 0.0003.
Values sent between devices are 32-bit elements; how exact they have to be, the bound alone decides.
No kernel may reach another device: no remote copies, remote signals or barrier semaphores. Data moves between devices by JAX's collectives and lax.ppermute only.
A program may use at most 64 MiB of HBM per device.

v0:
```python
import jax
import jax.numpy as jnp
from jax import lax
from jax.sharding import PartitionSpec as P

ITERS = 3


def shards(gradients, center, outside_sq, radius):
    workers_all = gradients.shape[0] * lax.axis_size("worker")
    root_total = jnp.sqrt(jnp.float32(center.shape[0] * lax.axis_size("mp")))
    value = center
    norms = jnp.zeros((gradients.shape[0],), jnp.float32)
    for step in range(ITERS):
        diff = gradients.astype(jnp.float32) - value[None, :]
        partial_value = jnp.sum(diff * diff, axis=1)
        squared = lax.psum(partial_value, "mp") + outside_sq[step]
        norms = jnp.sqrt(squared)
        factor = jnp.minimum(jnp.float32(1.0), radius[step] * root_total / norms)
        local = jnp.sum(factor[:, None] * diff, axis=0)
        summed = lax.psum(local, "worker")
        value = value + summed / jnp.float32(workers_all)
    return (value, norms)


def solution(mesh):
    placed = (P("worker", "mp"), P("mp"), P(None, "worker"), P())
    return jax.shard_map(
        shards, mesh=mesh, in_specs=placed, out_specs=(P("mp"), P("worker")), check_vma=False
    )
```

profile of v0, /device:TPU:0, one launch (start us, length us, event | category | flops | bytes accessed | tf_op | source)
XLA Modules:
  0.0 333.9 jit_solution(5382687448233932146)
XLA Ops:
  7.2 0.0 copy-start
  7.2 0.0 copy-start.1
  7.2 0.0 copy-start.2
  7.2 0.0 all-reduce.4.cloned.1.call-start
  7.2 5.5 %fusion.10 = f32[16]{0:T(128)S(1)} fusion(bf16[16,262144]{1,0:T(8,128)(2,1)} %param.4, f32[262144]{0:T(1024)} %param.5), kind=kLoop, calls=%fused_computation.13 | loop fusion | flops 16777200 | bytes 9437248 | tf_op jit(solution)/shard_map/reduce_sum | solution.py:16
  12.8 8.4 %psum.42 = f32[16]{0:T(128)S(1)} all-reduce(f32[16]{0:T(128)S(1)} %fusion.10), channel_id=1, replica_groups=mesh['worker'=8,'mp'=4] {'mp'}, use_global_device_ids=true, to_apply=%region_1.0 | all-reduce | flops 16 | bytes 128 | tf_op jit(solution)/shard_map/psum | solution.py:17
  21.1 0.0 copy-done.1
  21.1 0.7 fusion.20
  22.5 0.0 copy-done.2
  22.5 0.0 copy-done
  22.5 14.0 %fusion.11 = f32[262144]{0:T(1024)} fusion(bf16[16,262144]{1,0:T(8,128)(2,1)} %param.4, f32[16]{0:T(128)S(1)} %fusion.17, f32[262144]{0:T(1024)S(1)} %copy-done), kind=kLoop, calls=%fused_computation.14 | loop fusion | flops 16515072 | bytes 10485824 | tf_op jit(solution)/shard_map/reduce_sum | solution.py:20
  36.5 0.0 all-reduce.4.cloned.1.call-update
  36.5 0.0 all-reduce.6.cloned.1.call-start
  37.2 78.1 %all-reduce.4.cloned.1.call-done = f32[262144]{0:T(1024)} async-done(((f32[262144]{0:T(1024)}), f32[262144]{0:T(1024)}) %all-reduce.4.cloned.1.call-update) | async-done | bytes 1048592 | tf_op jit(solution)/shard_map/psum | solution.py:21
  115.4 1.3 multiply_add_fusion.2
  116.7 5.2 %fusion.8 = f32[16]{0:T(128)S(1)} fusion(bf16[16,262144]{1,0:T(8,128)(2,1)} %param.4, f32[262144]{0:T(1024)S(1)} %multiply_add_fusion.2), kind=kLoop, calls=%fused_computation.11 | loop fusion | flops 16777200 | bytes 9437248 | tf_op jit(solution)/shard_map/reduce_sum | solution.py:16
  121.9 6.5 %psum.44 = f32[16]{0:T(128)S(1)} all-reduce(f32[16]{0:T(128)S(1)} %fusion.8), channel_id=1, replica_groups=mesh['worker'=8,'mp'=4] {'mp'}, use_global_device_ids=true, to_apply=%region_5.0 | all-reduce | flops 16 | bytes 128 | tf_op jit(solution)/shard_map/psum | solution.py:17
  128.4 14.0 %fusion.9 = f32[262144]{0:T(1024)} fusion(bf16[16,262144]{1,0:T(8,128)(2,1)} %param.4, f32[16]{0:T(128)S(1)} %fusion.18, f32[262144]{0:T(1024)S(1)} %multiply_add_fusion.2), kind=kLoop, calls=%fused_computation.12 | loop fusion | flops 16515072 | bytes 10485824 | tf_op jit(solution)/shard_map/reduce_sum | solution.py:20
  142.4 0.0 all-reduce.6.cloned.1.call-update
  142.4 0.0 all-reduce.8.cloned.1.call-start
  143.1 76.9 %all-reduce.6.cloned.1.call-done = f32[262144]{0:T(1024)} async-done(((f32[262144]{0:T(1024)}), f32[262144]{0:T(1024)}) %all-reduce.6.cloned.1.call-update) | async-done | bytes 1048592 | tf_op jit(solution)/shard_map/psum | solution.py:21
  220.0 1.3 multiply_add_fusion.1
  221.3 5.2 %fusion.6 = f32[16]{0:T(128)S(1)} fusion(bf16[16,262144]{1,0:T(8,128)(2,1)} %param.4, f32[262144]{0:T(1024)S(1)} %multiply_add_fusion.1), kind=kLoop, calls=%fused_computation.9 | loop fusion | flops 16777200 | bytes 9437248 | tf_op jit(solution)/shard_map/reduce_sum | solution.py:16
  226.5 6.5 %psum.46 = f32[16]{0:T(128)S(1)} all-reduce(f32[16]{0:T(128)S(1)} %fusion.6), channel_id=1, replica_groups=mesh['worker'=8,'mp'=4] {'mp'}, use_global_device_ids=true, to_apply=%region_9.0 | all-reduce | flops 16 | bytes 128 | tf_op jit(solution)/shard_map/psum | solution.py:17
  233.0 0.5 divide_minimum_fusion
  233.5 14.0 %fusion.7 = f32[262144]{0:T(1024)} fusion(bf16[16,262144]{1,0:T(8,128)(2,1)} %param.4, f32[16]{0:T(128)S(1)} %get-tuple-element.2, f32[262144]{0:T(1024)S(1)} %multiply_add_fusion.1), kind=kLoop, calls=%fused_computation.10 | loop fusion | flops 16515072 | bytes 10485824 | tf_op jit(solution)/shard_map/reduce_sum | solution.py:20
  247.5 0.0 all-reduce.8.cloned.1.call-update
  247.5 77.6 %all-reduce.8.cloned.1.call-done = f32[262144]{0:T(1024)} async-done(((f32[262144]{0:T(1024)}), f32[262144]{0:T(1024)}) %all-reduce.8.cloned.1.call-update) | async-done | bytes 1048592 | tf_op jit(solution)/shard_map/psum | solution.py:21
  325.1 2.3 multiply_add_fusion
  (2 shorter events, 0.0 us)
Async XLA Ops:
  7.2 15.3 %copy-start = (f32[262144]{0:T(1024)S(1)}, f32[262144]{0:T(1024)}, u32[]{:S(2)}) copy-start(f32[262144]{0:T(1024)} %param.5) | copy-start | bytes 3145732
  7.2 14.0 %copy-start.1 = (f32[3]{0:T(128)S(1)}, f32[3]{0:T(128)}, u32[]{:S(2)}) copy-start(f32[3]{0:T(128)} %param.7) | copy-start | bytes 40
  7.2 15.3 %copy-start.2 = (f32[3,16]{1,0:T(4,128)S(1)}, f32[3,16]{1,0:T(4,128)}, u32[]{:S(2)}) copy-start(f32[3,16]{1,0:T(4,128)} %param.6) | copy-start | bytes 580
  7.2 108.2 %all-reduce.4.cloned.1.call-start = ((), (), s32[]{:S(2)}) async-start(), calls=%async_computation | async-start | bytes 2097152 | tf_op jit(solution)/shard_map/psum | solution.py:21
  36.5 183.5 %all-reduce.6.cloned.1.call-start = ((), (), s32[]{:S(2)}) async-start(), calls=%async_computation.1 | async-start | bytes 2097152 | tf_op jit(solution)/shard_map/psum | solution.py:21
  142.4 182.7 %all-reduce.8.cloned.1.call-start = ((), (), s32[]{:S(2)}) async-start(), calls=%async_computation.2 | async-start | bytes 2097152 | tf_op jit(solution)/shard_map/psum | solution.py:21
Sparse Core Ops, SparseCore 0:
  36.6 78.7 all-reduce.3
  142.5 77.4 all-reduce.5
  247.6 77.4 all-reduce.7
where the time goes:
time: 334 us
  waiting for transfers between devices  233 us (70%)
  other arithmetic  63.3 us (19%)
  blocking collectives  21.4 us (6%)
  between operations  15.8 us (5%)
    psum x3, waiting for transfers between devices, shards(): summed = lax.psum(local, 'worker')  233 us
    reduce_sum x3, other arithmetic, shards(): local = jnp.sum(factor[:, None] * diff, axis=0)  41.9 us
    psum x3, blocking collectives, shards(): squared = lax.psum(partial_value, 'mp') + outside_sq[step]  21.4 us
    reduce_sum x3, other arithmetic, shards(): partial_value = jnp.sum(diff * diff, axis=1)  15.9 us
  transfers between devices with their start and end apart: 3, of which 3 were waited for; matrix products, arithmetic and copies ran while one was open for 0% of the time, Pallas kernels for 0%

commit v1 on v0

v1 whole, which is shorter than its diff:
```python
import functools

import jax
import jax.numpy as jnp
from jax import lax
from jax.experimental import pallas as pl
from jax.experimental.pallas import tpu as pltpu
from jax.sharding import PartitionSpec as P

LANES = 128
GROUP = 8
BLOCK = 32
VMEM_LIMIT = 24 << 20


def bits_of(size):
    count = size.bit_length() - 1
    assert 1 << count == size
    return count


def swap(size, bit):
    return [(i, i ^ (1 << bit)) for i in range(size)]


def square_rows(x_ref, x_row, v_ref, v_row, rows, carry, limit):
    unroll = 16

    def step(i, acc):
        acc = list(acc)
        for r in range(0, unroll, 2):
            row = v_row + i * unroll + r
            first = v_ref[pl.ds(row, 1), :]
            second = v_ref[pl.ds(row + 1, 1), :]
            at = (x_row + i * unroll + r) * GROUP
            for g in range(len(acc) // 2):
                both = x_ref[g, pl.ds(pl.multiple_of(at, 2 * GROUP), 2 * GROUP), :].astype(jnp.float32)
                a = both[:GROUP] - first
                b = both[GROUP:] - second
                acc[2 * g] = acc[2 * g] + a * a
                acc[2 * g + 1] = acc[2 * g + 1] + b * b
        return tuple(acc)

    return lax.fori_loop(0, rows // unroll, step, carry)


def zero_carry(groups):
    return tuple(jnp.zeros((GROUP, LANES), jnp.float32) for _ in range(2 * groups))


def store_carry(o_ref, acc):
    for g in range(len(acc) // 2):
        o_ref[pl.ds(g * GROUP, GROUP), :] = acc[2 * g] + acc[2 * g + 1]


def load_body(chunks, x_hbm, v_ref, x_ref, o_ref, sems):
    groups, total, _ = x_ref.shape
    rows = total // chunks

    def copy(c):
        window = pl.ds(pl.multiple_of(c * rows, 2 * GROUP), rows)
        return pltpu.make_async_copy(x_hbm.at[:, window, :], x_ref.at[:, window, :], sems.at[c])

    for c in range(chunks):
        copy(c).start()
    acc = zero_carry(groups)
    per = rows // GROUP
    for c in range(chunks):
        copy(c).wait()
        acc = square_rows(x_ref, c * per, v_ref, c * per, per, acc, per)
    store_carry(o_ref, acc)


def square_body(pieces, offs_ref, x_ref, v_ref, o_ref):
    groups = x_ref.shape[0]
    rows = v_ref.shape[0] // pieces
    acc = zero_carry(groups)
    for j in range(pieces):
        acc = square_rows(x_ref, pl.multiple_of(offs_ref[j], BLOCK), v_ref, j * rows, rows, acc, rows)
    store_carry(o_ref, acc)


def weigh_body(pieces, relative, devices, workers, root_total, offs_ref, radius_ref, x_ref, v_ref, s_ref, out_ref, o_ref):
    groups = x_ref.shape[0]
    rows = o_ref.shape[0] // pieces
    depth = BLOCK * GROUP
    squared = jnp.sum(s_ref[...], axis=1, keepdims=True) + out_ref[:, 0:1]
    factor = jnp.minimum(jnp.float32(1.0), radius_ref[0] * root_total / jnp.sqrt(squared))
    keep = jnp.float32(1.0 / devices) - jnp.sum(factor, axis=0, keepdims=True) / jnp.float32(workers)
    factor = factor / jnp.float32(workers)
    lane = lax.broadcasted_iota(jnp.int32, (GROUP, depth), 1)
    sub = lax.broadcasted_iota(jnp.int32, (GROUP, depth), 0)
    block = lax.broadcasted_iota(jnp.int32, (BLOCK, depth), 0)
    place = lax.broadcasted_iota(jnp.int32, (BLOCK, depth), 1)
    weights = []
    for g in range(groups):
        one = jnp.where(lane % GROUP == sub, factor[g * GROUP:(g + 1) * GROUP], 0.0)
        one = jnp.sum(one, axis=0, keepdims=True)
        full = jnp.where(place // GROUP == block, one, 0.0)
        high = full.astype(jnp.bfloat16)
        low = (full - high.astype(jnp.float32)).astype(jnp.bfloat16)
        weights.append(jnp.concatenate([high, low], axis=0))
    for j in range(pieces):
        base = pl.multiple_of(offs_ref[j], BLOCK)

        def step(i, _):
            at = base + i * 2 * BLOCK
            total = None
            for g in range(groups):
                left = x_ref[g, pl.ds(pl.multiple_of(at * GROUP, depth), depth), :]
                right = x_ref[g, pl.ds(pl.multiple_of(at * GROUP + depth, depth), depth), :]
                part = jnp.dot(weights[g], jnp.concatenate([left, right], axis=1), preferred_element_type=jnp.float32)
                total = part if total is None else total + part
            total = total[:BLOCK] + total[BLOCK:]
            v_at = (j * rows if relative else base) + i * 2 * BLOCK
            o_at = j * rows + i * 2 * BLOCK
            for h in range(2):
                old = v_ref[pl.ds(pl.multiple_of(v_at + h * BLOCK, BLOCK), BLOCK), :]
                o_ref[pl.ds(pl.multiple_of(o_at + h * BLOCK, BLOCK), BLOCK), :] = keep * old + total[:, h * LANES:(h + 1) * LANES]
            return 0

        lax.fori_loop(0, rows // (2 * BLOCK), step, 0)


VM = pl.BlockSpec(memory_space=pltpu.VMEM)
SM = pl.BlockSpec(memory_space=pltpu.SMEM)
PARAMS = pltpu.CompilerParams(vmem_limit_bytes=VMEM_LIMIT)


def shards(gradients, center, outside_sq, radius):
    workers, size = gradients.shape
    iters = outside_sq.shape[0]
    devices = lax.axis_size("worker")
    parts = lax.axis_size("mp")
    levels = bits_of(devices)
    root_total = float(size * parts) ** 0.5
    groups = workers // GROUP
    rows = size // LANES
    position = lax.axis_index("worker")
    bit = [(position >> d) & 1 for d in range(levels)]
    x = gradients.reshape(groups, GROUP, rows, LANES).transpose(0, 2, 1, 3).reshape(groups, rows * GROUP, LANES)
    center = center.reshape(rows, LANES)

    orders = [list(range(levels)), [1, 0] + list(range(2, levels))]
    height = rows // len(orders)
    count = 1 << (levels - 2)
    piece = height >> (levels - 1)

    def offsets(s, first):
        order = orders[s]
        out = []
        for j in range(count):
            off = jnp.int32(s * height) + (bit[order[0]] ^ first) * (height >> 1)
            for k in range(1, levels - 1):
                r = (j >> (levels - 2 - k)) & 1
                off = off + (bit[order[k]] ^ r) * (height >> (k + 1))
            out.append(off)
        return jnp.stack(out).astype(jnp.int32)

    offs = [[offsets(s, f) for f in range(2)] for s in range(len(orders))]
    partial_shape = jax.ShapeDtypeStruct((workers, LANES), jnp.float32)

    chunks = 16
    x, partial = pl.pallas_call(
        functools.partial(load_body, chunks),
        out_shape=(jax.ShapeDtypeStruct(x.shape, x.dtype), partial_shape),
        in_specs=[pl.BlockSpec(memory_space=pl.ANY), VM],
        out_specs=(VM, VM),
        scratch_shapes=[pltpu.SemaphoreType.DMA((chunks,))],
        compiler_params=PARAMS,
        name="load",
    )(x, center)

    def squares(s, first, value):
        return pl.pallas_call(
            functools.partial(square_body, count),
            out_shape=partial_shape, in_specs=[SM, VM, VM], out_specs=VM, compiler_params=PARAMS, name="squares",
        )(offs[s][first], x, value)

    def weigh(s, first, value, relative, step, squared):
        return pl.pallas_call(
            functools.partial(weigh_body, count, relative, devices, workers * devices, root_total),
            out_shape=jax.ShapeDtypeStruct((height >> 1, LANES), jnp.float32),
            in_specs=[SM, SM, VM, VM, VM, VM], out_specs=VM, compiler_params=PARAMS, name="weigh",
        )(offs[s][first], radius[step][None], x, value, squared, outside[step])

    def exchange(value, d):
        return lax.ppermute(value, "worker", swap(devices, d))

    outside = [jnp.broadcast_to(outside_sq[t][:, None], (workers, LANES)) for t in range(iters)]
    value = None
    for t in range(iters):
        for b in range(bits_of(parts)):
            partial = partial + lax.ppermute(partial, "mp", swap(parts, b))
        squared = partial
        hold = []
        for s in range(len(orders)):
            sent = weigh(s, 1, center if t == 0 else value[s][1], t > 0, t, squared)
            hold.append(exchange(sent, orders[s][0]))
        for s in range(len(orders)):
            hold[s] = hold[s] + weigh(s, 0, center if t == 0 else value[s][0], t > 0, t, squared)
        for k in range(1, levels - 1):
            for s in range(len(orders)):
                half = hold[s].shape[0] // 2
                hold[s] = hold[s][:half] + exchange(hold[s][half:], orders[s][k])
        for s in range(len(orders)):
            hold[s] = hold[s] + exchange(hold[s], orders[s][levels - 1])
        for k in reversed(range(1, levels - 1)):
            for s in range(len(orders)):
                hold[s] = jnp.concatenate([hold[s], exchange(hold[s], orders[s][k])], axis=0)
        value = [[hold[s], exchange(hold[s], orders[s][0])] for s in range(len(orders))]
        if t + 1 < iters:
            partial = None
            for first in range(2):
                for s in range(len(orders)):
                    one = squares(s, first, value[s][first])
                    partial = one if partial is None else partial + one

    norms = jnp.sqrt(jnp.sum(squared, axis=1) + outside_sq[iters - 1])
    final = []
    for s in range(len(orders)):
        tree = [value[s][f][j * piece:(j + 1) * piece] for f in range(2) for j in range(count)]
        for k in reversed(range(levels - 1)):
            turned = bit[orders[s][k]] == 1
            tree = [
                jnp.where(turned, jnp.concatenate([b, a]), jnp.concatenate([a, b]))
                for a, b in zip(tree[0::2], tree[1::2])
            ]
        final.append(tree[0])
    return jnp.concatenate(final).reshape(size), norms


def solution(mesh):
    placed = (P("worker", "mp"), P("mp"), P(None, "worker"), P())
    return jax.shard_map(
        shards, mesh=mesh, in_specs=placed, out_specs=(P("mp"), P("worker")), check_vma=False
    )
```

time: 334 us -> 175 us (0.52)
  waiting for transfers between devices: 233 us -> 46.5 us
  other arithmetic: 63.3 us -> 2.68 us
  starting transfers between devices: 0.12 us -> 51.2 us
  Pallas kernels: 0 us -> 47.6 us
  local copies, waits for them, and re-layouts: 0.68 us -> 25.8 us
  blocking collectives: 21.4 us -> 0 us
  between operations: 15.8 us -> 1.1 us
    psum x3 -> x0, waiting for transfers between devices: 233 us -> none  [shards(): summed = lax.psum(local, 'worker')]
    reduce_sum x6 -> x1, other arithmetic: 57.8 us -> 0.11 us  [shards(): norms = jnp.sqrt(jnp.sum(squared, axis=1) + outside_sq[iters - 1])]
    ppermute x0 -> x36, starting transfers between devices: none -> 51.2 us  [the longest x30 44.7 us: exchange(): return lax.ppermute(value, 'worker', swap(devices, d))]
    pallas_call x0 -> x21, Pallas kernels: none -> 47.6 us  [the longest x12 33.6 us: weigh(): pl.pallas_call(functools.partial(weigh_body, count, relative, devices, wo...]
    ppermute x0 -> x36, waiting for transfers between devices: none -> 46.5 us  [the longest x30 38.2 us: exchange(): return lax.ppermute(value, 'worker', swap(devices, d))]
    unnamed x6 -> x22, local copies, waits for them, and re-layouts: 0.01 us -> 24.8 us
    psum x3 -> x0, blocking collectives: 21.4 us -> none  [shards(): squared = lax.psum(partial_value, 'mp') + outside_sq[step]]
    add x3 -> x25, other arithmetic: 4.95 us -> 0.43 us  [the longest x6 0.21 us: shards(): hold[s] + weigh(s, 0, center if t == 0 else value[s][0], t > 0, t, squared)]
  transfers between devices with their start and end apart: 3 -> 36, of which waited for: 3 -> 29; matrix products, arithmetic and copies ran while one was open for 0% -> 1% of each run, Pallas kernels for 0% -> 19%
where the time goes in v1:
time: 175 us
  starting transfers between devices  51.2 us (29%)
  Pallas kernels  47.6 us (27%)
  waiting for transfers between devices  46.5 us (27%)
  local copies, waits for them, and re-layouts  25.8 us (15%)
  other arithmetic  2.68 us (2%)
    ppermute x30, starting transfers between devices, exchange(): return lax.ppermute(value, 'worker', swap(devices, d))  44.7 us
    ppermute x30, waiting for transfers between devices, exchange(): return lax.ppermute(value, 'worker', swap(devices, d))  38.2 us
    pallas_call x12, Pallas kernels, weigh(): pl.pallas_call(functools.partial(weigh_body, count, relative, devices, wo...  33.6 us
    unnamed x22, local copies, waits for them, and re-layouts  24.8 us
    pallas_call x8, Pallas kernels, squares(): pl.pallas_call(functools.partial(square_body, count), out_shape=partial_s...  10.4 us
    ppermute x6, waiting for transfers between devices, shards(): partial = partial + lax.ppermute(partial, 'mp', swap(parts, b))  8.34 us
    ppermute x6, starting transfers between devices, shards(): partial = partial + lax.ppermute(partial, 'mp', swap(parts, b))  6.44 us
    pallas_call x1, Pallas kernels, shards(): pl.pallas_call(functools.partial(load_body, chunks), out_shape=(jax.Shape...  3.56 us
  transfers between devices with their start and end apart: 36, of which 29 were waited for; matrix products, arithmetic and copies ran while one was open for 1% of the time, Pallas kernels for 19%

profile of v1, /device:TPU:0, one launch (start us, length us, event | category | flops | bytes accessed | tf_op | source)
XLA Modules:
  0.0 174.8 jit_solution(9786792485597046718)
XLA Ops:
  1.9 3.4 %copy-done.8 = bf16[16,262144]{1,0:T(8,128)(2,1)S(1)} copy-done((bf16[16,262144]{1,0:T(8,128)(2,1)S(1)}, bf16[16,262144]{1,0:T(8,128)(2,1)}, u32[]{:S(2)}) %copy-start.8) | copy-done | bytes 8388632
  5.3 3.6 %load.1 = (bf16[2,16384,128]{2,1,0:T(8,128)(2,1)S(1)}, f32[16,128]{1,0:T(8,128)S(1)}) custom-call(bf16[2,16384,128]{2,1,0:T(8,128)(2,1)S(1)} %bitcast.29, f32[2048,128]{1,0:T(8,128)S(1)} %bitcast.24), custom_call_target="tpu_custom_call" | custom-call | tf_op jit(solution)/shard_map/load/pallas_call | solution.py:164
  8.8 3.3 %copy-done = bf16[2,16384,128]{2,1,0:T(8,128)(2,1)} copy-done((bf16[2,16384,128]{2,1,0:T(8,128)(2,1)}, bf16[2,16384,128]{2,1,0:T(8,128)(2,1)S(1)}, u32[]{:S(2)}) %copy-start) | copy-done | bytes 8388632
  13.5 2.8 %collective-permute-start.1 = (f32[16,128]{1,0:T(8,128)S(1)}, f32[16,128]{1,0:T(8,128)S(1)}, u32[]{:S(2)}, u32[]{:S(2)}) collective-permute-start(f32[16,128]{1,0:T(8,128)S(1)} %add.127), channel_id=1, source_target_pairs={{0,2},{1,3},{2,0},{3,1},{4,6},{5,7},{6,4},{7,5},{8,10},{9,11},{10,... | collective-permute-start | bytes 24584 | tf_op jit(solution)/shard_map/ppermute | solution.py:194
  18.0 3.4 %copy-done.1 = bf16[2,16384,128]{2,1,0:T(8,128)(2,1)S(1)} copy-done((bf16[2,16384,128]{2,1,0:T(8,128)(2,1)S(1)}, bf16[2,16384,128]{2,1,0:T(8,128)(2,1)}, u32[]{:S(2)}) %copy-start.1) | copy-done | bytes 8388632
  21.4 2.8 %weigh.12 = f32[512,128]{1,0:T(8,128)S(1)} custom-call(s32[2]{0:T(128)S(1)} %pad_add_fusion.offs_ref, f32[1]{0:T(128)} %get-tuple-element.19.radius_ref, bf16[2,16384,128]{2,1,0:T(8,128)(2,1)S(1)} %copy-done.1, f32[2048,128]{1,0:T(8,128)S(1)} %bitcast.25, f32[16,128]{1,0:T(8,128)S(1)} %add.128.s_ref, f32[16,128]{1,0:T(8,128)S(1)} %broadcast_in_dim.22.out_ref), custom_call_target="tpu_custom_call" | custom-call | tf_op jit(solution)/shard_map/weigh/pallas_call | solution.py:181
  26.3 3.4 %copy-done.2 = bf16[2,16384,128]{2,1,0:T(8,128)(2,1)S(1)} copy-done((bf16[2,16384,128]{2,1,0:T(8,128)(2,1)S(1)}, bf16[2,16384,128]{2,1,0:T(8,128)(2,1)}, u32[]{:S(2)}) %copy-start.2) | copy-done | bytes 8388632
  29.7 2.8 %weigh.14 = f32[512,128]{1,0:T(8,128)S(1)} custom-call(s32[2]{0:T(128)S(1)} %pad_add_fusion.3.offs_ref, f32[1]{0:T(128)} %get-tuple-element.19.radius_ref, bf16[2,16384,128]{2,1,0:T(8,128)(2,1)S(1)} %copy-done.2, f32[2048,128]{1,0:T(8,128)S(1)} %bitcast.26, f32[16,128]{1,0:T(8,128)S(1)} %add.128.s_ref, f32[16,128]{1,0:T(8,128)S(1)} %broadcast_in_dim.22.out_ref), custom_call_target="tpu_custom_call" | custom-call | tf_op jit(solution)/shard_map/weigh/pallas_call | solution.py:181
  34.2 3.4 %copy-done.3 = bf16[2,16384,128]{2,1,0:T(8,128)(2,1)S(1)} copy-done((bf16[2,16384,128]{2,1,0:T(8,128)(2,1)S(1)}, bf16[2,16384,128]{2,1,0:T(8,128)(2,1)}, u32[]{:S(2)}) %copy-start.3) | copy-done | bytes 8388632
  37.6 2.8 %weigh.13 = f32[512,128]{1,0:T(8,128)S(1)} custom-call(s32[2]{0:T(128)S(1)} %pad_add_fusion.1.offs_ref, f32[1]{0:T(128)} %get-tuple-element.19.radius_ref, bf16[2,16384,128]{2,1,0:T(8,128)(2,1)S(1)} %copy-done.3, f32[2048,128]{1,0:T(8,128)S(1)} %bitcast.27, f32[16,128]{1,0:T(8,128)S(1)} %add.128.s_ref, f32[16,128]{1,0:T(8,128)S(1)} %broadcast_in_dim.22.out_ref), custom_call_target="tpu_custom_call" | custom-call | tf_op jit(solution)/shard_map/weigh/pallas_call | solution.py:181
  41.0 3.4 %copy-done.4 = bf16[2,16384,128]{2,1,0:T(8,128)(2,1)S(1)} copy-done((bf16[2,16384,128]{2,1,0:T(8,128)(2,1)S(1)}, bf16[2,16384,128]{2,1,0:T(8,128)(2,1)}, u32[]{:S(2)}) %copy-start.4) | copy-done | bytes 8388632
  44.4 2.8 %weigh.15 = f32[512,128]{1,0:T(8,128)S(1)} custom-call(s32[2]{0:T(128)S(1)} %pad_add_fusion.2.offs_ref, f32[1]{0:T(128)} %get-tuple-element.19.radius_ref, bf16[2,16384,128]{2,1,0:T(8,128)(2,1)S(1)} %copy-done.4, f32[2048,128]{1,0:T(8,128)S(1)} %bitcast.28, f32[16,128]{1,0:T(8,128)S(1)} %add.128.s_ref, f32[16,128]{1,0:T(8,128)S(1)} %broadcast_in_dim.22.out_ref), custom_call_target="tpu_custom_call" | custom-call | tf_op jit(solution)/shard_map/weigh/pallas_call | solution.py:181
  47.4 3.1 %collective-permute-start.4 = (f32[256,128]{1,0:T(8,128)S(1)}, f32[256,128]{1,0:T(8,128)S(1)}, u32[]{:S(2)}, u32[]{:S(2)}) collective-permute-start(f32[256,128]{1,0:T(8,128)S(1)} %slice_add_fusion.5), channel_id=1, source_target_pairs={{0,16},{4,20},{8,24},{12,28},{16,0},{20,4},{24,8},{28,12},{1,17},{... | collective-permute-start | bytes 393224 | tf_op jit(solution)/shard_map/ppermute | solution.py:188
  52.3 2.7 %collective-permute-start.9 = (f32[256,128]{1,0:T(8,128)S(1)}, f32[256,128]{1,0:T(8,128)S(1)}, u32[]{:S(2)}, u32[]{:S(2)}) collective-permute-start(f32[256,128]{1,0:T(8,128)S(1)} %slice_add_fusion.4), channel_id=1, source_target_pairs={{0,16},{4,20},{8,24},{12,28},{16,0},{20,4},{24,8},{28,12},{1,17},{... | collective-permute-start | bytes 393224 | tf_op jit(solution)/shard_map/ppermute | solution.py:188
  56.8 3.3 %collective-permute-start.5 = (f32[256,128]{1,0:T(8,128)S(1)}, f32[256,128]{1,0:T(8,128)S(1)}, u32[]{:S(2)}, u32[]{:S(2)}) collective-permute-start(f32[256,128]{1,0:T(8,128)S(1)} %add.133), channel_id=1, source_target_pairs={{0,8},{4,12},{8,0},{12,4},{16,24},{20,28},{24,16},{28,20},{1,9},{5... | collective-permute-start | bytes 393224 | tf_op jit(solution)/shard_map/ppermute | solution.py:188
  63.1 2.7 %collective-permute-start.6 = (f32[512,128]{1,0:T(8,128)S(1)}, f32[512,128]{1,0:T(8,128)S(1)}, u32[]{:S(2)}, u32[]{:S(2)}) collective-permute-start(f32[512,128]{1,0:T(8,128)S(1)} %pad_maximum_fusion.v_ref), channel_id=1, source_target_pairs={{0,4},{4,0},{8,12},{12,8},{16,20},{20,16},{24,28},{28,24},{1,5},{5... | collective-permute-start | bytes 786440 | tf_op jit(solution)/shard_map/ppermute | solution.py:188
  68.0 3.4 %copy-done.5 = bf16[2,16384,128]{2,1,0:T(8,128)(2,1)S(1)} copy-done((bf16[2,16384,128]{2,1,0:T(8,128)(2,1)S(1)}, bf16[2,16384,128]{2,1,0:T(8,128)(2,1)}, u32[]{:S(2)}) %copy-start.5) | copy-done | bytes 8388632
  81.7 2.8 %weigh.16 = f32[512,128]{1,0:T(8,128)S(1)} custom-call(s32[2]{0:T(128)S(1)} %pad_add_fusion.offs_ref, f32[1]{0:T(128)} %get-tuple-element.21.radius_ref, bf16[2,16384,128]{2,1,0:T(8,128)(2,1)S(1)} %copy-done.5, f32[512,128]{1,0:T(8,128)S(1)} %collective-permute-done.6.v_ref, f32[16,128]{1,0:T(8,128)S(1)} %add.147.s_ref, f32[16,128]{1,0:T(8,128)S(1)} %broadcast_in_dim.24.out_ref), custom_call_target="tpu_custom_call" | custom-call | tf_op jit(solution)/shard_map/weigh/pallas_call | solution.py:181
  85.9 2.8 %weigh.18 = f32[512,128]{1,0:T(8,128)S(1)} custom-call(s32[2]{0:T(128)S(1)} %pad_add_fusion.3.offs_ref, f32[1]{0:T(128)} %get-tuple-element.21.radius_ref, bf16[2,16384,128]{2,1,0:T(8,128)(2,1)S(1)} %copy-done.5, f32[512,128]{1,0:T(8,128)S(1)} %collective-permute-done.11.v_ref, f32[16,128]{1,0:T(8,128)S(1)} %add.147.s_ref, ...), custom_call_target="tpu_custom_call" | custom-call | tf_op jit(solution)/shard_map/weigh/pallas_call | solution.py:181
  90.1 2.8 %weigh.17 = f32[512,128]{1,0:T(8,128)S(1)} custom-call(s32[2]{0:T(128)S(1)} %pad_add_fusion.1.offs_ref, f32[1]{0:T(128)} %get-tuple-element.21.radius_ref, bf16[2,16384,128]{2,1,0:T(8,128)(2,1)S(1)} %copy-done.5, f32[512,128]{1,0:T(8,128)S(1)} %pad_maximum_fusion.v_ref, f32[16,128]{1,0:T(8,128)S(1)} %add.147.s_ref, f32[16,128]{1,0:T(8,128)S(1)} %broadcast_in_dim.24.out_ref), custom_call_target="tpu_custom_call" | custom-call | tf_op jit(solution)/shard_map/weigh/pallas_call | solution.py:181
  93.8 2.8 %weigh.19 = f32[512,128]{1,0:T(8,128)S(1)} custom-call(s32[2]{0:T(128)S(1)} %pad_add_fusion.2.offs_ref, f32[1]{0:T(128)} %get-tuple-element.21.radius_ref, bf16[2,16384,128]{2,1,0:T(8,128)(2,1)S(1)} %copy-done.5, f32[512,128]{1,0:T(8,128)S(1)} %pad_maximum_fusion.1.v_ref, f32[16,128]{1,0:T(8,128)S(1)} %add.147.s_ref, f32[16,128]{1,0:T(8,128)S(1)} %broadcast_in_dim.24.out_ref), custom_call_target="tpu_custom_call" | custom-call | tf_op jit(solution)/shard_map/weigh/pallas_call | solution.py:181
  98.6 3.3 %collective-permute-start.16 = (f32[256,128]{1,0:T(8,128)S(1)}, f32[256,128]{1,0:T(8,128)S(1)}, u32[]{:S(2)}, u32[]{:S(2)}) collective-permute-start(f32[256,128]{1,0:T(8,128)S(1)} %slice_add_fusion.3), channel_id=1, source_target_pairs={{0,16},{4,20},{8,24},{12,28},{16,0},{20,4},{24,8},{28,12},{1,17},{... | collective-permute-start | bytes 393224 | tf_op jit(solution)/shard_map/ppermute | solution.py:188
  102.3 3.3 %collective-permute-start.21 = (f32[256,128]{1,0:T(8,128)S(1)}, f32[256,128]{1,0:T(8,128)S(1)}, u32[]{:S(2)}, u32[]{:S(2)}) collective-permute-start(f32[256,128]{1,0:T(8,128)S(1)} %slice_add_fusion.2), channel_id=1, source_target_pairs={{0,16},{4,20},{8,24},{12,28},{16,0},{20,4},{24,8},{28,12},{1,17},{... | collective-permute-start | bytes 393224 | tf_op jit(solution)/shard_map/ppermute | solution.py:188
  105.6 5.0 %collective-permute-done.16 = f32[256,128]{1,0:T(8,128)S(1)} collective-permute-done((f32[256,128]{1,0:T(8,128)S(1)}, f32[256,128]{1,0:T(8,128)S(1)}, u32[]{:S(2)}, u32[]{:S(2)}) %collective-permute-start.16) | collective-permute-done | bytes 131104 | tf_op jit(solution)/shard_map/ppermute | solution.py:188
  112.9 2.7 %collective-permute-done.17 = f32[256,128]{1,0:T(8,128)S(1)} collective-permute-done((f32[256,128]{1,0:T(8,128)S(1)}, f32[256,128]{1,0:T(8,128)S(1)}, u32[]{:S(2)}, u32[]{:S(2)}) %collective-permute-start.17) | collective-permute-done | bytes 131104 | tf_op jit(solution)/shard_map/ppermute | solution.py:188
  131.3 2.8 %weigh.20 = f32[512,128]{1,0:T(8,128)S(1)} custom-call(s32[2]{0:T(128)S(1)} %pad_add_fusion.offs_ref, f32[1]{0:T(128)} %get-tuple-element.20.radius_ref, bf16[2,16384,128]{2,1,0:T(8,128)(2,1)S(1)} %copy-done.5, f32[512,128]{1,0:T(8,128)S(1)} %collective-permute-done.18.v_ref, f32[16,128]{1,0:T(8,128)S(1)} %get-tuple-element.7.s_ref, ...), custom_call_target="tpu_custom_call" | custom-call | tf_op jit(solution)/shard_map/weigh/pallas_call | solution.py:181
  135.0 2.8 %weigh.22 = f32[512,128]{1,0:T(8,128)S(1)} custom-call(s32[2]{0:T(128)S(1)} %pad_add_fusion.3.offs_ref, f32[1]{0:T(128)} %get-tuple-element.20.radius_ref, bf16[2,16384,128]{2,1,0:T(8,128)(2,1)S(1)} %copy-done.5, f32[512,128]{1,0:T(8,128)S(1)} %collective-permute-done.23.v_ref, f32[16,128]{1,0:T(8,128)S(1)} %get-tuple-element.7.s_ref, ...), custom_call_target="tpu_custom_call" | custom-call | tf_op jit(solution)/shard_map/weigh/pallas_call | solution.py:181
  138.6 2.8 %weigh.21 = f32[512,128]{1,0:T(8,128)S(1)} custom-call(s32[2]{0:T(128)S(1)} %pad_add_fusion.1.offs_ref, f32[1]{0:T(128)} %get-tuple-element.20.radius_ref, bf16[2,16384,128]{2,1,0:T(8,128)(2,1)S(1)} %copy-done.5, f32[512,128]{1,0:T(8,128)S(1)} %pad_maximum_fusion.2.v_ref, f32[16,128]{1,0:T(8,128)S(1)} %get-tuple-element.7.s_ref, ...), custom_call_target="tpu_custom_call" | custom-call | tf_op jit(solution)/shard_map/weigh/pallas_call | solution.py:181
  142.8 2.8 %weigh.23 = f32[512,128]{1,0:T(8,128)S(1)} custom-call(s32[2]{0:T(128)S(1)} %pad_add_fusion.2.offs_ref, f32[1]{0:T(128)} %get-tuple-element.20.radius_ref, bf16[2,16384,128]{2,1,0:T(8,128)(2,1)S(1)} %copy-done.5, f32[512,128]{1,0:T(8,128)S(1)} %pad_maximum_fusion.3.v_ref, f32[16,128]{1,0:T(8,128)S(1)} %get-tuple-element.7.s_ref, ...), custom_call_target="tpu_custom_call" | custom-call | tf_op jit(solution)/shard_map/weigh/pallas_call | solution.py:181
  147.6 2.3 %collective-permute-start.28 = (f32[256,128]{1,0:T(8,128)S(1)}, f32[256,128]{1,0:T(8,128)S(1)}, u32[]{:S(2)}, u32[]{:S(2)}) collective-permute-start(f32[256,128]{1,0:T(8,128)S(1)} %slice_add_fusion.1), channel_id=1, source_target_pairs={{0,16},{4,20},{8,24},{12,28},{16,0},{20,4},{24,8},{28,12},{1,17},{... | collective-permute-start | bytes 393224 | tf_op jit(solution)/shard_map/ppermute | solution.py:188
  153.6 5.7 %collective-permute-done.28 = f32[256,128]{1,0:T(8,128)S(1)} collective-permute-done((f32[256,128]{1,0:T(8,128)S(1)}, f32[256,128]{1,0:T(8,128)S(1)}, u32[]{:S(2)}, u32[]{:S(2)}) %collective-permute-start.28) | collective-permute-done | bytes 131104 | tf_op jit(solution)/shard_map/ppermute | solution.py:188
  168.0 3.6 %collective-permute-done.30 = f32[512,128]{1,0:T(8,128)S(1)} collective-permute-done((f32[512,128]{1,0:T(8,128)S(1)}, f32[512,128]{1,0:T(8,128)S(1)}, u32[]{:S(2)}, u32[]{:S(2)}) %collective-permute-start.30) | collective-permute-done | bytes 262176 | tf_op jit(solution)/shard_map/ppermute | solution.py:188
  (138 shorter events, 72.6 us)
Async XLA Ops:
  13.5 4.4 %collective-permute-start.1 = (f32[16,128]{1,0:T(8,128)S(1)}, f32[16,128]{1,0:T(8,128)S(1)}, u32[]{:S(2)}, u32[]{:S(2)}) collective-permute-start(f32[16,128]{1,0:T(8,128)S(1)} %add.127), channel_id=1, source_target_pairs={{0,2},{1,3},{2,0},{3,1},{4,6},{5,7},{6,4},{7,5},{8,10},{9,11},{10,... | collective-permute-start | bytes 24584 | tf_op jit(solution)/shard_map/ppermute | solution.py:194
  24.1 16.2 %collective-permute-start.2 = (f32[512,128]{1,0:T(8,128)S(1)}, f32[512,128]{1,0:T(8,128)S(1)}, u32[]{:S(2)}, u32[]{:S(2)}) collective-permute-start(f32[512,128]{1,0:T(8,128)S(1)} %weigh.12), channel_id=1, source_target_pairs={{0,4},{4,0},{8,12},{12,8},{16,20},{20,16},{24,28},{28,24},{1,5},{5... | collective-permute-start | bytes 786440 | tf_op jit(solution)/shard_map/ppermute | solution.py:188
  32.5 14.7 %collective-permute-start.7 = (f32[512,128]{1,0:T(8,128)S(1)}, f32[512,128]{1,0:T(8,128)S(1)}, u32[]{:S(2)}, u32[]{:S(2)}) collective-permute-start(f32[512,128]{1,0:T(8,128)S(1)} %weigh.14), channel_id=1, source_target_pairs={{0,8},{4,12},{8,0},{12,4},{16,24},{20,28},{24,16},{28,20},{1,9},{5... | collective-permute-start | bytes 786440 | tf_op jit(solution)/shard_map/ppermute | solution.py:188
  40.4 7.0 %collective-permute-start.3 = (f32[256,128]{1,0:T(8,128)S(1)}, f32[256,128]{1,0:T(8,128)S(1)}, u32[]{:S(2)}, u32[]{:S(2)}) collective-permute-start(f32[256,128]{1,0:T(8,128)S(1)} %slice.101), channel_id=1, source_target_pairs={{0,8},{4,12},{8,0},{12,4},{16,24},{20,28},{24,16},{28,20},{1,9},{5... | collective-permute-start | bytes 393224 | tf_op jit(solution)/shard_map/ppermute | solution.py:188
  47.2 5.0 %collective-permute-start.8 = (f32[256,128]{1,0:T(8,128)S(1)}, f32[256,128]{1,0:T(8,128)S(1)}, u32[]{:S(2)}, u32[]{:S(2)}) collective-permute-start(f32[256,128]{1,0:T(8,128)S(1)} %slice.103), channel_id=1, source_target_pairs={{0,4},{4,0},{8,12},{12,8},{16,20},{20,16},{24,28},{28,24},{1,5},{5... | collective-permute-start | bytes 393224 | tf_op jit(solution)/shard_map/ppermute | solution.py:188
  47.4 9.4 %collective-permute-start.4 = (f32[256,128]{1,0:T(8,128)S(1)}, f32[256,128]{1,0:T(8,128)S(1)}, u32[]{:S(2)}, u32[]{:S(2)}) collective-permute-start(f32[256,128]{1,0:T(8,128)S(1)} %slice_add_fusion.5), channel_id=1, source_target_pairs={{0,16},{4,20},{8,24},{12,28},{16,0},{20,4},{24,8},{28,12},{1,17},{... | collective-permute-start | bytes 393224 | tf_op jit(solution)/shard_map/ppermute | solution.py:188
  52.3 8.2 %collective-permute-start.9 = (f32[256,128]{1,0:T(8,128)S(1)}, f32[256,128]{1,0:T(8,128)S(1)}, u32[]{:S(2)}, u32[]{:S(2)}) collective-permute-start(f32[256,128]{1,0:T(8,128)S(1)} %slice_add_fusion.4), channel_id=1, source_target_pairs={{0,16},{4,20},{8,24},{12,28},{16,0},{20,4},{24,8},{28,12},{1,17},{... | collective-permute-start | bytes 393224 | tf_op jit(solution)/shard_map/ppermute | solution.py:188
  56.8 6.2 %collective-permute-start.5 = (f32[256,128]{1,0:T(8,128)S(1)}, f32[256,128]{1,0:T(8,128)S(1)}, u32[]{:S(2)}, u32[]{:S(2)}) collective-permute-start(f32[256,128]{1,0:T(8,128)S(1)} %add.133), channel_id=1, source_target_pairs={{0,8},{4,12},{8,0},{12,4},{16,24},{20,28},{24,16},{28,20},{1,9},{5... | collective-permute-start | bytes 393224 | tf_op jit(solution)/shard_map/ppermute | solution.py:188
  60.5 6.4 %collective-permute-start.10 = (f32[256,128]{1,0:T(8,128)S(1)}, f32[256,128]{1,0:T(8,128)S(1)}, u32[]{:S(2)}, u32[]{:S(2)}) collective-permute-start(f32[256,128]{1,0:T(8,128)S(1)} %add.142), channel_id=1, source_target_pairs={{0,4},{4,0},{8,12},{12,8},{16,20},{20,16},{24,28},{28,24},{1,5},{5... | collective-permute-start | bytes 393224 | tf_op jit(solution)/shard_map/ppermute | solution.py:188
  63.1 10.9 %collective-permute-start.6 = (f32[512,128]{1,0:T(8,128)S(1)}, f32[512,128]{1,0:T(8,128)S(1)}, u32[]{:S(2)}, u32[]{:S(2)}) collective-permute-start(f32[512,128]{1,0:T(8,128)S(1)} %pad_maximum_fusion.v_ref), channel_id=1, source_target_pairs={{0,4},{4,0},{8,12},{12,8},{16,20},{20,16},{24,28},{28,24},{1,5},{5... | collective-permute-start | bytes 786440 | tf_op jit(solution)/shard_map/ppermute | solution.py:188
  66.9 8.4 %collective-permute-start.11 = (f32[512,128]{1,0:T(8,128)S(1)}, f32[512,128]{1,0:T(8,128)S(1)}, u32[]{:S(2)}, u32[]{:S(2)}) collective-permute-start(f32[512,128]{1,0:T(8,128)S(1)} %pad_maximum_fusion.1.v_ref), channel_id=1, source_target_pairs={{0,8},{4,12},{8,0},{12,4},{16,24},{20,28},{24,16},{28,20},{1,9},{5... | collective-permute-start | bytes 786440 | tf_op jit(solution)/shard_map/ppermute | solution.py:188
  84.5 8.5 %collective-permute-start.14 = (f32[512,128]{1,0:T(8,128)S(1)}, f32[512,128]{1,0:T(8,128)S(1)}, u32[]{:S(2)}, u32[]{:S(2)}) collective-permute-start(f32[512,128]{1,0:T(8,128)S(1)} %weigh.16), channel_id=1, source_target_pairs={{0,4},{4,0},{8,12},{12,8},{16,20},{20,16},{24,28},{28,24},{1,5},{5... | collective-permute-start | bytes 786440 | tf_op jit(solution)/shard_map/ppermute | solution.py:188
  88.7 8.4 %collective-permute-start.19 = (f32[512,128]{1,0:T(8,128)S(1)}, f32[512,128]{1,0:T(8,128)S(1)}, u32[]{:S(2)}, u32[]{:S(2)}) collective-permute-start(f32[512,128]{1,0:T(8,128)S(1)} %weigh.18), channel_id=1, source_target_pairs={{0,8},{4,12},{8,0},{12,4},{16,24},{20,28},{24,16},{28,20},{1,9},{5... | collective-permute-start | bytes 786440 | tf_op jit(solution)/shard_map/ppermute | solution.py:188
  93.0 5.5 %collective-permute-start.15 = (f32[256,128]{1,0:T(8,128)S(1)}, f32[256,128]{1,0:T(8,128)S(1)}, u32[]{:S(2)}, u32[]{:S(2)}) collective-permute-start(f32[256,128]{1,0:T(8,128)S(1)} %slice.105), channel_id=1, source_target_pairs={{0,8},{4,12},{8,0},{12,4},{16,24},{20,28},{24,16},{28,20},{1,9},{5... | collective-permute-start | bytes 393224 | tf_op jit(solution)/shard_map/ppermute | solution.py:188
  97.2 5.0 %collective-permute-start.20 = (f32[256,128]{1,0:T(8,128)S(1)}, f32[256,128]{1,0:T(8,128)S(1)}, u32[]{:S(2)}, u32[]{:S(2)}) collective-permute-start(f32[256,128]{1,0:T(8,128)S(1)} %slice.107), channel_id=1, source_target_pairs={{0,4},{4,0},{8,12},{12,8},{16,20},{20,16},{24,28},{28,24},{1,5},{5... | collective-permute-start | bytes 393224 | tf_op jit(solution)/shard_map/ppermute | solution.py:188
  98.6 12.0 %collective-permute-start.16 = (f32[256,128]{1,0:T(8,128)S(1)}, f32[256,128]{1,0:T(8,128)S(1)}, u32[]{:S(2)}, u32[]{:S(2)}) collective-permute-start(f32[256,128]{1,0:T(8,128)S(1)} %slice_add_fusion.3), channel_id=1, source_target_pairs={{0,16},{4,20},{8,24},{12,28},{16,0},{20,4},{24,8},{28,12},{1,17},{... | collective-permute-start | bytes 393224 | tf_op jit(solution)/shard_map/ppermute | solution.py:188
  102.3 9.7 %collective-permute-start.21 = (f32[256,128]{1,0:T(8,128)S(1)}, f32[256,128]{1,0:T(8,128)S(1)}, u32[]{:S(2)}, u32[]{:S(2)}) collective-permute-start(f32[256,128]{1,0:T(8,128)S(1)} %slice_add_fusion.2), channel_id=1, source_target_pairs={{0,16},{4,20},{8,24},{12,28},{16,0},{20,4},{24,8},{28,12},{1,17},{... | collective-permute-start | bytes 393224 | tf_op jit(solution)/shard_map/ppermute | solution.py:188
  110.6 5.0 %collective-permute-start.17 = (f32[256,128]{1,0:T(8,128)S(1)}, f32[256,128]{1,0:T(8,128)S(1)}, u32[]{:S(2)}, u32[]{:S(2)}) collective-permute-start(f32[256,128]{1,0:T(8,128)S(1)} %add.150), channel_id=1, source_target_pairs={{0,8},{4,12},{8,0},{12,4},{16,24},{20,28},{24,16},{28,20},{1,9},{5... | collective-permute-start | bytes 393224 | tf_op jit(solution)/shard_map/ppermute | solution.py:188
  112.0 6.4 %collective-permute-start.22 = (f32[256,128]{1,0:T(8,128)S(1)}, f32[256,128]{1,0:T(8,128)S(1)}, u32[]{:S(2)}, u32[]{:S(2)}) collective-permute-start(f32[256,128]{1,0:T(8,128)S(1)} %add.153), channel_id=1, source_target_pairs={{0,4},{4,0},{8,12},{12,8},{16,20},{20,16},{24,28},{28,24},{1,5},{5... | collective-permute-start | bytes 393224 | tf_op jit(solution)/shard_map/ppermute | solution.py:188
  115.6 6.4 %collective-permute-start.18 = (f32[512,128]{1,0:T(8,128)S(1)}, f32[512,128]{1,0:T(8,128)S(1)}, u32[]{:S(2)}, u32[]{:S(2)}) collective-permute-start(f32[512,128]{1,0:T(8,128)S(1)} %pad_maximum_fusion.2.v_ref), channel_id=1, source_target_pairs={{0,4},{4,0},{8,12},{12,8},{16,20},{20,16},{24,28},{28,24},{1,5},{5... | collective-permute-start | bytes 786440 | tf_op jit(solution)/shard_map/ppermute | solution.py:188
  118.5 6.4 %collective-permute-start.23 = (f32[512,128]{1,0:T(8,128)S(1)}, f32[512,128]{1,0:T(8,128)S(1)}, u32[]{:S(2)}, u32[]{:S(2)}) collective-permute-start(f32[512,128]{1,0:T(8,128)S(1)} %pad_maximum_fusion.3.v_ref), channel_id=1, source_target_pairs={{0,8},{4,12},{8,0},{12,4},{16,24},{20,28},{24,16},{28,20},{1,9},{5... | collective-permute-start | bytes 786440 | tf_op jit(solution)/shard_map/ppermute | solution.py:188
  127.5 3.7 %collective-permute-start.25 = (f32[16,128]{1,0:T(8,128)S(1)}, f32[16,128]{1,0:T(8,128)S(1)}, u32[]{:S(2)}, u32[]{:S(2)}) collective-permute-start(f32[16,128]{1,0:T(8,128)S(1)} %add.157), channel_id=1, source_target_pairs={{0,2},{1,3},{2,0},{3,1},{4,6},{5,7},{6,4},{7,5},{8,10},{9,11},{10,... | collective-permute-start | bytes 24584 | tf_op jit(solution)/shard_map/ppermute | solution.py:194
  134.1 7.3 %collective-permute-start.26 = (f32[512,128]{1,0:T(8,128)S(1)}, f32[512,128]{1,0:T(8,128)S(1)}, u32[]{:S(2)}, u32[]{:S(2)}) collective-permute-start(f32[512,128]{1,0:T(8,128)S(1)} %weigh.20), channel_id=1, source_target_pairs={{0,4},{4,0},{8,12},{12,8},{16,20},{20,16},{24,28},{28,24},{1,5},{5... | collective-permute-start | bytes 786440 | tf_op jit(solution)/shard_map/ppermute | solution.py:188
  137.8 8.4 %collective-permute-start.31 = (f32[512,128]{1,0:T(8,128)S(1)}, f32[512,128]{1,0:T(8,128)S(1)}, u32[]{:S(2)}, u32[]{:S(2)}) collective-permute-start(f32[512,128]{1,0:T(8,128)S(1)} %weigh.22), channel_id=1, source_target_pairs={{0,8},{4,12},{8,0},{12,4},{16,24},{20,28},{24,16},{28,20},{1,9},{5... | collective-permute-start | bytes 786440 | tf_op jit(solution)/shard_map/ppermute | solution.py:188
  141.5 6.2 %collective-permute-start.27 = (f32[256,128]{1,0:T(8,128)S(1)}, f32[256,128]{1,0:T(8,128)S(1)}, u32[]{:S(2)}, u32[]{:S(2)}) collective-permute-start(f32[256,128]{1,0:T(8,128)S(1)} %slice.109), channel_id=1, source_target_pairs={{0,8},{4,12},{8,0},{12,4},{16,24},{20,28},{24,16},{28,20},{1,9},{5... | collective-permute-start | bytes 393224 | tf_op jit(solution)/shard_map/ppermute | solution.py:188
  146.3 5.0 %collective-permute-start.32 = (f32[256,128]{1,0:T(8,128)S(1)}, f32[256,128]{1,0:T(8,128)S(1)}, u32[]{:S(2)}, u32[]{:S(2)}) collective-permute-start(f32[256,128]{1,0:T(8,128)S(1)} %slice.113), channel_id=1, source_target_pairs={{0,4},{4,0},{8,12},{12,8},{16,20},{20,16},{24,28},{28,24},{1,5},{5... | collective-permute-start | bytes 393224 | tf_op jit(solution)/shard_map/ppermute | solution.py:188
  147.6 11.6 %collective-permute-start.28 = (f32[256,128]{1,0:T(8,128)S(1)}, f32[256,128]{1,0:T(8,128)S(1)}, u32[]{:S(2)}, u32[]{:S(2)}) collective-permute-start(f32[256,128]{1,0:T(8,128)S(1)} %slice_add_fusion.1), channel_id=1, source_target_pairs={{0,16},{4,20},{8,24},{12,28},{16,0},{20,4},{24,8},{28,12},{1,17},{... | collective-permute-start | bytes 393224 | tf_op jit(solution)/shard_map/ppermute | solution.py:188
  151.3 9.6 %collective-permute-start.33 = (f32[256,128]{1,0:T(8,128)S(1)}, f32[256,128]{1,0:T(8,128)S(1)}, u32[]{:S(2)}, u32[]{:S(2)}) collective-permute-start(f32[256,128]{1,0:T(8,128)S(1)} %slice_add_fusion), channel_id=1, source_target_pairs={{0,16},{4,20},{8,24},{12,28},{16,0},{20,4},{24,8},{28,12},{1,17},{... | collective-permute-start | bytes 393224 | tf_op jit(solution)/shard_map/ppermute | solution.py:188
  159.3 5.0 %collective-permute-start.29 = (f32[256,128]{1,0:T(8,128)S(1)}, f32[256,128]{1,0:T(8,128)S(1)}, u32[]{:S(2)}, u32[]{:S(2)}) collective-permute-start(f32[256,128]{1,0:T(8,128)S(1)} %add.161), channel_id=1, source_target_pairs={{0,8},{4,12},{8,0},{12,4},{16,24},{20,28},{24,16},{28,20},{1,9},{5... | collective-permute-start | bytes 393224 | tf_op jit(solution)/shard_map/ppermute | solution.py:188
  160.9 6.3 %collective-permute-start.34 = (f32[256,128]{1,0:T(8,128)S(1)}, f32[256,128]{1,0:T(8,128)S(1)}, u32[]{:S(2)}, u32[]{:S(2)}) collective-permute-start(f32[256,128]{1,0:T(8,128)S(1)} %add.164), channel_id=1, source_target_pairs={{0,4},{4,0},{8,12},{12,8},{16,20},{20,16},{24,28},{28,24},{1,5},{5... | collective-permute-start | bytes 393224 | tf_op jit(solution)/shard_map/ppermute | solution.py:188
  164.4 7.2 %collective-permute-start.30 = (f32[512,128]{1,0:T(8,128)S(1)}, f32[512,128]{1,0:T(8,128)S(1)}, u32[]{:S(2)}, u32[]{:S(2)}) collective-permute-start(f32[512,128]{1,0:T(8,128)S(1)} %get-tuple-element.10), channel_id=1, source_target_pairs={{0,4},{4,0},{8,12},{12,8},{16,20},{20,16},{24,28},{28,24},{1,5},{5... | collective-permute-start | bytes 786440 | tf_op jit(solution)/shard_map/ppermute | solution.py:188
  167.2 6.4 %collective-permute-start.35 = (f32[512,128]{1,0:T(8,128)S(1)}, f32[512,128]{1,0:T(8,128)S(1)}, u32[]{:S(2)}, u32[]{:S(2)}) collective-permute-start(f32[512,128]{1,0:T(8,128)S(1)} %get-tuple-element.14), channel_id=1, source_target_pairs={{0,8},{4,12},{8,0},{12,4},{16,24},{20,28},{24,16},{28,20},{1,9},{5... | collective-permute-start | bytes 786440 | tf_op jit(solution)/shard_map/ppermute | solution.py:188
  (15 other events, 69.0 us)

commit v2 on v1

--- a/solution.py
+++ b/solution.py
@@ -71,21 +71,28 @@
     store_carry(o_ref, acc)
 
 
-def square_body(pieces, offs_ref, x_ref, v_ref, o_ref):
+def square_body(offsets, x_ref, v_ref, o_ref):
+    offs = offsets()
+    pieces = len(offs)
     groups = x_ref.shape[0]
     rows = v_ref.shape[0] // pieces
     acc = zero_carry(groups)
     for j in range(pieces):
-        acc = square_rows(x_ref, pl.multiple_of(offs_ref[j], BLOCK), v_ref, j * rows, rows, acc, rows)
+        acc = square_rows(x_ref, pl.multiple_of(offs[j], BLOCK), v_ref, j * rows, rows, acc, rows)
     store_carry(o_ref, acc)
 
 
-def weigh_body(pieces, relative, devices, workers, root_total, offs_ref, radius_ref, x_ref, v_ref, s_ref, out_ref, o_ref):
+def weigh_body(offsets, relative, step_at, devices, workers, root_total, radius_ref, x_ref, v_ref, s_ref, out_ref, o_ref):
+    offs = offsets()
+    pieces = len(offs)
     groups = x_ref.shape[0]
+    own = groups * GROUP
     rows = o_ref.shape[0] // pieces
     depth = BLOCK * GROUP
-    squared = jnp.sum(s_ref[...], axis=1, keepdims=True) + out_ref[:, 0:1]
-    factor = jnp.minimum(jnp.float32(1.0), radius_ref[0] * root_total / jnp.sqrt(squared))
+    corner = lax.broadcasted_iota(jnp.int32, (own, own), 0) == lax.broadcasted_iota(jnp.int32, (own, own), 1)
+    outside = jnp.sum(jnp.where(corner, out_ref[step_at:step_at + 1, :], 0.0), axis=1, keepdims=True)
+    squared = jnp.sum(s_ref[...], axis=1, keepdims=True) + outside
+    factor = jnp.minimum(jnp.float32(1.0), radius_ref[step_at] * root_total / jnp.sqrt(squared))
     keep = jnp.float32(1.0 / devices) - jnp.sum(factor, axis=0, keepdims=True) / jnp.float32(workers)
     factor = factor / jnp.float32(workers)
     lane = lax.broadcasted_iota(jnp.int32, (GROUP, depth), 1)
@@ -101,7 +108,7 @@
         low = (full - high.astype(jnp.float32)).astype(jnp.bfloat16)
         weights.append(jnp.concatenate([high, low], axis=0))
     for j in range(pieces):
-        base = pl.multiple_of(offs_ref[j], BLOCK)
+        base = pl.multiple_of(offs[j], BLOCK)
 
         def step(i, _):
             at = base + i * 2 * BLOCK
@@ -119,7 +126,7 @@
                 o_ref[pl.ds(pl.multiple_of(o_at + h * BLOCK, BLOCK), BLOCK), :] = keep * old + total[:, h * LANES:(h + 1) * LANES]
             return 0
 
-        lax.fori_loop(0, rows // (2 * BLOCK), step, 0)
+        lax.fori_loop(0, rows // (2 * BLOCK), step, 0, unroll=min(4, rows // (2 * BLOCK)))
 
 
 VM = pl.BlockSpec(memory_space=pltpu.VMEM)
@@ -136,92 +143,103 @@
     root_total = float(size * parts) ** 0.5
     groups = workers // GROUP
     rows = size // LANES
-    position = lax.axis_index("worker")
-    bit = [(position >> d) & 1 for d in range(levels)]
     x = gradients.reshape(groups, GROUP, rows, LANES).transpose(0, 2, 1, 3).reshape(groups, rows * GROUP, LANES)
     center = center.reshape(rows, LANES)
 
     orders = [list(range(levels)), [1, 0] + list(range(2, levels))]
-    height = rows // len(orders)
+    streams = len(orders)
+    height = rows // streams
     count = 1 << (levels - 2)
     piece = height >> (levels - 1)
 
+    def turns(s):
+        position = lax.axis_index("worker")
+        odd = lax.axis_index("mp") & 1
+        out = []
+        for k in range(levels):
+            ways = [(position >> orders[(s + c) % 2][k]) & 1 for c in range(2)]
+            out.append(ways[0] + odd * (ways[1] - ways[0]))
+        return out
+
     def offsets(s, first):
-        order = orders[s]
+        bit = turns(s)
         out = []
         for j in range(count):
-            off = jnp.int32(s * height) + (bit[order[0]] ^ first) * (height >> 1)
+            off = s * height + (bit[0] ^ first) * (height >> 1)
             for k in range(1, levels - 1):
                 r = (j >> (levels - 2 - k)) & 1
-                off = off + (bit[order[k]] ^ r) * (height >> (k + 1))
+                off = off + (bit[k] ^ r) * (height >> (k + 1))
             out.append(off)
-        return jnp.stack(out).astype(jnp.int32)
-
-    offs = [[offsets(s, f) for f in range(2)] for s in range(len(orders))]
+        return out
+
     partial_shape = jax.ShapeDtypeStruct((workers, LANES), jnp.float32)
 
     chunks = 16
     x, partial = pl.pallas_call(
         functools.partial(load_body, chunks),
         out_shape=(jax.ShapeDtypeStruct(x.shape, x.dtype), partial_shape),
-        in_specs=[pl.BlockSpec(memory_space=pl.ANY), VM],
+        in_specs=[pl.BlockSpec(memory_space=pltpu.HBM), VM],
         out_specs=(VM, VM),
         scratch_shapes=[pltpu.SemaphoreType.DMA((chunks,))],
         compiler_params=PARAMS,
         name="load",
-    )(x, center)
+    )(pltpu.with_memory_space_constraint(x, pltpu.HBM), center)
 
     def squares(s, first, value):
         return pl.pallas_call(
-            functools.partial(square_body, count),
-            out_shape=partial_shape, in_specs=[SM, VM, VM], out_specs=VM, compiler_params=PARAMS, name="squares",
-        )(offs[s][first], x, value)
+            functools.partial(square_body, functools.partial(offsets, s, first)),
+            out_shape=partial_shape, in_specs=[VM, VM], out_specs=VM, compiler_params=PARAMS, name="squares",
+        )(x, value)
 
     def weigh(s, first, value, relative, step, squared):
         return pl.pallas_call(
-            functools.partial(weigh_body, count, relative, devices, workers * devices, root_total),
+            functools.partial(weigh_body, functools.partial(offsets, s, first), relative, step, devices, workers * devices, root_total),
             out_shape=jax.ShapeDtypeStruct((height >> 1, LANES), jnp.float32),
-            in_specs=[SM, SM, VM, VM, VM, VM], out_specs=VM, compiler_params=PARAMS, name="weigh",
-        )(offs[s][first], radius[step][None], x, value, squared, outside[step])
-
-    def exchange(value, d):
-        return lax.ppermute(value, "worker", swap(devices, d))
-
-    outside = [jnp.broadcast_to(outside_sq[t][:, None], (workers, LANES)) for t in range(iters)]
+            in_specs=[SM, VM, VM, VM, VM], out_specs=VM, compiler_params=PARAMS, name="weigh",
+        )(radius, x, value, squared, outside_sq)
+
+    def exchange(value, s, k):
+        pairs = []
+        for w in range(devices):
+            for m in range(parts):
+                other = w ^ (1 << orders[(s + m) % 2][k])
+                pairs.append((w * parts + m, other * parts + m))
+        return lax.ppermute(value, ("worker", "mp"), pairs)
+
     value = None
     for t in range(iters):
         for b in range(bits_of(parts)):
             partial = partial + lax.ppermute(partial, "mp", swap(parts, b))
         squared = partial
         hold = []
-        for s in range(len(orders)):
+        for s in range(streams):
             sent = weigh(s, 1, center if t == 0 else value[s][1], t > 0, t, squared)
-            hold.append(exchange(sent, orders[s][0]))
-        for s in range(len(orders)):
+            hold.append(exchange(sent, s, 0))
+        for s in range(streams):
             hold[s] = hold[s] + weigh(s, 0, center if t == 0 else value[s][0], t > 0, t, squared)
         for k in range(1, levels - 1):
-            for s in range(len(orders)):
+            for s in range(streams):
                 half = hold[s].shape[0] // 2
-                hold[s] = hold[s][:half] + exchange(hold[s][half:], orders[s][k])
-        for s in range(len(orders)):
-            hold[s] = hold[s] + exchange(hold[s], orders[s][levels - 1])
+                hold[s] = hold[s][:half] + exchange(hold[s][half:], s, k)
+        for s in range(streams):
+            hold[s] = hold[s] + exchange(hold[s], s, levels - 1)
         for k in reversed(range(1, levels - 1)):
-            for s in range(len(orders)):
-                hold[s] = jnp.concatenate([hold[s], exchange(hold[s], orders[s][k])], axis=0)
-        value = [[hold[s], exchange(hold[s], orders[s][0])] for s in range(len(orders))]
+            for s in range(streams):
+                hold[s] = jnp.concatenate([hold[s], exchange(hold[s], s, k)], axis=0)
+        value = [[hold[s], exchange(hold[s], s, 0)] for s in range(streams)]
         if t + 1 < iters:
             partial = None
             for first in range(2):
-                for s in range(len(orders)):
+                for s in range(streams):
                     one = squares(s, first, value[s][first])
                     partial = one if partial is None else partial + one
 
     norms = jnp.sqrt(jnp.sum(squared, axis=1) + outside_sq[iters - 1])
     final = []
-    for s in range(len(orders)):
+    for s in range(streams):
         tree = [value[s][f][j * piece:(j + 1) * piece] for f in range(2) for j in range(count)]
         for k in reversed(range(levels - 1)):
-            turned = bit[orders[s][k]] == 1
+            turned = turns(s)[k] == 1
             tree = [
                 jnp.where(turned, jnp.concatenate([b, a]), jnp.concatenate([a, b]))
                 for a, b in zip(tree[0::2], tree[1::2])

time: 175 us -> 143 us (0.82)
  waiting for transfers between devices: 46.5 us -> 75 us
  Pallas kernels: 47.6 us -> 22.8 us
  local copies, waits for them, and re-layouts: 25.8 us -> 1.34 us
  starting transfers between devices: 51.2 us -> 40.3 us
    ppermute x30, waiting for transfers between devices: 38.2 us -> 66 us  [exchange(): return lax.ppermute(value, ('worker', 'mp'), pairs)]
    pallas_call x20, Pallas kernels: 44 us -> 18.8 us  [the longest x12 13 us: weigh(): pl.pallas_call(functools.partial(weigh_body, functools.partial(offsets, s...]
    unnamed x22 -> x6, local copies, waits for them, and re-layouts: 24.8 us -> 1.24 us
    ppermute x30, starting transfers between devices: 44.7 us -> 33.8 us  [exchange(): return lax.ppermute(value, ('worker', 'mp'), pairs)]
  transfers between devices with their start and end apart: 36 -> 36, of which waited for: 29 -> 29; matrix products, arithmetic and copies ran while one was open for 1% -> 1% of each run, Pallas kernels for 19% -> 10%
where the time goes in v2:
time: 143 us
  waiting for transfers between devices  75 us (52%)
  starting transfers between devices  40.3 us (28%)
  Pallas kernels  22.8 us (16%)
  other arithmetic  2.38 us (2%)
    ppermute x30, waiting for transfers between devices, exchange(): return lax.ppermute(value, ('worker', 'mp'), pairs)  66 us
    ppermute x30, starting transfers between devices, exchange(): return lax.ppermute(value, ('worker', 'mp'), pairs)  33.8 us
    pallas_call x12, Pallas kernels, weigh(): pl.pallas_call(functools.partial(weigh_body, functools.partial(offsets, s...  13 us
    ppermute x6, waiting for transfers between devices, shards(): partial = partial + lax.ppermute(partial, 'mp', swap(parts, b))  9.06 us
    ppermute x6, starting transfers between devices, shards(): partial = partial + lax.ppermute(partial, 'mp', swap(parts, b))  6.53 us
    pallas_call x8, Pallas kernels, squares(): pl.pallas_call(functools.partial(square_body, functools.partial(offsets,...  5.85 us
    pallas_call x1, Pallas kernels, shards(): pl.pallas_call(functools.partial(load_body, chunks), out_shape=(jax.Shape...  4.02 us
  transfers between devices with their start and end apart: 36, of which 29 were waited for; matrix products, arithmetic and copies ran while one was open for 1% of the time, Pallas kernels for 10%

profile of v2, /device:TPU:0, one launch (start us, length us, event | category | flops | bytes accessed | tf_op | source)
XLA Modules:
  0.0 142.9 jit_solution(12740344146680665387)
XLA Ops:
  1.9 4.0 %load.1 = (bf16[2,16384,128]{2,1,0:T(8,128)(2,1)S(1)}, f32[16,128]{1,0:T(8,128)S(1)}) custom-call(bf16[2,16384,128]{2,1,0:T(8,128)(2,1)} %bitcast.17, f32[2048,128]{1,0:T(8,128)S(1)} %bitcast.12), custom_call_target="tpu_custom_call" | custom-call | tf_op jit(solution)/shard_map/load/pallas_call | solution.py:178
  7.3 2.8 %collective-permute-start.1 = (f32[16,128]{1,0:T(8,128)S(1)}, f32[16,128]{1,0:T(8,128)S(1)}, u32[]{:S(2)}, u32[]{:S(2)}) collective-permute-start(f32[16,128]{1,0:T(8,128)S(1)} %add.103), channel_id=1, source_target_pairs={{0,2},{1,3},{2,0},{3,1},{4,6},{5,7},{6,4},{7,5},{8,10},{9,11},{10,... | collective-permute-start | bytes 24584 | tf_op jit(solution)/shard_map/ppermute | solution.py:212
  10.1 1.6 %collective-permute-done.1 = f32[16,128]{1,0:T(8,128)S(1)} collective-permute-done((f32[16,128]{1,0:T(8,128)S(1)}, f32[16,128]{1,0:T(8,128)S(1)}, u32[]{:S(2)}, u32[]{:S(2)}) %collective-permute-start.1) | collective-permute-done | bytes 8224 | tf_op jit(solution)/shard_map/ppermute | solution.py:212
  12.8 2.1 %collective-permute-start.2 = (f32[512,128]{1,0:T(8,128)S(1)}, f32[512,128]{1,0:T(8,128)S(1)}, u32[]{:S(2)}, u32[]{:S(2)}) collective-permute-start(f32[512,128]{1,0:T(8,128)S(1)} %weigh.12), channel_id=1, source_target_pairs={{0,4},{1,9},{2,6},{3,11},{4,0},{5,13},{6,2},{7,15},{8,12},{9,1},{1... | collective-permute-start | bytes 786440 | tf_op jit(solution)/shard_map/ppermute | solution.py:207
  16.0 1.6 %collective-permute-start.7 = (f32[512,128]{1,0:T(8,128)S(1)}, f32[512,128]{1,0:T(8,128)S(1)}, u32[]{:S(2)}, u32[]{:S(2)}) collective-permute-start(f32[512,128]{1,0:T(8,128)S(1)} %weigh.14), channel_id=1, source_target_pairs={{0,8},{1,5},{2,10},{3,7},{4,12},{5,1},{6,14},{7,3},{8,0},{9,13},{1... | collective-permute-start | bytes 786440 | tf_op jit(solution)/shard_map/ppermute | solution.py:207
  18.8 2.4 %collective-permute-done.2 = f32[512,128]{1,0:T(8,128)S(1)} collective-permute-done((f32[512,128]{1,0:T(8,128)S(1)}, f32[512,128]{1,0:T(8,128)S(1)}, u32[]{:S(2)}, u32[]{:S(2)}) %collective-permute-start.2) | collective-permute-done | bytes 262176 | tf_op jit(solution)/shard_map/ppermute | solution.py:207
  21.2 3.1 %collective-permute-start.3 = (f32[256,128]{1,0:T(8,128)S(1)}, f32[256,128]{1,0:T(8,128)S(1)}, u32[]{:S(2)}, u32[]{:S(2)}) collective-permute-start(f32[256,128]{1,0:T(8,128)S(1)} %slice.71), channel_id=1, source_target_pairs={{0,8},{1,5},{2,10},{3,7},{4,12},{5,1},{6,14},{7,3},{8,0},{9,13},{1... | collective-permute-start | bytes 393224 | tf_op jit(solution)/shard_map/ppermute | solution.py:207
  25.5 1.6 %collective-permute-start.8 = (f32[256,128]{1,0:T(8,128)S(1)}, f32[256,128]{1,0:T(8,128)S(1)}, u32[]{:S(2)}, u32[]{:S(2)}) collective-permute-start(f32[256,128]{1,0:T(8,128)S(1)} %slice.73), channel_id=1, source_target_pairs={{0,4},{1,9},{2,6},{3,11},{4,0},{5,13},{6,2},{7,15},{8,12},{9,1},{1... | collective-permute-start | bytes 393224 | tf_op jit(solution)/shard_map/ppermute | solution.py:207
  27.1 2.1 %collective-permute-done.3 = f32[256,128]{1,0:T(8,128)S(1)} collective-permute-done((f32[256,128]{1,0:T(8,128)S(1)}, f32[256,128]{1,0:T(8,128)S(1)}, u32[]{:S(2)}, u32[]{:S(2)}) %collective-permute-start.3) | collective-permute-done | bytes 131104 | tf_op jit(solution)/shard_map/ppermute | solution.py:207
  29.2 2.2 %collective-permute-start.4 = (f32[256,128]{1,0:T(8,128)S(1)}, f32[256,128]{1,0:T(8,128)S(1)}, u32[]{:S(2)}, u32[]{:S(2)}) collective-permute-start(f32[256,128]{1,0:T(8,128)S(1)} %slice_add_fusion.5), channel_id=1, source_target_pairs={{0,16},{1,17},{2,18},{3,19},{4,20},{5,21},{6,22},{7,23},{8,24},{9,... | collective-permute-start | bytes 393224 | tf_op jit(solution)/shard_map/ppermute | solution.py:207
  31.4 1.8 %collective-permute-start.9 = (f32[256,128]{1,0:T(8,128)S(1)}, f32[256,128]{1,0:T(8,128)S(1)}, u32[]{:S(2)}, u32[]{:S(2)}) collective-permute-start(f32[256,128]{1,0:T(8,128)S(1)} %slice_add_fusion.4), channel_id=1, source_target_pairs={{0,16},{1,17},{2,18},{3,19},{4,20},{5,21},{6,22},{7,23},{8,24},{9,... | collective-permute-start | bytes 393224 | tf_op jit(solution)/shard_map/ppermute | solution.py:207
  33.2 5.4 %collective-permute-done.4 = f32[256,128]{1,0:T(8,128)S(1)} collective-permute-done((f32[256,128]{1,0:T(8,128)S(1)}, f32[256,128]{1,0:T(8,128)S(1)}, u32[]{:S(2)}, u32[]{:S(2)}) %collective-permute-start.4) | collective-permute-done | bytes 131104 | tf_op jit(solution)/shard_map/ppermute | solution.py:207
  41.5 3.5 %collective-permute-done.5 = f32[256,128]{1,0:T(8,128)S(1)} collective-permute-done((f32[256,128]{1,0:T(8,128)S(1)}, f32[256,128]{1,0:T(8,128)S(1)}, u32[]{:S(2)}, u32[]{:S(2)}) %collective-permute-start.5) | collective-permute-done | bytes 131104 | tf_op jit(solution)/shard_map/ppermute | solution.py:207
  48.7 2.8 %collective-permute-done.6.v_ref = f32[512,128]{1,0:T(8,128)S(1)} collective-permute-done((f32[512,128]{1,0:T(8,128)S(1)}, f32[512,128]{1,0:T(8,128)S(1)}, u32[]{:S(2)}, u32[]{:S(2)}) %collective-permute-start.6) | collective-permute-done | bytes 262176 | tf_op jit(solution)/shard_map/ppermute | solution.py:207
  54.8 1.5 %collective-permute-start.13 = (f32[16,128]{1,0:T(8,128)S(1)}, f32[16,128]{1,0:T(8,128)S(1)}, u32[]{:S(2)}, u32[]{:S(2)}) collective-permute-start(f32[16,128]{1,0:T(8,128)S(1)} %add.114), channel_id=1, source_target_pairs={{0,2},{1,3},{2,0},{3,1},{4,6},{5,7},{6,4},{7,5},{8,10},{9,11},{10,... | collective-permute-start | bytes 24584 | tf_op jit(solution)/shard_map/ppermute | solution.py:212
  56.3 2.1 %collective-permute-done.13 = f32[16,128]{1,0:T(8,128)S(1)} collective-permute-done((f32[16,128]{1,0:T(8,128)S(1)}, f32[16,128]{1,0:T(8,128)S(1)}, u32[]{:S(2)}, u32[]{:S(2)}) %collective-permute-start.13) | collective-permute-done | bytes 8224 | tf_op jit(solution)/shard_map/ppermute | solution.py:212
  63.7 5.1 %collective-permute-done.14 = f32[512,128]{1,0:T(8,128)S(1)} collective-permute-done((f32[512,128]{1,0:T(8,128)S(1)}, f32[512,128]{1,0:T(8,128)S(1)}, u32[]{:S(2)}, u32[]{:S(2)}) %collective-permute-start.14) | collective-permute-done | bytes 262176 | tf_op jit(solution)/shard_map/ppermute | solution.py:207
  71.5 3.3 %collective-permute-done.15 = f32[256,128]{1,0:T(8,128)S(1)} collective-permute-done((f32[256,128]{1,0:T(8,128)S(1)}, f32[256,128]{1,0:T(8,128)S(1)}, u32[]{:S(2)}, u32[]{:S(2)}) %collective-permute-start.15) | collective-permute-done | bytes 131104 | tf_op jit(solution)/shard_map/ppermute | solution.py:207
  75.7 2.2 %collective-permute-start.21 = (f32[256,128]{1,0:T(8,128)S(1)}, f32[256,128]{1,0:T(8,128)S(1)}, u32[]{:S(2)}, u32[]{:S(2)}) collective-permute-start(f32[256,128]{1,0:T(8,128)S(1)} %slice_add_fusion.2), channel_id=1, source_target_pairs={{0,16},{1,17},{2,18},{3,19},{4,20},{5,21},{6,22},{7,23},{8,24},{9,... | collective-permute-start | bytes 393224 | tf_op jit(solution)/shard_map/ppermute | solution.py:207
  77.9 5.8 %collective-permute-done.16 = f32[256,128]{1,0:T(8,128)S(1)} collective-permute-done((f32[256,128]{1,0:T(8,128)S(1)}, f32[256,128]{1,0:T(8,128)S(1)}, u32[]{:S(2)}, u32[]{:S(2)}) %collective-permute-start.16) | collective-permute-done | bytes 131104 | tf_op jit(solution)/shard_map/ppermute | solution.py:207
  86.4 2.8 %collective-permute-done.17 = f32[256,128]{1,0:T(8,128)S(1)} collective-permute-done((f32[256,128]{1,0:T(8,128)S(1)}, f32[256,128]{1,0:T(8,128)S(1)}, u32[]{:S(2)}, u32[]{:S(2)}) %collective-permute-start.17) | collective-permute-done | bytes 131104 | tf_op jit(solution)/shard_map/ppermute | solution.py:207
  92.6 3.0 %collective-permute-done.18.v_ref = f32[512,128]{1,0:T(8,128)S(1)} collective-permute-done((f32[512,128]{1,0:T(8,128)S(1)}, f32[512,128]{1,0:T(8,128)S(1)}, u32[]{:S(2)}, u32[]{:S(2)}) %collective-permute-start.18) | collective-permute-done | bytes 262176 | tf_op jit(solution)/shard_map/ppermute | solution.py:207
  99.0 1.5 %collective-permute-start.25 = (f32[16,128]{1,0:T(8,128)S(1)}, f32[16,128]{1,0:T(8,128)S(1)}, u32[]{:S(2)}, u32[]{:S(2)}) collective-permute-start(f32[16,128]{1,0:T(8,128)S(1)} %add.125), channel_id=1, source_target_pairs={{0,2},{1,3},{2,0},{3,1},{4,6},{5,7},{6,4},{7,5},{8,10},{9,11},{10,... | collective-permute-start | bytes 24584 | tf_op jit(solution)/shard_map/ppermute | solution.py:212
  100.5 2.2 %collective-permute-done.25 = f32[16,128]{1,0:T(8,128)S(1)} collective-permute-done((f32[16,128]{1,0:T(8,128)S(1)}, f32[16,128]{1,0:T(8,128)S(1)}, u32[]{:S(2)}, u32[]{:S(2)}) %collective-permute-start.25) | collective-permute-done | bytes 8224 | tf_op jit(solution)/shard_map/ppermute | solution.py:212
  103.9 1.7 %collective-permute-start.26 = (f32[512,128]{1,0:T(8,128)S(1)}, f32[512,128]{1,0:T(8,128)S(1)}, u32[]{:S(2)}, u32[]{:S(2)}) collective-permute-start(f32[512,128]{1,0:T(8,128)S(1)} %weigh.20), channel_id=1, source_target_pairs={{0,4},{1,9},{2,6},{3,11},{4,0},{5,13},{6,2},{7,15},{8,12},{9,1},{1... | collective-permute-start | bytes 786440 | tf_op jit(solution)/shard_map/ppermute | solution.py:207
  107.9 5.2 %collective-permute-done.26 = f32[512,128]{1,0:T(8,128)S(1)} collective-permute-done((f32[512,128]{1,0:T(8,128)S(1)}, f32[512,128]{1,0:T(8,128)S(1)}, u32[]{:S(2)}, u32[]{:S(2)}) %collective-permute-start.26) | collective-permute-done | bytes 262176 | tf_op jit(solution)/shard_map/ppermute | solution.py:207
  114.4 1.7 %collective-permute-start.32 = (f32[256,128]{1,0:T(8,128)S(1)}, f32[256,128]{1,0:T(8,128)S(1)}, u32[]{:S(2)}, u32[]{:S(2)}) collective-permute-start(f32[256,128]{1,0:T(8,128)S(1)} %slice.83), channel_id=1, source_target_pairs={{0,4},{1,9},{2,6},{3,11},{4,0},{5,13},{6,2},{7,15},{8,12},{9,1},{1... | collective-permute-start | bytes 393224 | tf_op jit(solution)/shard_map/ppermute | solution.py:207
  116.1 3.5 %collective-permute-done.27 = f32[256,128]{1,0:T(8,128)S(1)} collective-permute-done((f32[256,128]{1,0:T(8,128)S(1)}, f32[256,128]{1,0:T(8,128)S(1)}, u32[]{:S(2)}, u32[]{:S(2)}) %collective-permute-start.27) | collective-permute-done | bytes 131104 | tf_op jit(solution)/shard_map/ppermute | solution.py:207
  119.6 1.7 %collective-permute-start.28 = (f32[256,128]{1,0:T(8,128)S(1)}, f32[256,128]{1,0:T(8,128)S(1)}, u32[]{:S(2)}, u32[]{:S(2)}) collective-permute-start(f32[256,128]{1,0:T(8,128)S(1)} %slice_add_fusion.1), channel_id=1, source_target_pairs={{0,16},{1,17},{2,18},{3,19},{4,20},{5,21},{6,22},{7,23},{8,24},{9,... | collective-permute-start | bytes 393224 | tf_op jit(solution)/shard_map/ppermute | solution.py:207
  122.7 5.5 %collective-permute-done.28 = f32[256,128]{1,0:T(8,128)S(1)} collective-permute-done((f32[256,128]{1,0:T(8,128)S(1)}, f32[256,128]{1,0:T(8,128)S(1)}, u32[]{:S(2)}, u32[]{:S(2)}) %collective-permute-start.28) | collective-permute-done | bytes 131104 | tf_op jit(solution)/shard_map/ppermute | solution.py:207
  130.6 4.1 %collective-permute-done.29 = f32[256,128]{1,0:T(8,128)S(1)} collective-permute-done((f32[256,128]{1,0:T(8,128)S(1)}, f32[256,128]{1,0:T(8,128)S(1)}, u32[]{:S(2)}, u32[]{:S(2)}) %collective-permute-start.29) | collective-permute-done | bytes 131104 | tf_op jit(solution)/shard_map/ppermute | solution.py:207
  136.0 5.1 %collective-permute-done.30 = f32[512,128]{1,0:T(8,128)S(1)} collective-permute-done((f32[512,128]{1,0:T(8,128)S(1)}, f32[512,128]{1,0:T(8,128)S(1)}, u32[]{:S(2)}, u32[]{:S(2)}) %collective-permute-start.30) | collective-permute-done | bytes 262176 | tf_op jit(solution)/shard_map/ppermute | solution.py:207
  (113 shorter events, 47.0 us)
Async XLA Ops:
  7.3 4.4 %collective-permute-start.1 = (f32[16,128]{1,0:T(8,128)S(1)}, f32[16,128]{1,0:T(8,128)S(1)}, u32[]{:S(2)}, u32[]{:S(2)}) collective-permute-start(f32[16,128]{1,0:T(8,128)S(1)} %add.103), channel_id=1, source_target_pairs={{0,2},{1,3},{2,0},{3,1},{4,6},{5,7},{6,4},{7,5},{8,10},{9,11},{10,... | collective-permute-start | bytes 24584 | tf_op jit(solution)/shard_map/ppermute | solution.py:212
  12.8 8.3 %collective-permute-start.2 = (f32[512,128]{1,0:T(8,128)S(1)}, f32[512,128]{1,0:T(8,128)S(1)}, u32[]{:S(2)}, u32[]{:S(2)}) collective-permute-start(f32[512,128]{1,0:T(8,128)S(1)} %weigh.12), channel_id=1, source_target_pairs={{0,4},{1,9},{2,6},{3,11},{4,0},{5,13},{6,2},{7,15},{8,12},{9,1},{1... | collective-permute-start | bytes 786440 | tf_op jit(solution)/shard_map/ppermute | solution.py:207
  16.0 9.4 %collective-permute-start.7 = (f32[512,128]{1,0:T(8,128)S(1)}, f32[512,128]{1,0:T(8,128)S(1)}, u32[]{:S(2)}, u32[]{:S(2)}) collective-permute-start(f32[512,128]{1,0:T(8,128)S(1)} %weigh.14), channel_id=1, source_target_pairs={{0,8},{1,5},{2,10},{3,7},{4,12},{5,1},{6,14},{7,3},{8,0},{9,13},{1... | collective-permute-start | bytes 786440 | tf_op jit(solution)/shard_map/ppermute | solution.py:207
  21.2 7.9 %collective-permute-start.3 = (f32[256,128]{1,0:T(8,128)S(1)}, f32[256,128]{1,0:T(8,128)S(1)}, u32[]{:S(2)}, u32[]{:S(2)}) collective-permute-start(f32[256,128]{1,0:T(8,128)S(1)} %slice.71), channel_id=1, source_target_pairs={{0,8},{1,5},{2,10},{3,7},{4,12},{5,1},{6,14},{7,3},{8,0},{9,13},{1... | collective-permute-start | bytes 393224 | tf_op jit(solution)/shard_map/ppermute | solution.py:207
  25.5 5.9 %collective-permute-start.8 = (f32[256,128]{1,0:T(8,128)S(1)}, f32[256,128]{1,0:T(8,128)S(1)}, u32[]{:S(2)}, u32[]{:S(2)}) collective-permute-start(f32[256,128]{1,0:T(8,128)S(1)} %slice.73), channel_id=1, source_target_pairs={{0,4},{1,9},{2,6},{3,11},{4,0},{5,13},{6,2},{7,15},{8,12},{9,1},{1... | collective-permute-start | bytes 393224 | tf_op jit(solution)/shard_map/ppermute | solution.py:207
  29.2 9.4 %collective-permute-start.4 = (f32[256,128]{1,0:T(8,128)S(1)}, f32[256,128]{1,0:T(8,128)S(1)}, u32[]{:S(2)}, u32[]{:S(2)}) collective-permute-start(f32[256,128]{1,0:T(8,128)S(1)} %slice_add_fusion.5), channel_id=1, source_target_pairs={{0,16},{1,17},{2,18},{3,19},{4,20},{5,21},{6,22},{7,23},{8,24},{9,... | collective-permute-start | bytes 393224 | tf_op jit(solution)/shard_map/ppermute | solution.py:207
  31.4 8.7 %collective-permute-start.9 = (f32[256,128]{1,0:T(8,128)S(1)}, f32[256,128]{1,0:T(8,128)S(1)}, u32[]{:S(2)}, u32[]{:S(2)}) collective-permute-start(f32[256,128]{1,0:T(8,128)S(1)} %slice_add_fusion.4), channel_id=1, source_target_pairs={{0,16},{1,17},{2,18},{3,19},{4,20},{5,21},{6,22},{7,23},{8,24},{9,... | collective-permute-start | bytes 393224 | tf_op jit(solution)/shard_map/ppermute | solution.py:207
  38.6 6.4 %collective-permute-start.5 = (f32[256,128]{1,0:T(8,128)S(1)}, f32[256,128]{1,0:T(8,128)S(1)}, u32[]{:S(2)}, u32[]{:S(2)}) collective-permute-start(f32[256,128]{1,0:T(8,128)S(1)} %add.107), channel_id=1, source_target_pairs={{0,8},{1,5},{2,10},{3,7},{4,12},{5,1},{6,14},{7,3},{8,0},{9,13},{1... | collective-permute-start | bytes 393224 | tf_op jit(solution)/shard_map/ppermute | solution.py:207
  40.1 6.3 %collective-permute-start.10 = (f32[256,128]{1,0:T(8,128)S(1)}, f32[256,128]{1,0:T(8,128)S(1)}, u32[]{:S(2)}, u32[]{:S(2)}) collective-permute-start(f32[256,128]{1,0:T(8,128)S(1)} %add.110), channel_id=1, source_target_pairs={{0,4},{1,9},{2,6},{3,11},{4,0},{5,13},{6,2},{7,15},{8,12},{9,1},{1... | collective-permute-start | bytes 393224 | tf_op jit(solution)/shard_map/ppermute | solution.py:207
  45.0 6.4 %collective-permute-start.6 = (f32[512,128]{1,0:T(8,128)S(1)}, f32[512,128]{1,0:T(8,128)S(1)}, u32[]{:S(2)}, u32[]{:S(2)}) collective-permute-start(f32[512,128]{1,0:T(8,128)S(1)} %pad_maximum_fusion.v_ref), channel_id=1, source_target_pairs={{0,4},{1,9},{2,6},{3,11},{4,0},{5,13},{6,2},{7,15},{8,12},{9,1},{1... | collective-permute-start | bytes 786440 | tf_op jit(solution)/shard_map/ppermute | solution.py:207
  46.3 6.4 %collective-permute-start.11 = (f32[512,128]{1,0:T(8,128)S(1)}, f32[512,128]{1,0:T(8,128)S(1)}, u32[]{:S(2)}, u32[]{:S(2)}) collective-permute-start(f32[512,128]{1,0:T(8,128)S(1)} %pad_maximum_fusion.1.v_ref), channel_id=1, source_target_pairs={{0,8},{1,5},{2,10},{3,7},{4,12},{5,1},{6,14},{7,3},{8,0},{9,13},{1... | collective-permute-start | bytes 786440 | tf_op jit(solution)/shard_map/ppermute | solution.py:207
  59.5 9.2 %collective-permute-start.14 = (f32[512,128]{1,0:T(8,128)S(1)}, f32[512,128]{1,0:T(8,128)S(1)}, u32[]{:S(2)}, u32[]{:S(2)}) collective-permute-start(f32[512,128]{1,0:T(8,128)S(1)} %weigh.16), channel_id=1, source_target_pairs={{0,4},{1,9},{2,6},{3,11},{4,0},{5,13},{6,2},{7,15},{8,12},{9,1},{1... | collective-permute-start | bytes 786440 | tf_op jit(solution)/shard_map/ppermute | solution.py:207
  62.0 8.6 %collective-permute-start.19 = (f32[512,128]{1,0:T(8,128)S(1)}, f32[512,128]{1,0:T(8,128)S(1)}, u32[]{:S(2)}, u32[]{:S(2)}) collective-permute-start(f32[512,128]{1,0:T(8,128)S(1)} %weigh.18), channel_id=1, source_target_pairs={{0,8},{1,5},{2,10},{3,7},{4,12},{5,1},{6,14},{7,3},{8,0},{9,13},{1... | collective-permute-start | bytes 786440 | tf_op jit(solution)/shard_map/ppermute | solution.py:207
  68.8 6.1 %collective-permute-start.15 = (f32[256,128]{1,0:T(8,128)S(1)}, f32[256,128]{1,0:T(8,128)S(1)}, u32[]{:S(2)}, u32[]{:S(2)}) collective-permute-start(f32[256,128]{1,0:T(8,128)S(1)} %slice.75), channel_id=1, source_target_pairs={{0,8},{1,5},{2,10},{3,7},{4,12},{5,1},{6,14},{7,3},{8,0},{9,13},{1... | collective-permute-start | bytes 393224 | tf_op jit(solution)/shard_map/ppermute | solution.py:207
  70.7 5.0 %collective-permute-start.20 = (f32[256,128]{1,0:T(8,128)S(1)}, f32[256,128]{1,0:T(8,128)S(1)}, u32[]{:S(2)}, u32[]{:S(2)}) collective-permute-start(f32[256,128]{1,0:T(8,128)S(1)} %slice.77), channel_id=1, source_target_pairs={{0,4},{1,9},{2,6},{3,11},{4,0},{5,13},{6,2},{7,15},{8,12},{9,1},{1... | collective-permute-start | bytes 393224 | tf_op jit(solution)/shard_map/ppermute | solution.py:207
  74.9 8.8 %collective-permute-start.16 = (f32[256,128]{1,0:T(8,128)S(1)}, f32[256,128]{1,0:T(8,128)S(1)}, u32[]{:S(2)}, u32[]{:S(2)}) collective-permute-start(f32[256,128]{1,0:T(8,128)S(1)} %slice_add_fusion.3), channel_id=1, source_target_pairs={{0,16},{1,17},{2,18},{3,19},{4,20},{5,21},{6,22},{7,23},{8,24},{9,... | collective-permute-start | bytes 393224 | tf_op jit(solution)/shard_map/ppermute | solution.py:207
  75.7 9.4 %collective-permute-start.21 = (f32[256,128]{1,0:T(8,128)S(1)}, f32[256,128]{1,0:T(8,128)S(1)}, u32[]{:S(2)}, u32[]{:S(2)}) collective-permute-start(f32[256,128]{1,0:T(8,128)S(1)} %slice_add_fusion.2), channel_id=1, source_target_pairs={{0,16},{1,17},{2,18},{3,19},{4,20},{5,21},{6,22},{7,23},{8,24},{9,... | collective-permute-start | bytes 393224 | tf_op jit(solution)/shard_map/ppermute | solution.py:207
  83.7 5.5 %collective-permute-start.17 = (f32[256,128]{1,0:T(8,128)S(1)}, f32[256,128]{1,0:T(8,128)S(1)}, u32[]{:S(2)}, u32[]{:S(2)}) collective-permute-start(f32[256,128]{1,0:T(8,128)S(1)} %add.118), channel_id=1, source_target_pairs={{0,8},{1,5},{2,10},{3,7},{4,12},{5,1},{6,14},{7,3},{8,0},{9,13},{1... | collective-permute-start | bytes 393224 | tf_op jit(solution)/shard_map/ppermute | solution.py:207
  85.1 5.5 %collective-permute-start.22 = (f32[256,128]{1,0:T(8,128)S(1)}, f32[256,128]{1,0:T(8,128)S(1)}, u32[]{:S(2)}, u32[]{:S(2)}) collective-permute-start(f32[256,128]{1,0:T(8,128)S(1)} %add.121), channel_id=1, source_target_pairs={{0,4},{1,9},{2,6},{3,11},{4,0},{5,13},{6,2},{7,15},{8,12},{9,1},{1... | collective-permute-start | bytes 393224 | tf_op jit(solution)/shard_map/ppermute | solution.py:207
  89.2 6.4 %collective-permute-start.18 = (f32[512,128]{1,0:T(8,128)S(1)}, f32[512,128]{1,0:T(8,128)S(1)}, u32[]{:S(2)}, u32[]{:S(2)}) collective-permute-start(f32[512,128]{1,0:T(8,128)S(1)} %pad_maximum_fusion.2.v_ref), channel_id=1, source_target_pairs={{0,4},{1,9},{2,6},{3,11},{4,0},{5,13},{6,2},{7,15},{8,12},{9,1},{1... | collective-permute-start | bytes 786440 | tf_op jit(solution)/shard_map/ppermute | solution.py:207
  90.6 6.4 %collective-permute-start.23 = (f32[512,128]{1,0:T(8,128)S(1)}, f32[512,128]{1,0:T(8,128)S(1)}, u32[]{:S(2)}, u32[]{:S(2)}) collective-permute-start(f32[512,128]{1,0:T(8,128)S(1)} %pad_maximum_fusion.3.v_ref), channel_id=1, source_target_pairs={{0,8},{1,5},{2,10},{3,7},{4,12},{5,1},{6,14},{7,3},{8,0},{9,13},{1... | collective-permute-start | bytes 786440 | tf_op jit(solution)/shard_map/ppermute | solution.py:207
  99.0 3.7 %collective-permute-start.25 = (f32[16,128]{1,0:T(8,128)S(1)}, f32[16,128]{1,0:T(8,128)S(1)}, u32[]{:S(2)}, u32[]{:S(2)}) collective-permute-start(f32[16,128]{1,0:T(8,128)S(1)} %add.125), channel_id=1, source_target_pairs={{0,2},{1,3},{2,0},{3,1},{4,6},{5,7},{6,4},{7,5},{8,10},{9,11},{10,... | collective-permute-start | bytes 24584 | tf_op jit(solution)/shard_map/ppermute | solution.py:212
  103.9 9.2 %collective-permute-start.26 = (f32[512,128]{1,0:T(8,128)S(1)}, f32[512,128]{1,0:T(8,128)S(1)}, u32[]{:S(2)}, u32[]{:S(2)}) collective-permute-start(f32[512,128]{1,0:T(8,128)S(1)} %weigh.20), channel_id=1, source_target_pairs={{0,4},{1,9},{2,6},{3,11},{4,0},{5,13},{6,2},{7,15},{8,12},{9,1},{1... | collective-permute-start | bytes 786440 | tf_op jit(solution)/shard_map/ppermute | solution.py:207
  106.7 7.7 %collective-permute-start.31 = (f32[512,128]{1,0:T(8,128)S(1)}, f32[512,128]{1,0:T(8,128)S(1)}, u32[]{:S(2)}, u32[]{:S(2)}) collective-permute-start(f32[512,128]{1,0:T(8,128)S(1)} %weigh.22), channel_id=1, source_target_pairs={{0,8},{1,5},{2,10},{3,7},{4,12},{5,1},{6,14},{7,3},{8,0},{9,13},{1... | collective-permute-start | bytes 786440 | tf_op jit(solution)/shard_map/ppermute | solution.py:207
  113.2 6.4 %collective-permute-start.27 = (f32[256,128]{1,0:T(8,128)S(1)}, f32[256,128]{1,0:T(8,128)S(1)}, u32[]{:S(2)}, u32[]{:S(2)}) collective-permute-start(f32[256,128]{1,0:T(8,128)S(1)} %slice.79), channel_id=1, source_target_pairs={{0,8},{1,5},{2,10},{3,7},{4,12},{5,1},{6,14},{7,3},{8,0},{9,13},{1... | collective-permute-start | bytes 393224 | tf_op jit(solution)/shard_map/ppermute | solution.py:207
  114.4 6.9 %collective-permute-start.32 = (f32[256,128]{1,0:T(8,128)S(1)}, f32[256,128]{1,0:T(8,128)S(1)}, u32[]{:S(2)}, u32[]{:S(2)}) collective-permute-start(f32[256,128]{1,0:T(8,128)S(1)} %slice.83), channel_id=1, source_target_pairs={{0,4},{1,9},{2,6},{3,11},{4,0},{5,13},{6,2},{7,15},{8,12},{9,1},{1... | collective-permute-start | bytes 393224 | tf_op jit(solution)/shard_map/ppermute | solution.py:207
  119.6 8.6 %collective-permute-start.28 = (f32[256,128]{1,0:T(8,128)S(1)}, f32[256,128]{1,0:T(8,128)S(1)}, u32[]{:S(2)}, u32[]{:S(2)}) collective-permute-start(f32[256,128]{1,0:T(8,128)S(1)} %slice_add_fusion.1), channel_id=1, source_target_pairs={{0,16},{1,17},{2,18},{3,19},{4,20},{5,21},{6,22},{7,23},{8,24},{9,... | collective-permute-start | bytes 393224 | tf_op jit(solution)/shard_map/ppermute | solution.py:207
  121.3 8.3 %collective-permute-start.33 = (f32[256,128]{1,0:T(8,128)S(1)}, f32[256,128]{1,0:T(8,128)S(1)}, u32[]{:S(2)}, u32[]{:S(2)}) collective-permute-start(f32[256,128]{1,0:T(8,128)S(1)} %slice_add_fusion), channel_id=1, source_target_pairs={{0,16},{1,17},{2,18},{3,19},{4,20},{5,21},{6,22},{7,23},{8,24},{9,... | collective-permute-start | bytes 393224 | tf_op jit(solution)/shard_map/ppermute | solution.py:207
  128.2 6.4 %collective-permute-start.29 = (f32[256,128]{1,0:T(8,128)S(1)}, f32[256,128]{1,0:T(8,128)S(1)}, u32[]{:S(2)}, u32[]{:S(2)}) collective-permute-start(f32[256,128]{1,0:T(8,128)S(1)} %add.129), channel_id=1, source_target_pairs={{0,8},{1,5},{2,10},{3,7},{4,12},{5,1},{6,14},{7,3},{8,0},{9,13},{1... | collective-permute-start | bytes 393224 | tf_op jit(solution)/shard_map/ppermute | solution.py:207
  129.6 5.7 %collective-permute-start.34 = (f32[256,128]{1,0:T(8,128)S(1)}, f32[256,128]{1,0:T(8,128)S(1)}, u32[]{:S(2)}, u32[]{:S(2)}) collective-permute-start(f32[256,128]{1,0:T(8,128)S(1)} %add.132), channel_id=1, source_target_pairs={{0,4},{1,9},{2,6},{3,11},{4,0},{5,13},{6,2},{7,15},{8,12},{9,1},{1... | collective-permute-start | bytes 393224 | tf_op jit(solution)/shard_map/ppermute | solution.py:207
  134.7 6.4 %collective-permute-start.30 = (f32[512,128]{1,0:T(8,128)S(1)}, f32[512,128]{1,0:T(8,128)S(1)}, u32[]{:S(2)}, u32[]{:S(2)}) collective-permute-start(f32[512,128]{1,0:T(8,128)S(1)} %get-tuple-element.10), channel_id=1, source_target_pairs={{0,4},{1,9},{2,6},{3,11},{4,0},{5,13},{6,2},{7,15},{8,12},{9,1},{1... | collective-permute-start | bytes 786440 | tf_op jit(solution)/shard_map/ppermute | solution.py:207
  135.3 6.4 %collective-permute-start.35 = (f32[512,128]{1,0:T(8,128)S(1)}, f32[512,128]{1,0:T(8,128)S(1)}, u32[]{:S(2)}, u32[]{:S(2)}) collective-permute-start(f32[512,128]{1,0:T(8,128)S(1)} %get-tuple-element.14), channel_id=1, source_target_pairs={{0,8},{1,5},{2,10},{3,7},{4,12},{5,1},{6,14},{7,3},{8,0},{9,13},{1... | collective-permute-start | bytes 786440 | tf_op jit(solution)/shard_map/ppermute | solution.py:207
  (7 other events, 31.0 us)

commit v3 on v2

v3 whole, which is shorter than its diff:
```python
import functools

import jax
import jax.numpy as jnp
from jax import lax
from jax.experimental import pallas as pl
from jax.experimental.pallas import tpu as pltpu
from jax.sharding import PartitionSpec as P

LANES = 128
GROUP = 8
BLOCK = 32
VMEM_LIMIT = 24 << 20
SHARES = (1, 1, 1, 1)
FULL = 1


def bits_of(size):
    count = size.bit_length() - 1
    assert 1 << count == size
    return count


def swap(size, bit):
    return [(i, i ^ (1 << bit)) for i in range(size)]


def square_rows(x_ref, x_row, v_ref, v_row, rows, carry):
    unroll = 16

    def step(i, acc):
        acc = list(acc)
        for r in range(0, unroll, 2):
            row = v_row + i * unroll + r
            first = v_ref[pl.ds(row, 1), :]
            second = v_ref[pl.ds(row + 1, 1), :]
            at = (x_row + i * unroll + r) * GROUP
            for g in range(len(acc) // 2):
                both = x_ref[g, pl.ds(pl.multiple_of(at, 2 * GROUP), 2 * GROUP), :].astype(jnp.float32)
                a = both[:GROUP] - first
                b = both[GROUP:] - second
                acc[2 * g] = acc[2 * g] + a * a
                acc[2 * g + 1] = acc[2 * g + 1] + b * b
        return tuple(acc)

    return lax.fori_loop(0, rows // unroll, step, carry)


def zero_carry(groups):
    return tuple(jnp.zeros((GROUP, LANES), jnp.float32) for _ in range(2 * groups))


def store_carry(o_ref, acc, extra_ref, step):
    for g in range(len(acc) // 2):
        total = acc[2 * g] + acc[2 * g + 1]
        if step is not None:
            total = total + extra_ref[step, g * GROUP:(g + 1) * GROUP, :]
        o_ref[g * GROUP:(g + 1) * GROUP, :] = total


def load_body(chunks, parts, x_hbm, v_hbm, out_ref, x_ref, v_ref, o_ref, extra_ref, sems):
    groups, total, _ = x_ref.shape
    rows = total // chunks
    per = rows // GROUP
    own = groups * GROUP

    def copies(c):
        window = pl.ds(c * rows, rows)
        part = pl.ds(c * per, per)
        return (
            pltpu.make_async_copy(x_hbm.at[:, window, :], x_ref.at[:, window, :], sems.at[0, c]),
            pltpu.make_async_copy(v_hbm.at[part, :], v_ref.at[part, :], sems.at[1, c]),
        )

    for c in range(chunks):
        for copy in copies(c):
            copy.start()
    corner = lax.broadcasted_iota(jnp.int32, (own, own), 0) == lax.broadcasted_iota(jnp.int32, (own, own), 1)
    lane = lax.broadcasted_iota(jnp.int32, (own, LANES), 1)
    for t in range(extra_ref.shape[0]):
        column = jnp.sum(jnp.where(corner, out_ref[t:t + 1, :], 0.0), axis=1, keepdims=True)
        extra_ref[t] = jnp.where(lane == 0, column / jnp.float32(parts), 0.0)
    acc = zero_carry(groups)
    for c in range(chunks):
        for copy in copies(c):
            copy.wait()
        acc = square_rows(x_ref, c * per, v_ref, c * per, per, acc)
    store_carry(o_ref, acc, extra_ref, 0)


def square_body(offsets, extra, x_ref, v_ref, *refs):
    offs = offsets()
    groups = x_ref.shape[0]
    rows = v_ref.shape[0] // len(offs)
    acc = zero_carry(groups)
    for j, off in enumerate(offs):
        acc = square_rows(x_ref, pl.multiple_of(off, BLOCK), v_ref, j * rows, rows, acc)
    store_carry(refs[-1], acc, refs[0], extra)


def build_weights(root, workers, devices, groups, s_ref, w_ref, k_ref):
    depth = BLOCK * GROUP
    ones = jnp.ones((GROUP, LANES), jnp.bfloat16)
    block = lax.broadcasted_iota(jnp.int32, (BLOCK, depth), 0)
    place = lax.broadcasted_iota(jnp.int32, (BLOCK, depth), 1)
    total = None
    for g in range(groups):
        one = s_ref[g * GROUP:(g + 1) * GROUP, :]
        two = jnp.concatenate([one, one], axis=0)
        high = two.astype(jnp.bfloat16)
        low = (two - high.astype(jnp.float32)).astype(jnp.bfloat16)
        squared = None
        for half in (high, low):
            tall = jnp.concatenate([half] * (BLOCK // 2), axis=0)
            part = lax.dot_general(ones, tall, (((1,), (1,)), ((), ())), preferred_element_type=jnp.float32)
            squared = part if squared is None else squared + part
        factor = jnp.minimum(jnp.float32(1.0), root / jnp.sqrt(squared))
        total = factor if total is None else total + factor
        factor = factor[0:1] / jnp.float32(workers)
        high = factor.astype(jnp.bfloat16).astype(jnp.float32)
        low = factor - high
        for h, half in enumerate((high, low)):
            w_ref[g, h * BLOCK:(h + 1) * BLOCK, :] = jnp.where(place // GROUP == block, half, 0.0).astype(jnp.bfloat16)
    share = jnp.sum(total, axis=1, keepdims=True) / jnp.float32(BLOCK * workers)
    k_ref[...] = jnp.broadcast_to(jnp.float32(1.0 / devices) - share, k_ref.shape)


def weigh_rows(offs, relative, x_ref, v_ref, w_ref, k_ref, o_ref):
    groups = x_ref.shape[0]
    rows = o_ref.shape[0] // len(offs)
    depth = BLOCK * GROUP
    keep = k_ref[0:1, :]
    steps = rows // (2 * BLOCK)
    for j, off in enumerate(offs):
        base = pl.multiple_of(off, BLOCK)

        def step(i, _):
            at = base + i * 2 * BLOCK
            total = None
            for g in range(groups):
                left = x_ref[g, pl.ds(pl.multiple_of(at * GROUP, depth), depth), :]
                right = x_ref[g, pl.ds(pl.multiple_of(at * GROUP + depth, depth), depth), :]
                part = jnp.dot(w_ref[g], jnp.concatenate([left, right], axis=1), preferred_element_type=jnp.float32)
                total = part if total is None else total + part
            total = total[:BLOCK] + total[BLOCK:]
            v_at = (j * rows if relative else base) + i * 2 * BLOCK
            o_at = j * rows + i * 2 * BLOCK
            for h in range(2):
                old = v_ref[pl.ds(pl.multiple_of(v_at + h * BLOCK, BLOCK), BLOCK), :]
                o_ref[pl.ds(pl.multiple_of(o_at + h * BLOCK, BLOCK), BLOCK), :] = keep * old + total[:, h * LANES:(h + 1) * LANES]
            return 0

        lax.fori_loop(0, steps, step, 0, unroll=min(4, steps))


def first_body(offsets, relative, step_at, devices, workers, root_total, radius_ref, x_ref, v_ref, s_ref, o_ref, w_ref, k_ref):
    build_weights(radius_ref[step_at] * root_total, workers, devices, x_ref.shape[0], s_ref, w_ref, k_ref)
    weigh_rows(offsets(), relative, x_ref, v_ref, w_ref, k_ref, o_ref)


def weigh_body(offsets, relative, x_ref, v_ref, w_ref, k_ref, o_ref):
    weigh_rows(offsets(), relative, x_ref, v_ref, w_ref, k_ref, o_ref)


VM = pl.BlockSpec(memory_space=pltpu.VMEM)
SM = pl.BlockSpec(memory_space=pltpu.SMEM)
PARAMS = pltpu.CompilerParams(vmem_limit_bytes=VMEM_LIMIT)


def shards(gradients, center, outside_sq, radius):
    workers, size = gradients.shape
    iters = outside_sq.shape[0]
    devices = lax.axis_size("worker")
    parts = lax.axis_size("mp")
    levels = bits_of(devices)
    root_total = float(size * parts) ** 0.5
    groups = workers // GROUP
    rows = size // LANES
    x = gradients.reshape(groups, GROUP, rows, LANES).transpose(0, 2, 1, 3).reshape(groups, rows * GROUP, LANES)
    center = center.reshape(rows, LANES)

    ways = [list(range(levels)), [1, 0] + list(range(2, levels))]
    streams = len(SHARES)
    split = levels - FULL
    count = 1 << (split - 1)
    heights = [rows * share // sum(SHARES) for share in SHARES]
    starts = [sum(heights[:s]) for s in range(streams)]

    def order(s, c):
        return ways[(s + c) % 2]

    def turns(s):
        position = lax.axis_index("worker")
        odd = lax.axis_index("mp") & 1
        out = []
        for k in range(split):
            even, uneven = [(position >> order(s, c)[k]) & 1 for c in range(2)]
            out.append(even + odd * (uneven - even))
        return out

    def offsets(s, first):
        bit = turns(s)
        out = []
        for j in range(count):
            off = starts[s] + (bit[0] ^ first) * (heights[s] >> 1)
            for k in range(1, split):
                r = (j >> (split - 1 - k)) & 1
                off = off + (bit[k] ^ r) * (heights[s] >> (k + 1))
            out.append(off)
        return out

    partial_shape = jax.ShapeDtypeStruct((workers, LANES), jnp.float32)

    chunks = 16
    x, center, partial, extra = pl.pallas_call(
        functools.partial(load_body, chunks, parts),
        out_shape=(
            jax.ShapeDtypeStruct(x.shape, x.dtype),
            jax.ShapeDtypeStruct(center.shape, center.dtype),
            partial_shape,
            jax.ShapeDtypeStruct((iters, workers, LANES), jnp.float32),
        ),
        in_specs=[pl.BlockSpec(memory_space=pltpu.HBM), pl.BlockSpec(memory_space=pltpu.HBM), VM],
        out_specs=(VM, VM, VM, VM),
        scratch_shapes=[pltpu.SemaphoreType.DMA((2, chunks))],
        compiler_params=PARAMS,
        name="load",
    )(pltpu.with_memory_space_constraint(x, pltpu.HBM), pltpu.with_memory_space_constraint(center, pltpu.HBM), outside_sq)

    def squares(s, first, value, step):
        more = [] if step is None else [extra]
        return pl.pallas_call(
            functools.partial(square_body, functools.partial(offsets, s, first), step),
            out_shape=partial_shape, in_specs=[VM] * (2 + len(more)), out_specs=VM, compiler_params=PARAMS, name="squares",
        )(x, value, *more)

    weight_shape = jax.ShapeDtypeStruct((groups, 2 * BLOCK, BLOCK * GROUP), jnp.bfloat16)
    keep_shape = jax.ShapeDtypeStruct((GROUP, LANES), jnp.float32)

    def half_shape(s):
        return jax.ShapeDtypeStruct((heights[s] >> 1, LANES), jnp.float32)

    def weigh_first(s, first, value, relative, step, squared):
        body = functools.partial(
            first_body, functools.partial(offsets, s, first), relative, step, devices, workers * devices, root_total
        )
        return pl.pallas_call(
            body, out_shape=(half_shape(s), weight_shape, keep_shape),
            in_specs=[SM, VM, VM, VM], out_specs=(VM, VM, VM), compiler_params=PARAMS, name="first",
        )(radius, x, value, squared)

    def weigh(s, first, value, relative, weights, keep):
        return pl.pallas_call(
            functools.partial(weigh_body, functools.partial(offsets, s, first), relative),
            out_shape=half_shape(s), in_specs=[VM, VM, VM, VM], out_specs=VM, compiler_params=PARAMS, name="weigh",
        )(x, value, weights, keep)

    def exchange(value, s, k):
        pairs = []
        for w in range(devices):
            for m in range(parts):
                other = w ^ (1 << order(s, m % 2)[k])
                pairs.append((w * parts + m, other * parts + m))
        return lax.ppermute(value, ("worker", "mp"), pairs)

    value = None
    for t in range(iters):
        for b in range(bits_of(parts)):
            partial = partial + lax.ppermute(partial, "mp", swap(parts, b))
        squared = partial
        hold = []
        relative = t > 0
        for s in range(streams):
            source = value[s][1] if relative else center
            if s == 0:
                sent, weights, keep = weigh_first(s, 1, source, relative, t, squared)
            else:
                sent = weigh(s, 1, source, relative, weights, keep)
            hold.append(exchange(sent, s, 0))
        for s in range(streams):
            source = value[s][0] if relative else center
            hold[s] = hold[s] + weigh(s, 0, source, relative, weights, keep)
        for k in range(1, split):
            for s in range(streams):
                half = hold[s].shape[0] // 2
                hold[s] = hold[s][:half] + exchange(hold[s][half:], s, k)
        for k in range(split, levels):
            for s in range(streams):
                hold[s] = hold[s] + exchange(hold[s], s, k)
        for k in reversed(range(1, split)):
            for s in range(streams):
                hold[s] = jnp.concatenate([hold[s], exchange(hold[s], s, k)], axis=0)
        value = [[hold[s], exchange(hold[s], s, 0)] for s in range(streams)]
        if t + 1 < iters:
            partial = None
            for first in range(2):
                for s in range(streams):
                    one = squares(s, first, value[s][first], t + 1 if partial is None else None)
                    partial = one if partial is None else partial + one

    norms = jnp.sqrt(jnp.sum(squared, axis=1))
    final = []
    for s in range(streams):
        piece = heights[s] >> split
        tree = [value[s][f][j * piece:(j + 1) * piece] for f in range(2) for j in range(count)]
        for k in reversed(range(split)):
            turned = turns(s)[k] == 1
            tree = [
                jnp.where(turned, jnp.concatenate([b, a]), jnp.concatenate([a, b]))
                for a, b in zip(tree[0::2], tree[1::2])
            ]
        final.append(tree[0])
    return jnp.concatenate(final).reshape(size), norms


def solution(mesh):
    placed = (P("worker", "mp"), P("mp"), P(None, "worker"), P())
    return jax.shard_map(
        shards, mesh=mesh, in_specs=placed, out_specs=(P("mp"), P("worker")), check_vma=False
    )
```

time: 143 us -> 135 us (0.944)
  waiting for transfers between devices: 75 us -> 33.3 us
  starting transfers between devices: 40.3 us -> 77 us
  Pallas kernels: 22.8 us -> 19.8 us
    ppermute x30 -> x60, waiting for transfers between devices: 66 us -> 24.2 us  [exchange(): return lax.ppermute(value, ('worker', 'mp'), pairs)]
    ppermute x30 -> x60, starting transfers between devices: 33.8 us -> 70.4 us  [exchange(): return lax.ppermute(value, ('worker', 'mp'), pairs)]
    pallas_call x12 -> x21, Pallas kernels: 13 us -> 6.45 us  [weigh(): pl.pallas_call(functools.partial(weigh_body, functools.partial(offsets, s...]
    pallas_call x1 -> x4, Pallas kernels: 4.02 us -> 7.2 us  [the longest x1 4.19 us: shards(): pl.pallas_call(functools.partial(load_body, chunks, parts), out_shape=(ja...]
    pallas_call x8 -> x16, Pallas kernels: 5.85 us -> 6.16 us  [squares(): pl.pallas_call(functools.partial(square_body, functools.partial(offsets,...]
  transfers between devices with their start and end apart: 36 -> 66, of which waited for: 29 -> 28; matrix products, arithmetic and copies ran while one was open for 1% -> 1% of each run, Pallas kernels for 10% -> 8%
where the time goes in v3:
time: 135 us
  starting transfers between devices  77 us (57%)
  waiting for transfers between devices  33.3 us (25%)
  Pallas kernels  19.8 us (15%)
  other arithmetic  1.93 us (1%)
  between operations  1.4 us (1%)
    ppermute x60, starting transfers between devices, exchange(): return lax.ppermute(value, ('worker', 'mp'), pairs)  70.4 us
    ppermute x60, waiting for transfers between devices, exchange(): return lax.ppermute(value, ('worker', 'mp'), pairs)  24.2 us
    ppermute x6, waiting for transfers between devices, shards(): partial = partial + lax.ppermute(partial, 'mp', swap(parts, b))  9.05 us
    ppermute x6, starting transfers between devices, shards(): partial = partial + lax.ppermute(partial, 'mp', swap(parts, b))  6.54 us
    pallas_call x21, Pallas kernels, weigh(): pl.pallas_call(functools.partial(weigh_body, functools.partial(offsets, s...  6.45 us
    pallas_call x16, Pallas kernels, squares(): pl.pallas_call(functools.partial(square_body, functools.partial(offsets,...  6.16 us
    pallas_call x1, Pallas kernels, shards(): pl.pallas_call(functools.partial(load_body, chunks, parts), out_shape=(ja...  4.19 us
    pallas_call x3, Pallas kernels, weigh_first(): pl.pallas_call(body, out_shape=(half_shape(s), weight_shape, keep_shape),...  3.02 us
  transfers between devices with their start and end apart: 66, of which 28 were waited for; matrix products, arithmetic and copies ran while one was open for 1% of the time, Pallas kernels for 8%

profile of v3, /device:TPU:0, one launch (start us, length us, event | category | flops | bytes accessed | tf_op | source)
XLA Modules:
  0.0 134.7 jit_solution(10232120330331748032)
XLA Ops:
  1.3 4.2 %load.1 = (bf16[2,16384,128]{2,1,0:T(8,128)(2,1)S(1)}, f32[2048,128]{1,0:T(8,128)S(1)}, f32[16,128]{1,0:T(8,128)S(1)}, f32[3,16,128]{2,1,0:T(8,128)S(1)}) custom-call(bf16[2,16384,128]{2,1,0:T(8,128)(2,1)} %bitcast.8, f32[2048,128]{1,0:T(8,128)} %bitcast.9, f32[3,16]{1,0:T(4,128)S(1)} %copy-done.1), custom_call_target="tpu_custom_call" | custom-call | tf_op jit(solution)/shard_map/load/pallas_call | solution.py:215
  6.9 2.8 %collective-permute-start.1 = (f32[16,128]{1,0:T(8,128)S(1)}, f32[16,128]{1,0:T(8,128)S(1)}, u32[]{:S(2)}, u32[]{:S(2)}) collective-permute-start(f32[16,128]{1,0:T(8,128)S(1)} %add.182), channel_id=1, source_target_pairs={{0,2},{1,3},{2,0},{3,1},{4,6},{5,7},{6,4},{7,5},{8,10},{9,11},{10,... | collective-permute-start | bytes 24584 | tf_op jit(solution)/shard_map/ppermute | solution.py:269
  9.7 1.6 %collective-permute-done.1 = f32[16,128]{1,0:T(8,128)S(1)} collective-permute-done((f32[16,128]{1,0:T(8,128)S(1)}, f32[16,128]{1,0:T(8,128)S(1)}, u32[]{:S(2)}, u32[]{:S(2)}) %collective-permute-start.1) | collective-permute-done | bytes 8224 | tf_op jit(solution)/shard_map/ppermute | solution.py:269
  12.7 2.2 %collective-permute-start.7 = (f32[256,128]{1,0:T(8,128)S(1)}, f32[256,128]{1,0:T(8,128)S(1)}, u32[]{:S(2)}, u32[]{:S(2)}) collective-permute-start(f32[256,128]{1,0:T(8,128)S(1)} %weigh.22), channel_id=1, source_target_pairs={{0,8},{1,5},{2,10},{3,7},{4,12},{5,1},{6,14},{7,3},{8,0},{9,13},{1... | collective-permute-start | bytes 393224 | tf_op jit(solution)/shard_map/ppermute | solution.py:264
  14.9 1.5 %collective-permute-start.2 = (f32[256,128]{1,0:T(8,128)S(1)}, f32[256,128]{1,0:T(8,128)S(1)}, u32[]{:S(2)}, u32[]{:S(2)}) collective-permute-start(f32[256,128]{1,0:T(8,128)S(1)} %get-tuple-element.18), channel_id=1, source_target_pairs={{0,4},{1,9},{2,6},{3,11},{4,0},{5,13},{6,2},{7,15},{8,12},{9,1},{1... | collective-permute-start | bytes 393224 | tf_op jit(solution)/shard_map/ppermute | solution.py:264
  19.3 2.0 %collective-permute-start.8 = (f32[128,128]{1,0:T(8,128)S(1)}, f32[128,128]{1,0:T(8,128)S(1)}, u32[]{:S(2)}, u32[]{:S(2)}) collective-permute-start(f32[128,128]{1,0:T(8,128)S(1)} %slice.135), channel_id=1, source_target_pairs={{0,4},{1,9},{2,6},{3,11},{4,0},{5,13},{6,2},{7,15},{8,12},{9,1},{1... | collective-permute-start | bytes 196616 | tf_op jit(solution)/shard_map/ppermute | solution.py:264
  22.3 1.6 %collective-permute-start.3 = (f32[128,128]{1,0:T(8,128)S(1)}, f32[128,128]{1,0:T(8,128)S(1)}, u32[]{:S(2)}, u32[]{:S(2)}) collective-permute-start(f32[128,128]{1,0:T(8,128)S(1)} %slice.133), channel_id=1, source_target_pairs={{0,8},{1,5},{2,10},{3,7},{4,12},{5,1},{6,14},{7,3},{8,0},{9,13},{1... | collective-permute-start | bytes 196616 | tf_op jit(solution)/shard_map/ppermute | solution.py:264
  25.6 2.7 %collective-permute-start.9 = (f32[128,128]{1,0:T(8,128)S(1)}, f32[128,128]{1,0:T(8,128)S(1)}, u32[]{:S(2)}, u32[]{:S(2)}) collective-permute-start(f32[128,128]{1,0:T(8,128)S(1)} %slice_add_fusion.10), channel_id=1, source_target_pairs={{0,16},{1,17},{2,18},{3,19},{4,20},{5,21},{6,22},{7,23},{8,24},{9,... | collective-permute-start | bytes 196616 | tf_op jit(solution)/shard_map/ppermute | solution.py:264
  29.3 2.4 %collective-permute-start.13 = (f32[128,128]{1,0:T(8,128)S(1)}, f32[128,128]{1,0:T(8,128)S(1)}, u32[]{:S(2)}, u32[]{:S(2)}) collective-permute-start(f32[128,128]{1,0:T(8,128)S(1)} %slice_add_fusion.9), channel_id=1, source_target_pairs={{0,16},{1,17},{2,18},{3,19},{4,20},{5,21},{6,22},{7,23},{8,24},{9,... | collective-permute-start | bytes 196616 | tf_op jit(solution)/shard_map/ppermute | solution.py:264
  32.4 3.3 %collective-permute-done.4 = f32[128,128]{1,0:T(8,128)S(1)} collective-permute-done((f32[128,128]{1,0:T(8,128)S(1)}, f32[128,128]{1,0:T(8,128)S(1)}, u32[]{:S(2)}, u32[]{:S(2)}) %collective-permute-start.4) | collective-permute-done | bytes 65568 | tf_op jit(solution)/shard_map/ppermute | solution.py:264
  41.5 1.3 collective-permute-start.19
  50.6 1.5 %collective-permute-start.23 = (f32[16,128]{1,0:T(8,128)S(1)}, f32[16,128]{1,0:T(8,128)S(1)}, u32[]{:S(2)}, u32[]{:S(2)}) collective-permute-start(f32[16,128]{1,0:T(8,128)S(1)} %add.203), channel_id=1, source_target_pairs={{0,2},{1,3},{2,0},{3,1},{4,6},{5,7},{6,4},{7,5},{8,10},{9,11},{10,... | collective-permute-start | bytes 24584 | tf_op jit(solution)/shard_map/ppermute | solution.py:269
  52.1 2.2 %collective-permute-done.23 = f32[16,128]{1,0:T(8,128)S(1)} collective-permute-done((f32[16,128]{1,0:T(8,128)S(1)}, f32[16,128]{1,0:T(8,128)S(1)}, u32[]{:S(2)}, u32[]{:S(2)}) %collective-permute-start.23) | collective-permute-done | bytes 8224 | tf_op jit(solution)/shard_map/ppermute | solution.py:269
  67.5 3.2 %collective-permute-start.31 = (f32[128,128]{1,0:T(8,128)S(1)}, f32[128,128]{1,0:T(8,128)S(1)}, u32[]{:S(2)}, u32[]{:S(2)}) collective-permute-start(f32[128,128]{1,0:T(8,128)S(1)} %slice_add_fusion.6), channel_id=1, source_target_pairs={{0,16},{1,17},{2,18},{3,19},{4,20},{5,21},{6,22},{7,23},{8,24},{9,... | collective-permute-start | bytes 196616 | tf_op jit(solution)/shard_map/ppermute | solution.py:264
  71.5 2.3 %collective-permute-start.35 = (f32[128,128]{1,0:T(8,128)S(1)}, f32[128,128]{1,0:T(8,128)S(1)}, u32[]{:S(2)}, u32[]{:S(2)}) collective-permute-start(f32[128,128]{1,0:T(8,128)S(1)} %slice_add_fusion.5), channel_id=1, source_target_pairs={{0,16},{1,17},{2,18},{3,19},{4,20},{5,21},{6,22},{7,23},{8,24},{9,... | collective-permute-start | bytes 196616 | tf_op jit(solution)/shard_map/ppermute | solution.py:264
  74.5 2.9 %collective-permute-done.26 = f32[128,128]{1,0:T(8,128)S(1)} collective-permute-done((f32[128,128]{1,0:T(8,128)S(1)}, f32[128,128]{1,0:T(8,128)S(1)}, u32[]{:S(2)}, u32[]{:S(2)}) %collective-permute-start.26) | collective-permute-done | bytes 65568 | tf_op jit(solution)/shard_map/ppermute | solution.py:264
  77.6 1.6 %collective-permute-start.32 = (f32[128,128]{1,0:T(8,128)S(1)}, f32[128,128]{1,0:T(8,128)S(1)}, u32[]{:S(2)}, u32[]{:S(2)}) collective-permute-start(f32[128,128]{1,0:T(8,128)S(1)} %add.210), channel_id=1, source_target_pairs={{0,4},{1,9},{2,6},{3,11},{4,0},{5,13},{6,2},{7,15},{8,12},{9,1},{1... | collective-permute-start | bytes 196616 | tf_op jit(solution)/shard_map/ppermute | solution.py:264
  79.3 1.9 %collective-permute-start.36 = (f32[128,128]{1,0:T(8,128)S(1)}, f32[128,128]{1,0:T(8,128)S(1)}, u32[]{:S(2)}, u32[]{:S(2)}) collective-permute-start(f32[128,128]{1,0:T(8,128)S(1)} %add.214), channel_id=1, source_target_pairs={{0,8},{1,5},{2,10},{3,7},{4,12},{5,1},{6,14},{7,3},{8,0},{9,13},{1... | collective-permute-start | bytes 196616 | tf_op jit(solution)/shard_map/ppermute | solution.py:264
  82.5 1.6 %collective-permute-start.28 = (f32[256,128]{1,0:T(8,128)S(1)}, f32[256,128]{1,0:T(8,128)S(1)}, u32[]{:S(2)}, u32[]{:S(2)}) collective-permute-start(f32[256,128]{1,0:T(8,128)S(1)} %pad_maximum_fusion.4.v_ref), channel_id=1, source_target_pairs={{0,4},{1,9},{2,6},{3,11},{4,0},{5,13},{6,2},{7,15},{8,12},{9,1},{1... | collective-permute-start | bytes 393224 | tf_op jit(solution)/shard_map/ppermute | solution.py:264
  84.7 1.3 collective-permute-start.42
  92.9 1.5 %collective-permute-start.45 = (f32[16,128]{1,0:T(8,128)S(1)}, f32[16,128]{1,0:T(8,128)S(1)}, u32[]{:S(2)}, u32[]{:S(2)}) collective-permute-start(f32[16,128]{1,0:T(8,128)S(1)} %add.224), channel_id=1, source_target_pairs={{0,2},{1,3},{2,0},{3,1},{4,6},{5,7},{6,4},{7,5},{8,10},{9,11},{10,... | collective-permute-start | bytes 24584 | tf_op jit(solution)/shard_map/ppermute | solution.py:269
  94.4 2.1 %collective-permute-done.45 = f32[16,128]{1,0:T(8,128)S(1)} collective-permute-done((f32[16,128]{1,0:T(8,128)S(1)}, f32[16,128]{1,0:T(8,128)S(1)}, u32[]{:S(2)}, u32[]{:S(2)}) %collective-permute-start.45) | collective-permute-done | bytes 8224 | tf_op jit(solution)/shard_map/ppermute | solution.py:269
  98.8 1.6 %collective-permute-start.51 = (f32[256,128]{1,0:T(8,128)S(1)}, f32[256,128]{1,0:T(8,128)S(1)}, u32[]{:S(2)}, u32[]{:S(2)}) collective-permute-start(f32[256,128]{1,0:T(8,128)S(1)} %weigh.36), channel_id=1, source_target_pairs={{0,8},{1,5},{2,10},{3,7},{4,12},{5,1},{6,14},{7,3},{8,0},{9,13},{1... | collective-permute-start | bytes 393224 | tf_op jit(solution)/shard_map/ppermute | solution.py:264
  101.6 1.3 collective-permute-start.61
  106.7 1.4 %collective-permute-start.57 = (f32[128,128]{1,0:T(8,128)S(1)}, f32[128,128]{1,0:T(8,128)S(1)}, u32[]{:S(2)}, u32[]{:S(2)}) collective-permute-start(f32[128,128]{1,0:T(8,128)S(1)} %slice.157), channel_id=1, source_target_pairs={{0,8},{1,5},{2,10},{3,7},{4,12},{5,1},{6,14},{7,3},{8,0},{9,13},{1... | collective-permute-start | bytes 196616 | tf_op jit(solution)/shard_map/ppermute | solution.py:264
  109.1 2.6 %collective-permute-start.48 = (f32[128,128]{1,0:T(8,128)S(1)}, f32[128,128]{1,0:T(8,128)S(1)}, u32[]{:S(2)}, u32[]{:S(2)}) collective-permute-start(f32[128,128]{1,0:T(8,128)S(1)} %slice_add_fusion.3), channel_id=1, source_target_pairs={{0,16},{1,17},{2,18},{3,19},{4,20},{5,21},{6,22},{7,23},{8,24},{9,... | collective-permute-start | bytes 196616 | tf_op jit(solution)/shard_map/ppermute | solution.py:264
  112.7 2.1 %collective-permute-start.58 = (f32[128,128]{1,0:T(8,128)S(1)}, f32[128,128]{1,0:T(8,128)S(1)}, u32[]{:S(2)}, u32[]{:S(2)}) collective-permute-start(f32[128,128]{1,0:T(8,128)S(1)} %slice_add_fusion.1), channel_id=1, source_target_pairs={{0,16},{1,17},{2,18},{3,19},{4,20},{5,21},{6,22},{7,23},{8,24},{9,... | collective-permute-start | bytes 196616 | tf_op jit(solution)/shard_map/ppermute | solution.py:264
  115.8 3.5 %collective-permute-done.48 = f32[128,128]{1,0:T(8,128)S(1)} collective-permute-done((f32[128,128]{1,0:T(8,128)S(1)}, f32[128,128]{1,0:T(8,128)S(1)}, u32[]{:S(2)}, u32[]{:S(2)}) %collective-permute-start.48) | collective-permute-done | bytes 65568 | tf_op jit(solution)/shard_map/ppermute | solution.py:264
  119.9 1.4 %collective-permute-done.53 = f32[128,128]{1,0:T(8,128)S(1)} collective-permute-done((f32[128,128]{1,0:T(8,128)S(1)}, f32[128,128]{1,0:T(8,128)S(1)}, u32[]{:S(2)}, u32[]{:S(2)}) %collective-permute-start.53) | collective-permute-done | bytes 65568 | tf_op jit(solution)/shard_map/ppermute | solution.py:264
  122.8 1.4 %collective-permute-start.64 = (f32[128,128]{1,0:T(8,128)S(1)}, f32[128,128]{1,0:T(8,128)S(1)}, u32[]{:S(2)}, u32[]{:S(2)}) collective-permute-start(f32[128,128]{1,0:T(8,128)S(1)} %add.237), channel_id=1, source_target_pairs={{0,4},{1,9},{2,6},{3,11},{4,0},{5,13},{6,2},{7,15},{8,12},{9,1},{1... | collective-permute-start | bytes 196616 | tf_op jit(solution)/shard_map/ppermute | solution.py:264
  129.2 1.4 %collective-permute-done.50 = f32[256,128]{1,0:T(8,128)S(1)} collective-permute-done((f32[256,128]{1,0:T(8,128)S(1)}, f32[256,128]{1,0:T(8,128)S(1)}, u32[]{:S(2)}, u32[]{:S(2)}) %collective-permute-start.50) | collective-permute-done | bytes 131104 | tf_op jit(solution)/shard_map/ppermute | solution.py:264
  130.8 1.5 %collective-permute-done.60 = f32[256,128]{1,0:T(8,128)S(1)} collective-permute-done((f32[256,128]{1,0:T(8,128)S(1)}, f32[256,128]{1,0:T(8,128)S(1)}, u32[]{:S(2)}, u32[]{:S(2)}) %collective-permute-start.60) | collective-permute-done | bytes 131104 | tf_op jit(solution)/shard_map/ppermute | solution.py:264
  (227 shorter events, 67.5 us)
Async XLA Ops:
  12.7 6.5 %collective-permute-start.7 = (f32[256,128]{1,0:T(8,128)S(1)}, f32[256,128]{1,0:T(8,128)S(1)}, u32[]{:S(2)}, u32[]{:S(2)}) collective-permute-start(f32[256,128]{1,0:T(8,128)S(1)} %weigh.22), channel_id=1, source_target_pairs={{0,8},{1,5},{2,10},{3,7},{4,12},{5,1},{6,14},{7,3},{8,0},{9,13},{1... | collective-permute-start | bytes 393224 | tf_op jit(solution)/shard_map/ppermute | solution.py:264
  14.9 7.4 %collective-permute-start.2 = (f32[256,128]{1,0:T(8,128)S(1)}, f32[256,128]{1,0:T(8,128)S(1)}, u32[]{:S(2)}, u32[]{:S(2)}) collective-permute-start(f32[256,128]{1,0:T(8,128)S(1)} %get-tuple-element.18), channel_id=1, source_target_pairs={{0,4},{1,9},{2,6},{3,11},{4,0},{5,13},{6,2},{7,15},{8,12},{9,1},{1... | collective-permute-start | bytes 393224 | tf_op jit(solution)/shard_map/ppermute | solution.py:264
  16.7 7.2 %collective-permute-start.11 = (f32[256,128]{1,0:T(8,128)S(1)}, f32[256,128]{1,0:T(8,128)S(1)}, u32[]{:S(2)}, u32[]{:S(2)}) collective-permute-start(f32[256,128]{1,0:T(8,128)S(1)} %weigh.24), channel_id=1, source_target_pairs={{0,4},{1,9},{2,6},{3,11},{4,0},{5,13},{6,2},{7,15},{8,12},{9,1},{1... | collective-permute-start | bytes 393224 | tf_op jit(solution)/shard_map/ppermute | solution.py:264
  17.6 6.9 %collective-permute-start.15 = (f32[256,128]{1,0:T(8,128)S(1)}, f32[256,128]{1,0:T(8,128)S(1)}, u32[]{:S(2)}, u32[]{:S(2)}) collective-permute-start(f32[256,128]{1,0:T(8,128)S(1)} %weigh.26), channel_id=1, source_target_pairs={{0,8},{1,5},{2,10},{3,7},{4,12},{5,1},{6,14},{7,3},{8,0},{9,13},{1... | collective-permute-start | bytes 393224 | tf_op jit(solution)/shard_map/ppermute | solution.py:264
  19.3 6.3 %collective-permute-start.8 = (f32[128,128]{1,0:T(8,128)S(1)}, f32[128,128]{1,0:T(8,128)S(1)}, u32[]{:S(2)}, u32[]{:S(2)}) collective-permute-start(f32[128,128]{1,0:T(8,128)S(1)} %slice.135), channel_id=1, source_target_pairs={{0,4},{1,9},{2,6},{3,11},{4,0},{5,13},{6,2},{7,15},{8,12},{9,1},{1... | collective-permute-start | bytes 196616 | tf_op jit(solution)/shard_map/ppermute | solution.py:264
  24.5 7.1 %collective-permute-start.16 = (f32[128,128]{1,0:T(8,128)S(1)}, f32[128,128]{1,0:T(8,128)S(1)}, u32[]{:S(2)}, u32[]{:S(2)}) collective-permute-start(f32[128,128]{1,0:T(8,128)S(1)} %slice.139), channel_id=1, source_target_pairs={{0,4},{1,9},{2,6},{3,11},{4,0},{5,13},{6,2},{7,15},{8,12},{9,1},{1... | collective-permute-start | bytes 196616 | tf_op jit(solution)/shard_map/ppermute | solution.py:264
  25.6 10.9 %collective-permute-start.9 = (f32[128,128]{1,0:T(8,128)S(1)}, f32[128,128]{1,0:T(8,128)S(1)}, u32[]{:S(2)}, u32[]{:S(2)}) collective-permute-start(f32[128,128]{1,0:T(8,128)S(1)} %slice_add_fusion.10), channel_id=1, source_target_pairs={{0,16},{1,17},{2,18},{3,19},{4,20},{5,21},{6,22},{7,23},{8,24},{9,... | collective-permute-start | bytes 196616 | tf_op jit(solution)/shard_map/ppermute | solution.py:264
  28.2 7.4 %collective-permute-start.4 = (f32[128,128]{1,0:T(8,128)S(1)}, f32[128,128]{1,0:T(8,128)S(1)}, u32[]{:S(2)}, u32[]{:S(2)}) collective-permute-start(f32[128,128]{1,0:T(8,128)S(1)} %slice_add_fusion.11), channel_id=1, source_target_pairs={{0,16},{1,17},{2,18},{3,19},{4,20},{5,21},{6,22},{7,23},{8,24},{9,... | collective-permute-start | bytes 196616 | tf_op jit(solution)/shard_map/ppermute | solution.py:264
  29.3 8.3 %collective-permute-start.13 = (f32[128,128]{1,0:T(8,128)S(1)}, f32[128,128]{1,0:T(8,128)S(1)}, u32[]{:S(2)}, u32[]{:S(2)}) collective-permute-start(f32[128,128]{1,0:T(8,128)S(1)} %slice_add_fusion.9), channel_id=1, source_target_pairs={{0,16},{1,17},{2,18},{3,19},{4,20},{5,21},{6,22},{7,23},{8,24},{9,... | collective-permute-start | bytes 196616 | tf_op jit(solution)/shard_map/ppermute | solution.py:264
  31.7 7.1 %collective-permute-start.17 = (f32[128,128]{1,0:T(8,128)S(1)}, f32[128,128]{1,0:T(8,128)S(1)}, u32[]{:S(2)}, u32[]{:S(2)}) collective-permute-start(f32[128,128]{1,0:T(8,128)S(1)} %slice_add_fusion.8), channel_id=1, source_target_pairs={{0,16},{1,17},{2,18},{3,19},{4,20},{5,21},{6,22},{7,23},{8,24},{9,... | collective-permute-start | bytes 196616 | tf_op jit(solution)/shard_map/ppermute | solution.py:264
  55.6 6.4 %collective-permute-start.29 = (f32[256,128]{1,0:T(8,128)S(1)}, f32[256,128]{1,0:T(8,128)S(1)}, u32[]{:S(2)}, u32[]{:S(2)}) collective-permute-start(f32[256,128]{1,0:T(8,128)S(1)} %weigh.29), channel_id=1, source_target_pairs={{0,8},{1,5},{2,10},{3,7},{4,12},{5,1},{6,14},{7,3},{8,0},{9,13},{1... | collective-permute-start | bytes 393224 | tf_op jit(solution)/shard_map/ppermute | solution.py:264
  56.7 7.4 %collective-permute-start.24 = (f32[256,128]{1,0:T(8,128)S(1)}, f32[256,128]{1,0:T(8,128)S(1)}, u32[]{:S(2)}, u32[]{:S(2)}) collective-permute-start(f32[256,128]{1,0:T(8,128)S(1)} %get-tuple-element.22), channel_id=1, source_target_pairs={{0,4},{1,9},{2,6},{3,11},{4,0},{5,13},{6,2},{7,15},{8,12},{9,1},{1... | collective-permute-start | bytes 393224 | tf_op jit(solution)/shard_map/ppermute | solution.py:264
  57.9 7.3 %collective-permute-start.33 = (f32[256,128]{1,0:T(8,128)S(1)}, f32[256,128]{1,0:T(8,128)S(1)}, u32[]{:S(2)}, u32[]{:S(2)}) collective-permute-start(f32[256,128]{1,0:T(8,128)S(1)} %weigh.31), channel_id=1, source_target_pairs={{0,4},{1,9},{2,6},{3,11},{4,0},{5,13},{6,2},{7,15},{8,12},{9,1},{1... | collective-permute-start | bytes 393224 | tf_op jit(solution)/shard_map/ppermute | solution.py:264
  59.4 6.9 %collective-permute-start.37 = (f32[256,128]{1,0:T(8,128)S(1)}, f32[256,128]{1,0:T(8,128)S(1)}, u32[]{:S(2)}, u32[]{:S(2)}) collective-permute-start(f32[256,128]{1,0:T(8,128)S(1)} %weigh.33), channel_id=1, source_target_pairs={{0,8},{1,5},{2,10},{3,7},{4,12},{5,1},{6,14},{7,3},{8,0},{9,13},{1... | collective-permute-start | bytes 393224 | tf_op jit(solution)/shard_map/ppermute | solution.py:264
  64.1 6.5 %collective-permute-start.25 = (f32[128,128]{1,0:T(8,128)S(1)}, f32[128,128]{1,0:T(8,128)S(1)}, u32[]{:S(2)}, u32[]{:S(2)}) collective-permute-start(f32[128,128]{1,0:T(8,128)S(1)} %slice.141), channel_id=1, source_target_pairs={{0,8},{1,5},{2,10},{3,7},{4,12},{5,1},{6,14},{7,3},{8,0},{9,13},{1... | collective-permute-start | bytes 196616 | tf_op jit(solution)/shard_map/ppermute | solution.py:264
  65.2 6.2 %collective-permute-start.34 = (f32[128,128]{1,0:T(8,128)S(1)}, f32[128,128]{1,0:T(8,128)S(1)}, u32[]{:S(2)}, u32[]{:S(2)}) collective-permute-start(f32[128,128]{1,0:T(8,128)S(1)} %slice.145), channel_id=1, source_target_pairs={{0,8},{1,5},{2,10},{3,7},{4,12},{5,1},{6,14},{7,3},{8,0},{9,13},{1... | collective-permute-start | bytes 196616 | tf_op jit(solution)/shard_map/ppermute | solution.py:264
  66.3 7.4 %collective-permute-start.38 = (f32[128,128]{1,0:T(8,128)S(1)}, f32[128,128]{1,0:T(8,128)S(1)}, u32[]{:S(2)}, u32[]{:S(2)}) collective-permute-start(f32[128,128]{1,0:T(8,128)S(1)} %slice.147), channel_id=1, source_target_pairs={{0,4},{1,9},{2,6},{3,11},{4,0},{5,13},{6,2},{7,15},{8,12},{9,1},{1... | collective-permute-start | bytes 196616 | tf_op jit(solution)/shard_map/ppermute | solution.py:264
  67.5 10.1 %collective-permute-start.31 = (f32[128,128]{1,0:T(8,128)S(1)}, f32[128,128]{1,0:T(8,128)S(1)}, u32[]{:S(2)}, u32[]{:S(2)}) collective-permute-start(f32[128,128]{1,0:T(8,128)S(1)} %slice_add_fusion.6), channel_id=1, source_target_pairs={{0,16},{1,17},{2,18},{3,19},{4,20},{5,21},{6,22},{7,23},{8,24},{9,... | collective-permute-start | bytes 196616 | tf_op jit(solution)/shard_map/ppermute | solution.py:264
  70.7 6.8 %collective-permute-start.26 = (f32[128,128]{1,0:T(8,128)S(1)}, f32[128,128]{1,0:T(8,128)S(1)}, u32[]{:S(2)}, u32[]{:S(2)}) collective-permute-start(f32[128,128]{1,0:T(8,128)S(1)} %slice_add_fusion.7), channel_id=1, source_target_pairs={{0,16},{1,17},{2,18},{3,19},{4,20},{5,21},{6,22},{7,23},{8,24},{9,... | collective-permute-start | bytes 196616 | tf_op jit(solution)/shard_map/ppermute | solution.py:264
  71.5 7.9 %collective-permute-start.35 = (f32[128,128]{1,0:T(8,128)S(1)}, f32[128,128]{1,0:T(8,128)S(1)}, u32[]{:S(2)}, u32[]{:S(2)}) collective-permute-start(f32[128,128]{1,0:T(8,128)S(1)} %slice_add_fusion.5), channel_id=1, source_target_pairs={{0,16},{1,17},{2,18},{3,19},{4,20},{5,21},{6,22},{7,23},{8,24},{9,... | collective-permute-start | bytes 196616 | tf_op jit(solution)/shard_map/ppermute | solution.py:264
  73.8 7.5 %collective-permute-start.39 = (f32[128,128]{1,0:T(8,128)S(1)}, f32[128,128]{1,0:T(8,128)S(1)}, u32[]{:S(2)}, u32[]{:S(2)}) collective-permute-start(f32[128,128]{1,0:T(8,128)S(1)} %slice_add_fusion.4), channel_id=1, source_target_pairs={{0,16},{1,17},{2,18},{3,19},{4,20},{5,21},{6,22},{7,23},{8,24},{9,... | collective-permute-start | bytes 196616 | tf_op jit(solution)/shard_map/ppermute | solution.py:264
  77.6 6.5 %collective-permute-start.32 = (f32[128,128]{1,0:T(8,128)S(1)}, f32[128,128]{1,0:T(8,128)S(1)}, u32[]{:S(2)}, u32[]{:S(2)}) collective-permute-start(f32[128,128]{1,0:T(8,128)S(1)} %add.210), channel_id=1, source_target_pairs={{0,4},{1,9},{2,6},{3,11},{4,0},{5,13},{6,2},{7,15},{8,12},{9,1},{1... | collective-permute-start | bytes 196616 | tf_op jit(solution)/shard_map/ppermute | solution.py:264
  97.6 6.0 %collective-permute-start.46 = (f32[256,128]{1,0:T(8,128)S(1)}, f32[256,128]{1,0:T(8,128)S(1)}, u32[]{:S(2)}, u32[]{:S(2)}) collective-permute-start(f32[256,128]{1,0:T(8,128)S(1)} %get-tuple-element.25), channel_id=1, source_target_pairs={{0,4},{1,9},{2,6},{3,11},{4,0},{5,13},{6,2},{7,15},{8,12},{9,1},{1... | collective-permute-start | bytes 393224 | tf_op jit(solution)/shard_map/ppermute | solution.py:264
  98.8 6.8 %collective-permute-start.51 = (f32[256,128]{1,0:T(8,128)S(1)}, f32[256,128]{1,0:T(8,128)S(1)}, u32[]{:S(2)}, u32[]{:S(2)}) collective-permute-start(f32[256,128]{1,0:T(8,128)S(1)} %weigh.36), channel_id=1, source_target_pairs={{0,8},{1,5},{2,10},{3,7},{4,12},{5,1},{6,14},{7,3},{8,0},{9,13},{1... | collective-permute-start | bytes 393224 | tf_op jit(solution)/shard_map/ppermute | solution.py:264
  101.6 6.5 %collective-permute-start.61 = (f32[256,128]{1,0:T(8,128)S(1)}, f32[256,128]{1,0:T(8,128)S(1)}, u32[]{:S(2)}, u32[]{:S(2)}) collective-permute-start(f32[256,128]{1,0:T(8,128)S(1)} %weigh.40), channel_id=1, source_target_pairs={{0,8},{1,5},{2,10},{3,7},{4,12},{5,1},{6,14},{7,3},{8,0},{9,13},{1... | collective-permute-start | bytes 393224 | tf_op jit(solution)/shard_map/ppermute | solution.py:264
  105.6 6.0 %collective-permute-start.52 = (f32[128,128]{1,0:T(8,128)S(1)}, f32[128,128]{1,0:T(8,128)S(1)}, u32[]{:S(2)}, u32[]{:S(2)}) collective-permute-start(f32[128,128]{1,0:T(8,128)S(1)} %slice.153), channel_id=1, source_target_pairs={{0,4},{1,9},{2,6},{3,11},{4,0},{5,13},{6,2},{7,15},{8,12},{9,1},{1... | collective-permute-start | bytes 196616 | tf_op jit(solution)/shard_map/ppermute | solution.py:264
  108.2 6.6 %collective-permute-start.62 = (f32[128,128]{1,0:T(8,128)S(1)}, f32[128,128]{1,0:T(8,128)S(1)}, u32[]{:S(2)}, u32[]{:S(2)}) collective-permute-start(f32[128,128]{1,0:T(8,128)S(1)} %slice.161), channel_id=1, source_target_pairs={{0,4},{1,9},{2,6},{3,11},{4,0},{5,13},{6,2},{7,15},{8,12},{9,1},{1... | collective-permute-start | bytes 196616 | tf_op jit(solution)/shard_map/ppermute | solution.py:264
  109.1 10.2 %collective-permute-start.48 = (f32[128,128]{1,0:T(8,128)S(1)}, f32[128,128]{1,0:T(8,128)S(1)}, u32[]{:S(2)}, u32[]{:S(2)}) collective-permute-start(f32[128,128]{1,0:T(8,128)S(1)} %slice_add_fusion.3), channel_id=1, source_target_pairs={{0,16},{1,17},{2,18},{3,19},{4,20},{5,21},{6,22},{7,23},{8,24},{9,... | collective-permute-start | bytes 196616 | tf_op jit(solution)/shard_map/ppermute | solution.py:264
  111.7 9.6 %collective-permute-start.53 = (f32[128,128]{1,0:T(8,128)S(1)}, f32[128,128]{1,0:T(8,128)S(1)}, u32[]{:S(2)}, u32[]{:S(2)}) collective-permute-start(f32[128,128]{1,0:T(8,128)S(1)} %slice_add_fusion.2), channel_id=1, source_target_pairs={{0,16},{1,17},{2,18},{3,19},{4,20},{5,21},{6,22},{7,23},{8,24},{9,... | collective-permute-start | bytes 196616 | tf_op jit(solution)/shard_map/ppermute | solution.py:264
  112.7 9.5 %collective-permute-start.58 = (f32[128,128]{1,0:T(8,128)S(1)}, f32[128,128]{1,0:T(8,128)S(1)}, u32[]{:S(2)}, u32[]{:S(2)}) collective-permute-start(f32[128,128]{1,0:T(8,128)S(1)} %slice_add_fusion.1), channel_id=1, source_target_pairs={{0,16},{1,17},{2,18},{3,19},{4,20},{5,21},{6,22},{7,23},{8,24},{9,... | collective-permute-start | bytes 196616 | tf_op jit(solution)/shard_map/ppermute | solution.py:264
  114.8 8.0 %collective-permute-start.63 = (f32[128,128]{1,0:T(8,128)S(1)}, f32[128,128]{1,0:T(8,128)S(1)}, u32[]{:S(2)}, u32[]{:S(2)}) collective-permute-start(f32[128,128]{1,0:T(8,128)S(1)} %slice_add_fusion), channel_id=1, source_target_pairs={{0,16},{1,17},{2,18},{3,19},{4,20},{5,21},{6,22},{7,23},{8,24},{9,... | collective-permute-start | bytes 196616 | tf_op jit(solution)/shard_map/ppermute | solution.py:264
  124.2 6.5 %collective-permute-start.50 = (f32[256,128]{1,0:T(8,128)S(1)}, f32[256,128]{1,0:T(8,128)S(1)}, u32[]{:S(2)}, u32[]{:S(2)}) collective-permute-start(f32[256,128]{1,0:T(8,128)S(1)} %get-tuple-element.32), channel_id=1, source_target_pairs={{0,4},{1,9},{2,6},{3,11},{4,0},{5,13},{6,2},{7,15},{8,12},{9,1},{1... | collective-permute-start | bytes 393224 | tf_op jit(solution)/shard_map/ppermute | solution.py:264
  (36 other events, 174.0 us)

commit v4 on v3

--- a/solution.py
+++ b/solution.py
@@ -7,6 +7,7 @@
 from jax.experimental.pallas import tpu as pltpu
 from jax.sharding import PartitionSpec as P
 
+
 LANES = 128
 GROUP = 8
 BLOCK = 32
@@ -19,10 +20,6 @@
     count = size.bit_length() - 1
     assert 1 << count == size
     return count
-
-
-def swap(size, bit):
-    return [(i, i ^ (1 << bit)) for i in range(size)]
 
 
 def square_rows(x_ref, x_row, v_ref, v_row, rows, carry):
@@ -58,7 +55,7 @@
         o_ref[g * GROUP:(g + 1) * GROUP, :] = total
 
 
-def load_body(chunks, parts, x_hbm, v_hbm, out_ref, x_ref, v_ref, o_ref, extra_ref, sems):
+def load_body(chunks, parts, x_hbm, v_hbm, out_hbm, x_ref, v_ref, o_ref, extra_ref, out_ref, sems, sem):
     groups, total, _ = x_ref.shape
     rows = total // chunks
     per = rows // GROUP
@@ -72,19 +69,22 @@
             pltpu.make_async_copy(v_hbm.at[part, :], v_ref.at[part, :], sems.at[1, c]),
         )
 
+    small = pltpu.make_async_copy(out_hbm, out_ref, sem)
+    small.start()
     for c in range(chunks):
         for copy in copies(c):
             copy.start()
+    acc = zero_carry(groups)
+    for c in range(chunks):
+        for copy in copies(c):
+            copy.wait()
+        acc = square_rows(x_ref, c * per, v_ref, c * per, per, acc)
+    small.wait()
     corner = lax.broadcasted_iota(jnp.int32, (own, own), 0) == lax.broadcasted_iota(jnp.int32, (own, own), 1)
     lane = lax.broadcasted_iota(jnp.int32, (own, LANES), 1)
     for t in range(extra_ref.shape[0]):
         column = jnp.sum(jnp.where(corner, out_ref[t:t + 1, :], 0.0), axis=1, keepdims=True)
         extra_ref[t] = jnp.where(lane == 0, column / jnp.float32(parts), 0.0)
-    acc = zero_carry(groups)
-    for c in range(chunks):
-        for copy in copies(c):
-            copy.wait()
-        acc = square_rows(x_ref, c * per, v_ref, c * per, per, acc)
     store_carry(o_ref, acc, extra_ref, 0)
 
 
@@ -220,12 +220,14 @@
             partial_shape,
             jax.ShapeDtypeStruct((iters, workers, LANES), jnp.float32),
         ),
-        in_specs=[pl.BlockSpec(memory_space=pltpu.HBM), pl.BlockSpec(memory_space=pltpu.HBM), VM],
+        in_specs=[pl.BlockSpec(memory_space=pltpu.HBM)] * 3,
         out_specs=(VM, VM, VM, VM),
-        scratch_shapes=[pltpu.SemaphoreType.DMA((2, chunks))],
+        scratch_shapes=[
+            pltpu.VMEM((iters, workers), jnp.float32), pltpu.SemaphoreType.DMA((2, chunks)), pltpu.SemaphoreType.DMA,
+        ],
         compiler_params=PARAMS,
         name="load",
-    )(pltpu.with_memory_space_constraint(x, pltpu.HBM), pltpu.with_memory_space_constraint(center, pltpu.HBM), outside_sq)
+    )(*[pltpu.with_memory_space_constraint(a, pltpu.HBM) for a in (x, center, outside_sq)])
 
     def squares(s, first, value, step):
         more = [] if step is None else [extra]
@@ -255,6 +257,11 @@
             out_shape=half_shape(s), in_specs=[VM, VM, VM, VM], out_specs=VM, compiler_params=PARAMS, name="weigh",
         )(x, value, weights, keep)
 
+    def over_parts(one):
+        for mask in [(1 << b) | 1 for b in reversed(range(1, bits_of(parts)))] + [1]:
+            one = one + lax.ppermute(one, "mp", [(i, i ^ mask) for i in range(parts)])
+        return one
+
     def exchange(value, s, k):
         pairs = []
         for w in range(devices):
@@ -265,11 +272,10 @@
 
     value = None
     for t in range(iters):
-        for b in range(bits_of(parts)):
-            partial = partial + lax.ppermute(partial, "mp", swap(parts, b))
-        squared = partial
+        squared = over_parts(partial)
         hold = []
         relative = t > 0
+
         for s in range(streams):
             source = value[s][1] if relative else center
             if s == 0:
@@ -279,18 +285,24 @@
             hold.append(exchange(sent, s, 0))
         for s in range(streams):
             source = value[s][0] if relative else center
-            hold[s] = hold[s] + weigh(s, 0, source, relative, weights, keep)
+            own = weigh(s, 0, source, relative, weights, keep)
+            hold[s] = hold[s] + own
         for k in range(1, split):
             for s in range(streams):
                 half = hold[s].shape[0] // 2
-                hold[s] = hold[s][:half] + exchange(hold[s][half:], s, k)
+                other = exchange(hold[s][half:], s, k)
+                hold[s] = hold[s][:half] + other
         for k in range(split, levels):
             for s in range(streams):
-                hold[s] = hold[s] + exchange(hold[s], s, k)
+                other = exchange(hold[s], s, k)
+                hold[s] = hold[s] + other
         for k in reversed(range(1, split)):
             for s in range(streams):
-                hold[s] = jnp.concatenate([hold[s], exchange(hold[s], s, k)], axis=0)
-        value = [[hold[s], exchange(hold[s], s, 0)] for s in range(streams)]
+                other = exchange(hold[s], s, k)
+                hold[s] = jnp.concatenate([hold[s], other], axis=0)
+        value = []
+        for s in range(streams):
+            value.append([hold[s], exchange(hold[s], s, 0)])
         if t + 1 < iters:
             partial = None
             for first in range(2):
@@ -315,6 +327,5 @@
 
 def solution(mesh):
     placed = (P("worker", "mp"), P("mp"), P(None, "worker"), P())
-    return jax.shard_map(
-        shards, mesh=mesh, in_specs=placed, out_specs=(P("mp"), P("worker")), check_vma=False
-    )
+
+    return jax.shard_map(shards, mesh=mesh, in_specs=placed, out_specs=(P("mp"), P("worker")), check_vma=False)

time: 135 us -> 136 us (level)
  waiting for transfers between devices: 33.3 us -> 36.6 us
  starting transfers between devices: 77 us -> 75.2 us
    ppermute x6, starting transfers between devices: 6.54 us -> 3.38 us  [over_parts(): one = one + lax.ppermute(one, 'mp', [(i, i ^ mask) for i in range(parts)])]
    ppermute x60, waiting for transfers between devices: 24.2 us -> 26.1 us  [exchange(): return lax.ppermute(value, ('worker', 'mp'), pairs)]
    ppermute x6, waiting for transfers between devices: 9.05 us -> 10.5 us  [over_parts(): one = one + lax.ppermute(one, 'mp', [(i, i ^ mask) for i in range(parts)])]
    ppermute x60, starting transfers between devices: 70.4 us -> 71.8 us  [exchange(): return lax.ppermute(value, ('worker', 'mp'), pairs)]
  transfers between devices with their start and end apart: 66 -> 66, of which waited for: 28 -> 27; matrix products, arithmetic and copies ran while one was open for 1% -> 1% of each run, Pallas kernels for 8% -> 8%
where the time goes in v4:
time: 136 us
  starting transfers between devices  75.2 us (55%)
  waiting for transfers between devices  36.6 us (27%)
  Pallas kernels  19.9 us (15%)
  other arithmetic  1.93 us (1%)
  between operations  1.44 us (1%)
    ppermute x60, starting transfers between devices, exchange(): return lax.ppermute(value, ('worker', 'mp'), pairs)  71.8 us
    ppermute x60, waiting for transfers between devices, exchange(): return lax.ppermute(value, ('worker', 'mp'), pairs)  26.1 us
    ppermute x6, waiting for transfers between devices, over_parts(): one = one + lax.ppermute(one, 'mp', [(i, i ^ mask) for i in range(parts)])  10.5 us
    pallas_call x21, Pallas kernels, weigh(): pl.pallas_call(functools.partial(weigh_body, functools.partial(offsets, s...  6.41 us
    pallas_call x16, Pallas kernels, squares(): pl.pallas_call(functools.partial(square_body, functools.partial(offsets,...  6.18 us
    pallas_call x1, Pallas kernels, shards(): pl.pallas_call(functools.partial(load_body, chunks, parts), out_shape=(ja...  4.29 us
    ppermute x6, starting transfers between devices, over_parts(): one = one + lax.ppermute(one, 'mp', [(i, i ^ mask) for i in range(parts)])  3.38 us
    pallas_call x3, Pallas kernels, weigh_first(): pl.pallas_call(body, out_shape=(half_shape(s), weight_shape, keep_shape),...  3.02 us
  transfers between devices with their start and end apart: 66, of which 27 were waited for; matrix products, arithmetic and copies ran while one was open for 1% of the time, Pallas kernels for 8%

profile of v4, /device:TPU:0, one launch (start us, length us, event | category | flops | bytes accessed | tf_op | source)
XLA Modules:
  0.0 135.7 jit_solution(18445697413767214101)
XLA Ops:
  0.6 4.3 %load.1 = (bf16[2,16384,128]{2,1,0:T(8,128)(2,1)S(1)}, f32[2048,128]{1,0:T(8,128)S(1)}, f32[16,128]{1,0:T(8,128)S(1)}, f32[3,16,128]{2,1,0:T(8,128)S(1)}) custom-call(bf16[2,16384,128]{2,1,0:T(8,128)(2,1)} %bitcast.8, f32[2048,128]{1,0:T(8,128)} %bitcast.9, f32[3,16]{1,0:T(4,128)} %out_hbm.1), custom_call_target="tpu_custom_call" | custom-call | tf_op jit(solution)/shard_map/load/pallas_call | solution.py:215
  4.9 2.5 %collective-permute-start = (f32[16,128]{1,0:T(8,128)S(1)}, f32[16,128]{1,0:T(8,128)S(1)}, u32[]{:S(2)}, u32[]{:S(2)}) collective-permute-start(f32[16,128]{1,0:T(8,128)S(1)} %get-tuple-element.17), channel_id=1, source_target_pairs={{0,3},{1,2},{2,1},{3,0},{4,7},{5,6},{6,5},{7,4},{8,11},{9,10},{10,... | collective-permute-start | bytes 24584 | tf_op jit(solution)/shard_map/ppermute | solution.py:262
  11.6 2.2 %collective-permute-start.7 = (f32[256,128]{1,0:T(8,128)S(1)}, f32[256,128]{1,0:T(8,128)S(1)}, u32[]{:S(2)}, u32[]{:S(2)}) collective-permute-start(f32[256,128]{1,0:T(8,128)S(1)} %weigh.22), channel_id=1, source_target_pairs={{0,8},{1,5},{2,10},{3,7},{4,12},{5,1},{6,14},{7,3},{8,0},{9,13},{1... | collective-permute-start | bytes 393224 | tf_op jit(solution)/shard_map/ppermute | solution.py:271
  13.8 1.5 %collective-permute-start.2 = (f32[256,128]{1,0:T(8,128)S(1)}, f32[256,128]{1,0:T(8,128)S(1)}, u32[]{:S(2)}, u32[]{:S(2)}) collective-permute-start(f32[256,128]{1,0:T(8,128)S(1)} %get-tuple-element.18), channel_id=1, source_target_pairs={{0,4},{1,9},{2,6},{3,11},{4,0},{5,13},{6,2},{7,15},{8,12},{9,1},{1... | collective-permute-start | bytes 393224 | tf_op jit(solution)/shard_map/ppermute | solution.py:271
  17.3 2.9 %collective-permute-start.8 = (f32[128,128]{1,0:T(8,128)S(1)}, f32[128,128]{1,0:T(8,128)S(1)}, u32[]{:S(2)}, u32[]{:S(2)}) collective-permute-start(f32[128,128]{1,0:T(8,128)S(1)} %slice.135), channel_id=1, source_target_pairs={{0,4},{1,9},{2,6},{3,11},{4,0},{5,13},{6,2},{7,15},{8,12},{9,1},{1... | collective-permute-start | bytes 196616 | tf_op jit(solution)/shard_map/ppermute | solution.py:271
  21.2 1.6 %collective-permute-start.3 = (f32[128,128]{1,0:T(8,128)S(1)}, f32[128,128]{1,0:T(8,128)S(1)}, u32[]{:S(2)}, u32[]{:S(2)}) collective-permute-start(f32[128,128]{1,0:T(8,128)S(1)} %slice.133), channel_id=1, source_target_pairs={{0,8},{1,5},{2,10},{3,7},{4,12},{5,1},{6,14},{7,3},{8,0},{9,13},{1... | collective-permute-start | bytes 196616 | tf_op jit(solution)/shard_map/ppermute | solution.py:271
  24.0 2.7 %collective-permute-start.9 = (f32[128,128]{1,0:T(8,128)S(1)}, f32[128,128]{1,0:T(8,128)S(1)}, u32[]{:S(2)}, u32[]{:S(2)}) collective-permute-start(f32[128,128]{1,0:T(8,128)S(1)} %slice_add_fusion.10), channel_id=1, source_target_pairs={{0,16},{1,17},{2,18},{3,19},{4,20},{5,21},{6,22},{7,23},{8,24},{9,... | collective-permute-start | bytes 196616 | tf_op jit(solution)/shard_map/ppermute | solution.py:271
  26.7 2.1 %collective-permute-start.4 = (f32[128,128]{1,0:T(8,128)S(1)}, f32[128,128]{1,0:T(8,128)S(1)}, u32[]{:S(2)}, u32[]{:S(2)}) collective-permute-start(f32[128,128]{1,0:T(8,128)S(1)} %slice_add_fusion.11), channel_id=1, source_target_pairs={{0,16},{1,17},{2,18},{3,19},{4,20},{5,21},{6,22},{7,23},{8,24},{9,... | collective-permute-start | bytes 196616 | tf_op jit(solution)/shard_map/ppermute | solution.py:271
  29.9 2.0 %collective-permute-start.17 = (f32[128,128]{1,0:T(8,128)S(1)}, f32[128,128]{1,0:T(8,128)S(1)}, u32[]{:S(2)}, u32[]{:S(2)}) collective-permute-start(f32[128,128]{1,0:T(8,128)S(1)} %slice_add_fusion.8), channel_id=1, source_target_pairs={{0,16},{1,17},{2,18},{3,19},{4,20},{5,21},{6,22},{7,23},{8,24},{9,... | collective-permute-start | bytes 196616 | tf_op jit(solution)/shard_map/ppermute | solution.py:271
  31.9 4.3 %collective-permute-done.4 = f32[128,128]{1,0:T(8,128)S(1)} collective-permute-done((f32[128,128]{1,0:T(8,128)S(1)}, f32[128,128]{1,0:T(8,128)S(1)}, u32[]{:S(2)}, u32[]{:S(2)}) %collective-permute-start.4) | collective-permute-done | bytes 65568 | tf_op jit(solution)/shard_map/ppermute | solution.py:271
  36.3 1.5 %collective-permute-start.10 = (f32[128,128]{1,0:T(8,128)S(1)}, f32[128,128]{1,0:T(8,128)S(1)}, u32[]{:S(2)}, u32[]{:S(2)}) collective-permute-start(f32[128,128]{1,0:T(8,128)S(1)} %add.189), channel_id=1, source_target_pairs={{0,4},{1,9},{2,6},{3,11},{4,0},{5,13},{6,2},{7,15},{8,12},{9,1},{1... | collective-permute-start | bytes 196616 | tf_op jit(solution)/shard_map/ppermute | solution.py:271
  37.9 2.1 %collective-permute-start.14 = (f32[128,128]{1,0:T(8,128)S(1)}, f32[128,128]{1,0:T(8,128)S(1)}, u32[]{:S(2)}, u32[]{:S(2)}) collective-permute-start(f32[128,128]{1,0:T(8,128)S(1)} %add.193), channel_id=1, source_target_pairs={{0,8},{1,5},{2,10},{3,7},{4,12},{5,1},{6,14},{7,3},{8,0},{9,13},{1... | collective-permute-start | bytes 196616 | tf_op jit(solution)/shard_map/ppermute | solution.py:271
  40.6 1.5 %collective-permute-start.6 = (f32[256,128]{1,0:T(8,128)S(1)}, f32[256,128]{1,0:T(8,128)S(1)}, u32[]{:S(2)}, u32[]{:S(2)}) collective-permute-start(f32[256,128]{1,0:T(8,128)S(1)} %pad_maximum_fusion.v_ref), channel_id=1, source_target_pairs={{0,4},{1,9},{2,6},{3,11},{4,0},{5,13},{6,2},{7,15},{8,12},{9,1},{1... | collective-permute-start | bytes 393224 | tf_op jit(solution)/shard_map/ppermute | solution.py:271
  43.0 1.5 %collective-permute-start.20 = (f32[256,128]{1,0:T(8,128)S(1)}, f32[256,128]{1,0:T(8,128)S(1)}, u32[]{:S(2)}, u32[]{:S(2)}) collective-permute-start(f32[256,128]{1,0:T(8,128)S(1)} %pad_maximum_fusion.2.v_ref), channel_id=1, source_target_pairs={{0,4},{1,9},{2,6},{3,11},{4,0},{5,13},{6,2},{7,15},{8,12},{9,1},{1... | collective-permute-start | bytes 393224 | tf_op jit(solution)/shard_map/ppermute | solution.py:271
  50.4 3.1 %collective-permute-done.22 = f32[16,128]{1,0:T(8,128)S(1)} collective-permute-done((f32[16,128]{1,0:T(8,128)S(1)}, f32[16,128]{1,0:T(8,128)S(1)}, u32[]{:S(2)}, u32[]{:S(2)}) %collective-permute-start.22) | collective-permute-done | bytes 8224 | tf_op jit(solution)/shard_map/ppermute | solution.py:262
  64.0 1.7 %collective-permute-start.25 = (f32[128,128]{1,0:T(8,128)S(1)}, f32[128,128]{1,0:T(8,128)S(1)}, u32[]{:S(2)}, u32[]{:S(2)}) collective-permute-start(f32[128,128]{1,0:T(8,128)S(1)} %slice.141), channel_id=1, source_target_pairs={{0,8},{1,5},{2,10},{3,7},{4,12},{5,1},{6,14},{7,3},{8,0},{9,13},{1... | collective-permute-start | bytes 196616 | tf_op jit(solution)/shard_map/ppermute | solution.py:271
  66.2 1.6 %collective-permute-start.38 = (f32[128,128]{1,0:T(8,128)S(1)}, f32[128,128]{1,0:T(8,128)S(1)}, u32[]{:S(2)}, u32[]{:S(2)}) collective-permute-start(f32[128,128]{1,0:T(8,128)S(1)} %slice.147), channel_id=1, source_target_pairs={{0,4},{1,9},{2,6},{3,11},{4,0},{5,13},{6,2},{7,15},{8,12},{9,1},{1... | collective-permute-start | bytes 196616 | tf_op jit(solution)/shard_map/ppermute | solution.py:271
  67.8 1.8 %collective-permute-start.31 = (f32[128,128]{1,0:T(8,128)S(1)}, f32[128,128]{1,0:T(8,128)S(1)}, u32[]{:S(2)}, u32[]{:S(2)}) collective-permute-start(f32[128,128]{1,0:T(8,128)S(1)} %slice_add_fusion.6), channel_id=1, source_target_pairs={{0,16},{1,17},{2,18},{3,19},{4,20},{5,21},{6,22},{7,23},{8,24},{9,... | collective-permute-start | bytes 196616 | tf_op jit(solution)/shard_map/ppermute | solution.py:271
  69.6 2.1 %collective-permute-start.26 = (f32[128,128]{1,0:T(8,128)S(1)}, f32[128,128]{1,0:T(8,128)S(1)}, u32[]{:S(2)}, u32[]{:S(2)}) collective-permute-start(f32[128,128]{1,0:T(8,128)S(1)} %slice_add_fusion.7), channel_id=1, source_target_pairs={{0,16},{1,17},{2,18},{3,19},{4,20},{5,21},{6,22},{7,23},{8,24},{9,... | collective-permute-start | bytes 196616 | tf_op jit(solution)/shard_map/ppermute | solution.py:271
  72.8 2.0 %collective-permute-start.39 = (f32[128,128]{1,0:T(8,128)S(1)}, f32[128,128]{1,0:T(8,128)S(1)}, u32[]{:S(2)}, u32[]{:S(2)}) collective-permute-start(f32[128,128]{1,0:T(8,128)S(1)} %slice_add_fusion.4), channel_id=1, source_target_pairs={{0,16},{1,17},{2,18},{3,19},{4,20},{5,21},{6,22},{7,23},{8,24},{9,... | collective-permute-start | bytes 196616 | tf_op jit(solution)/shard_map/ppermute | solution.py:271
  74.8 4.8 %collective-permute-done.26 = f32[128,128]{1,0:T(8,128)S(1)} collective-permute-done((f32[128,128]{1,0:T(8,128)S(1)}, f32[128,128]{1,0:T(8,128)S(1)}, u32[]{:S(2)}, u32[]{:S(2)}) %collective-permute-start.26) | collective-permute-done | bytes 65568 | tf_op jit(solution)/shard_map/ppermute | solution.py:271
  80.9 2.1 %collective-permute-start.36 = (f32[128,128]{1,0:T(8,128)S(1)}, f32[128,128]{1,0:T(8,128)S(1)}, u32[]{:S(2)}, u32[]{:S(2)}) collective-permute-start(f32[128,128]{1,0:T(8,128)S(1)} %add.214), channel_id=1, source_target_pairs={{0,8},{1,5},{2,10},{3,7},{4,12},{5,1},{6,14},{7,3},{8,0},{9,13},{1... | collective-permute-start | bytes 196616 | tf_op jit(solution)/shard_map/ppermute | solution.py:271
  86.5 1.5 %collective-permute-start.42 = (f32[256,128]{1,0:T(8,128)S(1)}, f32[256,128]{1,0:T(8,128)S(1)}, u32[]{:S(2)}, u32[]{:S(2)}) collective-permute-start(f32[256,128]{1,0:T(8,128)S(1)} %pad_maximum_fusion.6.v_ref), channel_id=1, source_target_pairs={{0,4},{1,9},{2,6},{3,11},{4,0},{5,13},{6,2},{7,15},{8,12},{9,1},{1... | collective-permute-start | bytes 393224 | tf_op jit(solution)/shard_map/ppermute | solution.py:271
  93.7 3.1 %collective-permute-done.44 = f32[16,128]{1,0:T(8,128)S(1)} collective-permute-done((f32[16,128]{1,0:T(8,128)S(1)}, f32[16,128]{1,0:T(8,128)S(1)}, u32[]{:S(2)}, u32[]{:S(2)}) %collective-permute-start.44) | collective-permute-done | bytes 8224 | tf_op jit(solution)/shard_map/ppermute | solution.py:262
  107.1 1.6 %collective-permute-start.52 = (f32[128,128]{1,0:T(8,128)S(1)}, f32[128,128]{1,0:T(8,128)S(1)}, u32[]{:S(2)}, u32[]{:S(2)}) collective-permute-start(f32[128,128]{1,0:T(8,128)S(1)} %slice.153), channel_id=1, source_target_pairs={{0,4},{1,9},{2,6},{3,11},{4,0},{5,13},{6,2},{7,15},{8,12},{9,1},{1... | collective-permute-start | bytes 196616 | tf_op jit(solution)/shard_map/ppermute | solution.py:271
  109.1 1.7 %collective-permute-start.62 = (f32[128,128]{1,0:T(8,128)S(1)}, f32[128,128]{1,0:T(8,128)S(1)}, u32[]{:S(2)}, u32[]{:S(2)}) collective-permute-start(f32[128,128]{1,0:T(8,128)S(1)} %slice.161), channel_id=1, source_target_pairs={{0,4},{1,9},{2,6},{3,11},{4,0},{5,13},{6,2},{7,15},{8,12},{9,1},{1... | collective-permute-start | bytes 196616 | tf_op jit(solution)/shard_map/ppermute | solution.py:271
  110.7 1.6 %collective-permute-start.48 = (f32[128,128]{1,0:T(8,128)S(1)}, f32[128,128]{1,0:T(8,128)S(1)}, u32[]{:S(2)}, u32[]{:S(2)}) collective-permute-start(f32[128,128]{1,0:T(8,128)S(1)} %slice_add_fusion.3), channel_id=1, source_target_pairs={{0,16},{1,17},{2,18},{3,19},{4,20},{5,21},{6,22},{7,23},{8,24},{9,... | collective-permute-start | bytes 196616 | tf_op jit(solution)/shard_map/ppermute | solution.py:271
  112.3 1.5 %collective-permute-start.53 = (f32[128,128]{1,0:T(8,128)S(1)}, f32[128,128]{1,0:T(8,128)S(1)}, u32[]{:S(2)}, u32[]{:S(2)}) collective-permute-start(f32[128,128]{1,0:T(8,128)S(1)} %slice_add_fusion.2), channel_id=1, source_target_pairs={{0,16},{1,17},{2,18},{3,19},{4,20},{5,21},{6,22},{7,23},{8,24},{9,... | collective-permute-start | bytes 196616 | tf_op jit(solution)/shard_map/ppermute | solution.py:271
  113.8 1.6 %collective-permute-start.58 = (f32[128,128]{1,0:T(8,128)S(1)}, f32[128,128]{1,0:T(8,128)S(1)}, u32[]{:S(2)}, u32[]{:S(2)}) collective-permute-start(f32[128,128]{1,0:T(8,128)S(1)} %slice_add_fusion.1), channel_id=1, source_target_pairs={{0,16},{1,17},{2,18},{3,19},{4,20},{5,21},{6,22},{7,23},{8,24},{9,... | collective-permute-start | bytes 196616 | tf_op jit(solution)/shard_map/ppermute | solution.py:271
  116.9 3.3 %collective-permute-done.48 = f32[128,128]{1,0:T(8,128)S(1)} collective-permute-done((f32[128,128]{1,0:T(8,128)S(1)}, f32[128,128]{1,0:T(8,128)S(1)}, u32[]{:S(2)}, u32[]{:S(2)}) %collective-permute-start.48) | collective-permute-done | bytes 65568 | tf_op jit(solution)/shard_map/ppermute | solution.py:271
  130.1 1.9 %collective-permute-done.50 = f32[256,128]{1,0:T(8,128)S(1)} collective-permute-done((f32[256,128]{1,0:T(8,128)S(1)}, f32[256,128]{1,0:T(8,128)S(1)}, u32[]{:S(2)}, u32[]{:S(2)}) %collective-permute-start.50) | collective-permute-done | bytes 131104 | tf_op jit(solution)/shard_map/ppermute | solution.py:271
  132.1 2.1 %collective-permute-done.60 = f32[256,128]{1,0:T(8,128)S(1)} collective-permute-done((f32[256,128]{1,0:T(8,128)S(1)}, f32[256,128]{1,0:T(8,128)S(1)}, u32[]{:S(2)}, u32[]{:S(2)}) %collective-permute-start.60) | collective-permute-done | bytes 131104 | tf_op jit(solution)/shard_map/ppermute | solution.py:271
  (225 shorter events, 62.7 us)
Async XLA Ops:
  13.8 7.4 %collective-permute-start.2 = (f32[256,128]{1,0:T(8,128)S(1)}, f32[256,128]{1,0:T(8,128)S(1)}, u32[]{:S(2)}, u32[]{:S(2)}) collective-permute-start(f32[256,128]{1,0:T(8,128)S(1)} %get-tuple-element.18), channel_id=1, source_target_pairs={{0,4},{1,9},{2,6},{3,11},{4,0},{5,13},{6,2},{7,15},{8,12},{9,1},{1... | collective-permute-start | bytes 393224 | tf_op jit(solution)/shard_map/ppermute | solution.py:271
  15.6 7.2 %collective-permute-start.11 = (f32[256,128]{1,0:T(8,128)S(1)}, f32[256,128]{1,0:T(8,128)S(1)}, u32[]{:S(2)}, u32[]{:S(2)}) collective-permute-start(f32[256,128]{1,0:T(8,128)S(1)} %weigh.24), channel_id=1, source_target_pairs={{0,4},{1,9},{2,6},{3,11},{4,0},{5,13},{6,2},{7,15},{8,12},{9,1},{1... | collective-permute-start | bytes 393224 | tf_op jit(solution)/shard_map/ppermute | solution.py:271
  16.4 6.9 %collective-permute-start.15 = (f32[256,128]{1,0:T(8,128)S(1)}, f32[256,128]{1,0:T(8,128)S(1)}, u32[]{:S(2)}, u32[]{:S(2)}) collective-permute-start(f32[256,128]{1,0:T(8,128)S(1)} %weigh.26), channel_id=1, source_target_pairs={{0,8},{1,5},{2,10},{3,7},{4,12},{5,1},{6,14},{7,3},{8,0},{9,13},{1... | collective-permute-start | bytes 393224 | tf_op jit(solution)/shard_map/ppermute | solution.py:271
  17.3 6.8 %collective-permute-start.8 = (f32[128,128]{1,0:T(8,128)S(1)}, f32[128,128]{1,0:T(8,128)S(1)}, u32[]{:S(2)}, u32[]{:S(2)}) collective-permute-start(f32[128,128]{1,0:T(8,128)S(1)} %slice.135), channel_id=1, source_target_pairs={{0,4},{1,9},{2,6},{3,11},{4,0},{5,13},{6,2},{7,15},{8,12},{9,1},{1... | collective-permute-start | bytes 196616 | tf_op jit(solution)/shard_map/ppermute | solution.py:271
  22.8 6.0 %collective-permute-start.12 = (f32[128,128]{1,0:T(8,128)S(1)}, f32[128,128]{1,0:T(8,128)S(1)}, u32[]{:S(2)}, u32[]{:S(2)}) collective-permute-start(f32[128,128]{1,0:T(8,128)S(1)} %slice.137), channel_id=1, source_target_pairs={{0,8},{1,5},{2,10},{3,7},{4,12},{5,1},{6,14},{7,3},{8,0},{9,13},{1... | collective-permute-start | bytes 196616 | tf_op jit(solution)/shard_map/ppermute | solution.py:271
  23.4 6.5 %collective-permute-start.16 = (f32[128,128]{1,0:T(8,128)S(1)}, f32[128,128]{1,0:T(8,128)S(1)}, u32[]{:S(2)}, u32[]{:S(2)}) collective-permute-start(f32[128,128]{1,0:T(8,128)S(1)} %slice.139), channel_id=1, source_target_pairs={{0,4},{1,9},{2,6},{3,11},{4,0},{5,13},{6,2},{7,15},{8,12},{9,1},{1... | collective-permute-start | bytes 196616 | tf_op jit(solution)/shard_map/ppermute | solution.py:271
  24.0 12.3 %collective-permute-start.9 = (f32[128,128]{1,0:T(8,128)S(1)}, f32[128,128]{1,0:T(8,128)S(1)}, u32[]{:S(2)}, u32[]{:S(2)}) collective-permute-start(f32[128,128]{1,0:T(8,128)S(1)} %slice_add_fusion.10), channel_id=1, source_target_pairs={{0,16},{1,17},{2,18},{3,19},{4,20},{5,21},{6,22},{7,23},{8,24},{9,... | collective-permute-start | bytes 196616 | tf_op jit(solution)/shard_map/ppermute | solution.py:271
  26.7 9.5 %collective-permute-start.4 = (f32[128,128]{1,0:T(8,128)S(1)}, f32[128,128]{1,0:T(8,128)S(1)}, u32[]{:S(2)}, u32[]{:S(2)}) collective-permute-start(f32[128,128]{1,0:T(8,128)S(1)} %slice_add_fusion.11), channel_id=1, source_target_pairs={{0,16},{1,17},{2,18},{3,19},{4,20},{5,21},{6,22},{7,23},{8,24},{9,... | collective-permute-start | bytes 196616 | tf_op jit(solution)/shard_map/ppermute | solution.py:271
  28.8 9.1 %collective-permute-start.13 = (f32[128,128]{1,0:T(8,128)S(1)}, f32[128,128]{1,0:T(8,128)S(1)}, u32[]{:S(2)}, u32[]{:S(2)}) collective-permute-start(f32[128,128]{1,0:T(8,128)S(1)} %slice_add_fusion.9), channel_id=1, source_target_pairs={{0,16},{1,17},{2,18},{3,19},{4,20},{5,21},{6,22},{7,23},{8,24},{9,... | collective-permute-start | bytes 196616 | tf_op jit(solution)/shard_map/ppermute | solution.py:271
  29.9 10.1 %collective-permute-start.17 = (f32[128,128]{1,0:T(8,128)S(1)}, f32[128,128]{1,0:T(8,128)S(1)}, u32[]{:S(2)}, u32[]{:S(2)}) collective-permute-start(f32[128,128]{1,0:T(8,128)S(1)} %slice_add_fusion.8), channel_id=1, source_target_pairs={{0,16},{1,17},{2,18},{3,19},{4,20},{5,21},{6,22},{7,23},{8,24},{9,... | collective-permute-start | bytes 196616 | tf_op jit(solution)/shard_map/ppermute | solution.py:271
  40.6 6.6 %collective-permute-start.6 = (f32[256,128]{1,0:T(8,128)S(1)}, f32[256,128]{1,0:T(8,128)S(1)}, u32[]{:S(2)}, u32[]{:S(2)}) collective-permute-start(f32[256,128]{1,0:T(8,128)S(1)} %pad_maximum_fusion.v_ref), channel_id=1, source_target_pairs={{0,4},{1,9},{2,6},{3,11},{4,0},{5,13},{6,2},{7,15},{8,12},{9,1},{1... | collective-permute-start | bytes 393224 | tf_op jit(solution)/shard_map/ppermute | solution.py:271
  56.0 6.4 %collective-permute-start.29 = (f32[256,128]{1,0:T(8,128)S(1)}, f32[256,128]{1,0:T(8,128)S(1)}, u32[]{:S(2)}, u32[]{:S(2)}) collective-permute-start(f32[256,128]{1,0:T(8,128)S(1)} %weigh.29), channel_id=1, source_target_pairs={{0,8},{1,5},{2,10},{3,7},{4,12},{5,1},{6,14},{7,3},{8,0},{9,13},{1... | collective-permute-start | bytes 393224 | tf_op jit(solution)/shard_map/ppermute | solution.py:271
  56.7 7.2 %collective-permute-start.24 = (f32[256,128]{1,0:T(8,128)S(1)}, f32[256,128]{1,0:T(8,128)S(1)}, u32[]{:S(2)}, u32[]{:S(2)}) collective-permute-start(f32[256,128]{1,0:T(8,128)S(1)} %get-tuple-element.22), channel_id=1, source_target_pairs={{0,4},{1,9},{2,6},{3,11},{4,0},{5,13},{6,2},{7,15},{8,12},{9,1},{1... | collective-permute-start | bytes 393224 | tf_op jit(solution)/shard_map/ppermute | solution.py:271
  58.5 7.2 %collective-permute-start.33 = (f32[256,128]{1,0:T(8,128)S(1)}, f32[256,128]{1,0:T(8,128)S(1)}, u32[]{:S(2)}, u32[]{:S(2)}) collective-permute-start(f32[256,128]{1,0:T(8,128)S(1)} %weigh.31), channel_id=1, source_target_pairs={{0,4},{1,9},{2,6},{3,11},{4,0},{5,13},{6,2},{7,15},{8,12},{9,1},{1... | collective-permute-start | bytes 393224 | tf_op jit(solution)/shard_map/ppermute | solution.py:271
  59.4 6.7 %collective-permute-start.37 = (f32[256,128]{1,0:T(8,128)S(1)}, f32[256,128]{1,0:T(8,128)S(1)}, u32[]{:S(2)}, u32[]{:S(2)}) collective-permute-start(f32[256,128]{1,0:T(8,128)S(1)} %weigh.33), channel_id=1, source_target_pairs={{0,8},{1,5},{2,10},{3,7},{4,12},{5,1},{6,14},{7,3},{8,0},{9,13},{1... | collective-permute-start | bytes 393224 | tf_op jit(solution)/shard_map/ppermute | solution.py:271
  65.8 5.9 %collective-permute-start.34 = (f32[128,128]{1,0:T(8,128)S(1)}, f32[128,128]{1,0:T(8,128)S(1)}, u32[]{:S(2)}, u32[]{:S(2)}) collective-permute-start(f32[128,128]{1,0:T(8,128)S(1)} %slice.145), channel_id=1, source_target_pairs={{0,8},{1,5},{2,10},{3,7},{4,12},{5,1},{6,14},{7,3},{8,0},{9,13},{1... | collective-permute-start | bytes 196616 | tf_op jit(solution)/shard_map/ppermute | solution.py:271
  66.2 6.6 %collective-permute-start.38 = (f32[128,128]{1,0:T(8,128)S(1)}, f32[128,128]{1,0:T(8,128)S(1)}, u32[]{:S(2)}, u32[]{:S(2)}) collective-permute-start(f32[128,128]{1,0:T(8,128)S(1)} %slice.147), channel_id=1, source_target_pairs={{0,4},{1,9},{2,6},{3,11},{4,0},{5,13},{6,2},{7,15},{8,12},{9,1},{1... | collective-permute-start | bytes 196616 | tf_op jit(solution)/shard_map/ppermute | solution.py:271
  67.8 11.8 %collective-permute-start.31 = (f32[128,128]{1,0:T(8,128)S(1)}, f32[128,128]{1,0:T(8,128)S(1)}, u32[]{:S(2)}, u32[]{:S(2)}) collective-permute-start(f32[128,128]{1,0:T(8,128)S(1)} %slice_add_fusion.6), channel_id=1, source_target_pairs={{0,16},{1,17},{2,18},{3,19},{4,20},{5,21},{6,22},{7,23},{8,24},{9,... | collective-permute-start | bytes 196616 | tf_op jit(solution)/shard_map/ppermute | solution.py:271
  69.6 9.9 %collective-permute-start.26 = (f32[128,128]{1,0:T(8,128)S(1)}, f32[128,128]{1,0:T(8,128)S(1)}, u32[]{:S(2)}, u32[]{:S(2)}) collective-permute-start(f32[128,128]{1,0:T(8,128)S(1)} %slice_add_fusion.7), channel_id=1, source_target_pairs={{0,16},{1,17},{2,18},{3,19},{4,20},{5,21},{6,22},{7,23},{8,24},{9,... | collective-permute-start | bytes 196616 | tf_op jit(solution)/shard_map/ppermute | solution.py:271
  71.7 9.2 %collective-permute-start.35 = (f32[128,128]{1,0:T(8,128)S(1)}, f32[128,128]{1,0:T(8,128)S(1)}, u32[]{:S(2)}, u32[]{:S(2)}) collective-permute-start(f32[128,128]{1,0:T(8,128)S(1)} %slice_add_fusion.5), channel_id=1, source_target_pairs={{0,16},{1,17},{2,18},{3,19},{4,20},{5,21},{6,22},{7,23},{8,24},{9,... | collective-permute-start | bytes 196616 | tf_op jit(solution)/shard_map/ppermute | solution.py:271
  72.8 10.2 %collective-permute-start.39 = (f32[128,128]{1,0:T(8,128)S(1)}, f32[128,128]{1,0:T(8,128)S(1)}, u32[]{:S(2)}, u32[]{:S(2)}) collective-permute-start(f32[128,128]{1,0:T(8,128)S(1)} %slice_add_fusion.4), channel_id=1, source_target_pairs={{0,16},{1,17},{2,18},{3,19},{4,20},{5,21},{6,22},{7,23},{8,24},{9,... | collective-permute-start | bytes 196616 | tf_op jit(solution)/shard_map/ppermute | solution.py:271
  79.7 6.1 %collective-permute-start.32 = (f32[128,128]{1,0:T(8,128)S(1)}, f32[128,128]{1,0:T(8,128)S(1)}, u32[]{:S(2)}, u32[]{:S(2)}) collective-permute-start(f32[128,128]{1,0:T(8,128)S(1)} %add.210), channel_id=1, source_target_pairs={{0,4},{1,9},{2,6},{3,11},{4,0},{5,13},{6,2},{7,15},{8,12},{9,1},{1... | collective-permute-start | bytes 196616 | tf_op jit(solution)/shard_map/ppermute | solution.py:271
  99.1 6.2 %collective-permute-start.46 = (f32[256,128]{1,0:T(8,128)S(1)}, f32[256,128]{1,0:T(8,128)S(1)}, u32[]{:S(2)}, u32[]{:S(2)}) collective-permute-start(f32[256,128]{1,0:T(8,128)S(1)} %get-tuple-element.25), channel_id=1, source_target_pairs={{0,4},{1,9},{2,6},{3,11},{4,0},{5,13},{6,2},{7,15},{8,12},{9,1},{1... | collective-permute-start | bytes 393224 | tf_op jit(solution)/shard_map/ppermute | solution.py:271
  100.1 6.9 %collective-permute-start.51 = (f32[256,128]{1,0:T(8,128)S(1)}, f32[256,128]{1,0:T(8,128)S(1)}, u32[]{:S(2)}, u32[]{:S(2)}) collective-permute-start(f32[256,128]{1,0:T(8,128)S(1)} %weigh.36), channel_id=1, source_target_pairs={{0,8},{1,5},{2,10},{3,7},{4,12},{5,1},{6,14},{7,3},{8,0},{9,13},{1... | collective-permute-start | bytes 393224 | tf_op jit(solution)/shard_map/ppermute | solution.py:271
  101.8 6.9 %collective-permute-start.56 = (f32[256,128]{1,0:T(8,128)S(1)}, f32[256,128]{1,0:T(8,128)S(1)}, u32[]{:S(2)}, u32[]{:S(2)}) collective-permute-start(f32[256,128]{1,0:T(8,128)S(1)} %weigh.38), channel_id=1, source_target_pairs={{0,4},{1,9},{2,6},{3,11},{4,0},{5,13},{6,2},{7,15},{8,12},{9,1},{1... | collective-permute-start | bytes 393224 | tf_op jit(solution)/shard_map/ppermute | solution.py:271
  103.1 5.9 %collective-permute-start.61 = (f32[256,128]{1,0:T(8,128)S(1)}, f32[256,128]{1,0:T(8,128)S(1)}, u32[]{:S(2)}, u32[]{:S(2)}) collective-permute-start(f32[256,128]{1,0:T(8,128)S(1)} %weigh.40), channel_id=1, source_target_pairs={{0,8},{1,5},{2,10},{3,7},{4,12},{5,1},{6,14},{7,3},{8,0},{9,13},{1... | collective-permute-start | bytes 393224 | tf_op jit(solution)/shard_map/ppermute | solution.py:271
  109.1 6.3 %collective-permute-start.62 = (f32[128,128]{1,0:T(8,128)S(1)}, f32[128,128]{1,0:T(8,128)S(1)}, u32[]{:S(2)}, u32[]{:S(2)}) collective-permute-start(f32[128,128]{1,0:T(8,128)S(1)} %slice.161), channel_id=1, source_target_pairs={{0,4},{1,9},{2,6},{3,11},{4,0},{5,13},{6,2},{7,15},{8,12},{9,1},{1... | collective-permute-start | bytes 196616 | tf_op jit(solution)/shard_map/ppermute | solution.py:271
  110.7 9.5 %collective-permute-start.48 = (f32[128,128]{1,0:T(8,128)S(1)}, f32[128,128]{1,0:T(8,128)S(1)}, u32[]{:S(2)}, u32[]{:S(2)}) collective-permute-start(f32[128,128]{1,0:T(8,128)S(1)} %slice_add_fusion.3), channel_id=1, source_target_pairs={{0,16},{1,17},{2,18},{3,19},{4,20},{5,21},{6,22},{7,23},{8,24},{9,... | collective-permute-start | bytes 196616 | tf_op jit(solution)/shard_map/ppermute | solution.py:271
  112.3 10.0 %collective-permute-start.53 = (f32[128,128]{1,0:T(8,128)S(1)}, f32[128,128]{1,0:T(8,128)S(1)}, u32[]{:S(2)}, u32[]{:S(2)}) collective-permute-start(f32[128,128]{1,0:T(8,128)S(1)} %slice_add_fusion.2), channel_id=1, source_target_pairs={{0,16},{1,17},{2,18},{3,19},{4,20},{5,21},{6,22},{7,23},{8,24},{9,... | collective-permute-start | bytes 196616 | tf_op jit(solution)/shard_map/ppermute | solution.py:271
  113.8 9.7 %collective-permute-start.58 = (f32[128,128]{1,0:T(8,128)S(1)}, f32[128,128]{1,0:T(8,128)S(1)}, u32[]{:S(2)}, u32[]{:S(2)}) collective-permute-start(f32[128,128]{1,0:T(8,128)S(1)} %slice_add_fusion.1), channel_id=1, source_target_pairs={{0,16},{1,17},{2,18},{3,19},{4,20},{5,21},{6,22},{7,23},{8,24},{9,... | collective-permute-start | bytes 196616 | tf_op jit(solution)/shard_map/ppermute | solution.py:271
  115.4 8.8 %collective-permute-start.63 = (f32[128,128]{1,0:T(8,128)S(1)}, f32[128,128]{1,0:T(8,128)S(1)}, u32[]{:S(2)}, u32[]{:S(2)}) collective-permute-start(f32[128,128]{1,0:T(8,128)S(1)} %slice_add_fusion), channel_id=1, source_target_pairs={{0,16},{1,17},{2,18},{3,19},{4,20},{5,21},{6,22},{7,23},{8,24},{9,... | collective-permute-start | bytes 196616 | tf_op jit(solution)/shard_map/ppermute | solution.py:271
  125.6 6.4 %collective-permute-start.50 = (f32[256,128]{1,0:T(8,128)S(1)}, f32[256,128]{1,0:T(8,128)S(1)}, u32[]{:S(2)}, u32[]{:S(2)}) collective-permute-start(f32[256,128]{1,0:T(8,128)S(1)} %get-tuple-element.32), channel_id=1, source_target_pairs={{0,4},{1,9},{2,6},{3,11},{4,0},{5,13},{6,2},{7,15},{8,12},{9,1},{1... | collective-permute-start | bytes 393224 | tf_op jit(solution)/shard_map/ppermute | solution.py:271
  (35 other events, 170.4 us)
